TPU v7x, 32 devices: a whole 2x2x4 slice. The times are simulated.
32 devices in a mesh: fsdp: 2 (over core), ctx: 4 (over y, x), tp: 4 (over z).
Axes of the slice: x: 2, y: 2, z: 4, core: 2. Of those that a mesh axis runs over, the one named last changes fastest.
Arguments:
- tokens: bfloat16 [8, 1024, 2048], P('fsdp', 'ctx'), may hold values from -6 to 6
- segment_ids: int32 [8, 1024], P('fsdp', 'ctx'), may hold values from 0 to 7, never falling along the last dimension, each value on 1 to 512 neighbouring positions
- w_in: float32 [3, 2048, 2048], P(None, 'fsdp', 'tp'), may hold values from -0.125 to 0.125
- w_out: float32 [2048, 2048], P('tp', 'fsdp'), may hold values from -0.125 to 0.125
- w_glu: float32 [2048, 2, 5632], P('fsdp', None, 'tp'), may hold values from -0.125 to 0.125
- w_down: float32 [5632, 2048], P('tp', 'fsdp'), may hold values from -0.078125 to 0.078125
- gain_one: float32 [2048], P('fsdp'), may hold values from 0.5 to 1.5
- gain_two: float32 [2048], P('fsdp'), may hold values from 0.5 to 1.5
- gate_gain: float32 [2048], P('tp'), may hold values from 0.5 to 1.5
- lower: float32 [2048], P('tp'), may hold values from 0.94 to 0.9995
- cotangent: bfloat16 [8, 1024, 2048], P('fsdp', 'ctx'), may hold values from -6 to 6
Outputs:
- output: bfloat16 [8, 1024, 2048], P('fsdp', 'ctx')
- grad_tokens: float32 [8, 1024, 2048], P('fsdp', 'ctx')
- grad_w_in: float32 [3, 2048, 2048], P(None, 'fsdp', 'tp')
- grad_w_out: float32 [2048, 2048], P('tp', 'fsdp')
- grad_w_glu: float32 [2048, 2, 5632], P('fsdp', None, 'tp')
- grad_w_down: float32 [5632, 2048], P('tp', 'fsdp')
- grad_gain_one: float32 [2048], P('fsdp')
- grad_gain_two: float32 [2048], P('fsdp')
- grad_gate_gain: float32 [2048], P('tp')
- grad_lower: float32 [2048], P('tp')
Inputs may be any that keep to these rules, and one draw needn't show every extreme that they name: `segment_ids`: within each sequence the document numbers start at 0, never fall, and each document has 1 to 512 tokens, one of them exactly 512.
All inputs are finite; a program needn't handle non-finite values.
Results may differ from a plain program's by a relative error of at most 0.02.
Values may be sent and summed in bfloat16 or wider, within the bound.
A program may use at most 256 MiB of HBM per device.

v0:
```python
import jax
import jax.numpy as jnp
from jax import lax
from jax.sharding import PartitionSpec as P

EPS = 1e-06
FLOAT = jnp.float32
HALF = jnp.bfloat16


def entering(value, axis, join, neutral, backward):
    count, mine = (lax.axis_size(axis), lax.axis_index(axis))
    pieces = jax.tree.map(lambda part: lax.all_gather(part, axis), value)
    if backward:
        pieces = jax.tree.map(lambda part: part[::-1], pieces)
        mine = count - 1 - mine
    so_far = jax.tree.map(
        lambda part, zero: jnp.full_like(part, 0) + jnp.asarray(zero, part.dtype), value, neutral
    )

    def hop(position, so_far):
        longer = join(so_far, jax.tree.map(lambda part: part[position], pieces))
        return jax.tree.map(lambda new, old: jnp.where(position < mine, new, old), longer, so_far)

    return lax.fori_loop(0, count - 1, hop, so_far)


def link(earlier, later):
    return (earlier[0] * later[0], later[0] * earlier[1] + later[1])


def chain_link(earlier, later):
    mult_a, sum_a, first_a, last_a = earlier
    mult_b, sum_b, first_b, last_b = later
    joined = ((last_a == first_b) | (last_a < 0.0) | (first_b < 0.0)).astype(FLOAT)[:, None]
    first = jnp.where(first_a < 0.0, first_b, first_a)
    last = jnp.where(last_b < 0.0, last_a, last_b)
    return (mult_a * mult_b * joined, sum_b + mult_b * joined * sum_a, first, last)


def rms_scale(values):
    return lax.rsqrt(jnp.mean(values * values, -1, keepdims=True) + EPS)


def silu_slope(values):
    sig = jax.nn.sigmoid(values)
    return sig * (1.0 + values * (1.0 - sig))


def local(
    tokens, segment_ids, w_in, w_out, w_glu, w_down, gain_one, gain_two, gate_gain, lower, cotangent
):
    n_seq, length, width = tokens.shape
    rows = n_seq * length
    w_in_all, w_out_all, w_glu_all, w_down_all, gain_one_all, gain_two_all = (
        lax.all_gather(w_in.astype(HALF), "fsdp", axis=1, tiled=True),
        lax.all_gather(w_out.astype(HALF), "fsdp", axis=1, tiled=True),
        lax.all_gather(w_glu.astype(HALF), "fsdp", axis=0, tiled=True),
        lax.all_gather(w_down.astype(HALF), "fsdp", axis=1, tiled=True),
        lax.all_gather(gain_one.astype(HALF), "fsdp", axis=0, tiled=True),
        lax.all_gather(gain_two.astype(HALF), "fsdp", axis=0, tiled=True),
    )
    chan = w_in_all.shape[2]
    gain_a = gain_one_all.astype(FLOAT)
    gain_b = gain_two_all.astype(FLOAT)
    flat = tokens.reshape(rows, width).astype(FLOAT)
    scale_one = rms_scale(flat)
    normed = (flat * scale_one * gain_a).astype(HALF)
    proj = jnp.einsum("td,wdc->wtc", normed, w_in_all, preferred_element_type=FLOAT)
    inp = proj[0].reshape(n_seq, length, chan)
    forget = proj[1].reshape(n_seq, length, chan)
    gate = proj[2].reshape(n_seq, length, chan)
    fsig = jax.nn.sigmoid(forget)
    decay = lower + (1.0 - lower) * fsig
    silu_inp = jax.nn.silu(inp)
    update = silu_inp * (1.0 - decay)
    same = (segment_ids[:, 1:] == segment_ids[:, :-1]).astype(FLOAT)
    keep = jnp.concatenate([jnp.ones((n_seq, 1), FLOAT), same], 1)
    mult = decay * keep[:, :, None]
    reach, local_state = lax.associative_scan(link, (mult, update), axis=1)
    seg_float = segment_ids.astype(FLOAT)
    identity = (
        jnp.ones((n_seq, chan), FLOAT),
        jnp.zeros((n_seq, chan), FLOAT),
        -jnp.ones((n_seq,), FLOAT),
        -jnp.ones((n_seq,), FLOAT),
    )
    prior = entering(
        (reach[:, -1], local_state[:, -1], seg_float[:, 0], seg_float[:, -1]),
        "ctx",
        chain_link,
        identity,
        False,
    )
    joined = ((prior[3] == seg_float[:, 0]) | (prior[3] < 0.0)).astype(FLOAT)[:, None]
    carry_in = prior[1] * joined
    state = local_state + reach * carry_in[:, None, :]
    squares = lax.psum(jnp.sum(state * state, -1), "tp")
    gate_scale = lax.rsqrt(squares / width + EPS)[..., None]
    unit = state * gate_scale
    swish = jax.nn.silu(gate)
    gated = (unit * gate_gain * swish).astype(HALF).reshape(rows, chan)
    mixed = lax.psum(
        jnp.dot(gated, w_out_all, preferred_element_type=FLOAT).astype(jnp.bfloat16), "tp"
    ).astype(jnp.float32)
    resid = flat + mixed
    scale_two = rms_scale(resid)
    normed_two = (resid * scale_two * gain_b).astype(HALF)
    glu = jnp.einsum("td,dwf->wtf", normed_two, w_glu_all, preferred_element_type=FLOAT)
    silu_glu = jax.nn.silu(glu[0])
    act = (silu_glu * glu[1]).astype(HALF)
    down = lax.psum(
        jnp.dot(act, w_down_all, preferred_element_type=FLOAT).astype(jnp.bfloat16), "tp"
    ).astype(jnp.float32)
    output = (resid + down).astype(HALF).reshape(n_seq, length, width)
    grad_y_half = cotangent.reshape(rows, width)
    grad_y = grad_y_half.astype(FLOAT)
    grad_act = jnp.einsum("te,fe->tf", grad_y_half, w_down_all, preferred_element_type=FLOAT)
    grad_w_down = jnp.einsum("tf,te->fe", act, grad_y_half, preferred_element_type=FLOAT)
    grad_gate_pre = grad_act * glu[1] * silu_slope(glu[0])
    grad_up_pre = grad_act * silu_glu
    grad_glu = jnp.stack([grad_gate_pre, grad_up_pre]).astype(HALF)
    grad_normed_two = lax.psum(
        jnp.einsum("wtf,dwf->td", grad_glu, w_glu_all, preferred_element_type=FLOAT).astype(
            jnp.bfloat16
        ),
        "tp",
    ).astype(jnp.float32)
    grad_w_glu = jnp.einsum("td,wtf->dwf", normed_two, grad_glu, preferred_element_type=FLOAT)
    grad_gain_two = jnp.sum(grad_normed_two * resid * scale_two, 0)
    inner_two = gain_b * grad_normed_two
    grad_resid = (
        grad_y
        + scale_two * inner_two
        - resid * scale_two**3 * jnp.mean(inner_two * resid, -1, keepdims=True)
    )
    grad_mixed = grad_resid.astype(HALF)
    grad_gated = jnp.einsum(
        "te,ce->tc", grad_mixed, w_out_all, preferred_element_type=FLOAT
    ).reshape(n_seq, length, chan)
    grad_w_out = jnp.einsum("tc,te->ce", gated, grad_mixed, preferred_element_type=FLOAT)
    grad_gate_gain = jnp.sum(grad_gated * unit * swish, (0, 1))
    grad_gate_logit = grad_gated * unit * gate_gain * silu_slope(gate)
    grad_unit = grad_gated * gate_gain * swish
    cross = lax.psum(jnp.sum(grad_unit * state, -1), "tp")
    grad_from_norm = gate_scale * grad_unit - state * gate_scale**3 * (cross / width)[..., None]
    ahead = jnp.concatenate([mult[:, 1:], jnp.ones((n_seq, 1, chan), FLOAT)], 1)
    back_reach, local_grad = lax.associative_scan(
        link, (ahead, grad_from_norm), axis=1, reverse=True
    )
    later = entering(
        (reach[:, -1], mult[:, 0] * local_grad[:, 0], seg_float[:, -1], seg_float[:, 0]),
        "ctx",
        chain_link,
        identity,
        True,
    )
    linked = ((later[3] == seg_float[:, -1]) | (later[3] < 0.0)).astype(FLOAT)[:, None]
    carry_back = later[1] * linked
    grad_state = local_grad + back_reach * carry_back[:, None, :]
    prev_state = jnp.concatenate([carry_in[:, None, :], state[:, :-1]], 1)
    grad_decay = grad_state * (prev_state * keep[:, :, None] - silu_inp)
    grad_inp = grad_state * (1.0 - decay) * silu_slope(inp)
    grad_forget = grad_decay * (1.0 - lower) * fsig * (1.0 - fsig)
    grad_lower = jnp.sum(grad_decay * (1.0 - fsig), (0, 1))
    grad_proj = (
        jnp.stack([grad_inp, grad_forget, grad_gate_logit]).reshape(3, rows, chan).astype(HALF)
    )
    grad_normed = lax.psum(
        jnp.einsum("wtc,wdc->td", grad_proj, w_in_all, preferred_element_type=FLOAT).astype(
            jnp.bfloat16
        ),
        "tp",
    ).astype(jnp.float32)
    grad_w_in = jnp.einsum("td,wtc->wdc", normed, grad_proj, preferred_element_type=FLOAT)
    grad_gain_one = jnp.sum(grad_normed * flat * scale_one, 0)
    inner_one = gain_a * grad_normed
    grad_tokens = (
        grad_resid
        + scale_one * inner_one
        - flat * scale_one**3 * jnp.mean(inner_one * flat, -1, keepdims=True)
    )
    local_grads = (grad_w_in, grad_w_out, grad_w_glu, grad_w_down, grad_gain_one, grad_gain_two)
    pieces = (
        lax.psum_scatter(
            local_grads[0].astype(jnp.bfloat16), "fsdp", scatter_dimension=1, tiled=True
        ).astype(jnp.float32),
        lax.psum_scatter(
            local_grads[1].astype(jnp.bfloat16), "fsdp", scatter_dimension=1, tiled=True
        ).astype(jnp.float32),
        lax.psum_scatter(
            local_grads[2].astype(jnp.bfloat16), "fsdp", scatter_dimension=0, tiled=True
        ).astype(jnp.float32),
        lax.psum_scatter(
            local_grads[3].astype(jnp.bfloat16), "fsdp", scatter_dimension=1, tiled=True
        ).astype(jnp.float32),
        lax.psum_scatter(
            local_grads[4].astype(jnp.bfloat16), "fsdp", scatter_dimension=0, tiled=True
        ).astype(jnp.float32),
        lax.psum_scatter(
            local_grads[5].astype(jnp.bfloat16), "fsdp", scatter_dimension=0, tiled=True
        ).astype(jnp.float32),
    )
    pieces = (
        lax.psum(pieces[0].astype(jnp.bfloat16), "ctx").astype(jnp.float32),
        lax.psum(pieces[1].astype(jnp.bfloat16), "ctx").astype(jnp.float32),
        lax.psum(pieces[2].astype(jnp.bfloat16), "ctx").astype(jnp.float32),
        lax.psum(pieces[3].astype(jnp.bfloat16), "ctx").astype(jnp.float32),
        lax.psum(pieces[4].astype(jnp.bfloat16), "ctx").astype(jnp.float32),
        lax.psum(pieces[5].astype(jnp.bfloat16), "ctx").astype(jnp.float32),
    )
    channel = lax.psum((grad_gate_gain, grad_lower), ("fsdp", "ctx"))
    return (
        output,
        grad_tokens.reshape(n_seq, length, width),
        pieces[0],
        pieces[1],
        pieces[2],
        pieces[3],
        pieces[4],
        pieces[5],
        channel[0],
        channel[1],
    )


def solution(mesh):
    return jax.shard_map(
        local,
        mesh=mesh,
        in_specs=(
            P("fsdp", "ctx", None),
            P("fsdp", "ctx"),
            P(None, "fsdp", "tp"),
            P("tp", "fsdp"),
            P("fsdp", None, "tp"),
            P("tp", "fsdp"),
            P("fsdp"),
            P("fsdp"),
            P("tp"),
            P("tp"),
            P("fsdp", "ctx", None),
        ),
        out_specs=(
            P("fsdp", "ctx", None),
            P("fsdp", "ctx", None),
            P(None, "fsdp", "tp"),
            P("tp", "fsdp"),
            P("fsdp", None, "tp"),
            P("tp", "fsdp"),
            P("fsdp"),
            P("fsdp"),
            P("tp"),
            P("tp"),
        ),
        check_vma=False,
    )
```

profile of v0, /device:TPU:0, one launch (start us, length us, event | category | flops | bytes accessed | tf_op | source)
XLA Modules:
  0.0 1620.4 jit_solution(13375770906683467710)
XLA Ops:
  7.2 5.0 convert_element_type.166
  20.7 11.4 all-reduce.72
  32.9 5.2 fusion.26
  38.1 10.5 fusion.45
  53.3 4.3 slice.539
  57.7 4.2 slice.535
  61.8 7.3 slice.537
  69.1 7.3 slice.536
  156.1 4.2 slice.534
  161.0 7.4 slice.591
  189.2 4.4 pad.228
  204.0 7.0 all-gather
  219.8 8.4 all-gather.1
  232.8 11.9 psum.98
  247.0 5.9 convolution_convert_fusion.3
  253.0 8.3 copy.40
  261.4 4.7 convert_element_type.178
  267.9 137.4 %all-reduce.82.cloned.1.call-done = bf16[1024,2048]{1,0:T(8,128)(2,1)} async-done(((bf16[1024,2048]{1,0:T(8,128)(2,1)}), bf16[1024,2048]{1,0:T(8,128)(2,1)}) %all-reduce.82.cloned.1.call-update) | async-done | bytes 4194320 | tf_op jit(solution)/shard_map/psum | solution.py:103
  405.3 5.0 multiply_reduce_fusion
  411.3 4.6 multiply_convert_fusion
  415.9 13.6 all-gather.14.cloned.1.call-done
  429.5 18.6 %convolution_bitcast_fusion = f32[2,1024,1408]{2,1,0:T(8,128)} fusion(bf16[2048,2,1408]{2,0,1:T(8,128)(2,1)} %all-gather.14.cloned.1.call-done, bf16[1024,2048]{1,0:T(8,128)(2,1)} %multiply_convert_fusion), kind=kOutput, calls=%fused_computation.58 | convolution fusion | flops 11811160064 | bytes 27262976 | tf_op jit(solution)/shard_map/td,dwf->wtf/dot_general | solution.py:109
  448.7 14.3 fusion.44
  465.4 16.2 %bitcast_convert_fusion.1 = bf16[1024,2048]{1,0:T(8,128)(2,1)} fusion(bf16[2048,2,1408]{2,0,1:T(8,128)(2,1)} %all-gather.14.cloned.1.call-done, bf16[1,1024,1408]{2,1,0:T(8,128)(2,1)S(1)} %get-tuple-element.427, bf16[1,1024,1408]{2,1,0:T(8,128)(2,1)S(1)} %get-tuple-element.426), kind=kOutput, calls=%fused_computation.45 | convolution fusion | flops 11816140800 | bytes 21495808 | tf_op jit(solution)/shard_map/wtf,dwf->td/dot_general | solution.py:124
  481.7 156.2 %all-reduce.84.cloned.1.call-done = bf16[1024,2048]{1,0:T(8,128)(2,1)} async-done(((bf16[1024,2048]{1,0:T(8,128)(2,1)}), bf16[1024,2048]{1,0:T(8,128)(2,1)}) %all-reduce.84.cloned.1.call-update) | async-done | bytes 4194320 | tf_op jit(solution)/shard_map/psum | solution.py:123
  638.0 8.8 fusion.21
  646.8 5.0 fusion.18
  664.4 7.4 slice.616
  671.8 7.3 slice.625
  679.1 6.0 slice.618
  685.7 8.9 slice.617
  694.7 8.9 slice.626
  703.5 5.3 slice.619
  708.8 13.2 convolution_convert_fusion.1
  722.3 6.5 fusion.54
  730.1 9.5 psum.102
  743.8 7.3 slice.622
  751.1 6.0 slice.620
  757.1 8.9 slice.623
  766.0 5.2 slice.621
  848.0 7.4 slice.678
  857.4 9.0 slice.679
  892.3 4.3 pad.260
  896.6 4.3 pad.245
  902.8 4.3 pad.244
  915.4 4.9 pad.246
  927.6 16.8 %rev.20 = f32[4,256,512]{2,1,0:T(8,128)} reverse(f32[4,256,512]{2,1,0:T(8,128)} %add.570), dimensions={1} | reverse | bytes 4194304 | tf_op jit(solution)/shard_map/rev | solution.py:148
  946.8 5.0 pad.262
  959.2 16.6 %rev.21 = f32[4,256,512]{2,1,0:T(8,128)} reverse(f32[4,256,512]{2,1,0:T(8,128)} %add.578), dimensions={1} | reverse | bytes 4194304 | tf_op jit(solution)/shard_map/rev | solution.py:148
  976.8 8.7 all-gather.4
  985.6 6.5 while.33
  992.2 4.4 multiply_reduce_fusion.1
  999.1 8.8 convert_bitcast_fusion
  1008.0 18.3 %convolution_convert_fusion = bf16[2048,2,1408]{2,0,1:T(8,128)(2,1)} fusion(bf16[1024,2048]{1,0:T(8,128)(2,1)} %multiply_convert_fusion, bf16[1,1024,1408]{2,1,0:T(8,128)(2,1)} %copy-done.85, bf16[1,1024,1408]{2,1,0:T(8,128)(2,1)} %copy-done.84), kind=kOutput, calls=%fused_computation.25 | convolution fusion | flops 11828461568 | bytes 21495808 | tf_op jit(solution)/shard_map/td,wtf->dwf/dot_general | solution.py:129
  1026.6 13.6 convolution_convert_fusion.2
  1040.2 11.6 bitcast_convert_fusion
  1053.9 15.3 all-reduce.71
  1069.2 271.6 %all-reduce.86.cloned.1.call-done = (bf16[1024,2048]{1,0:T(8,128)(2,1)}, bf16[1024,2048]{1,0:T(8,128)(2,1)}) async-done(((bf16[1024,2048]{1,0:T(8,128)(2,1)}, bf16[1024,2048]{1,0:T(8,128)(2,1)}), (bf16[1024,2048]{1,0:T(8,128)(2,1)}, bf16[1024,2048]{1,0:T(8,128)(2,1)})) %all-reduce.86.cloned.1.call-update) | async-done | bytes 8388624 | tf_op jit(solution)/shard_map/psum | solution.py:112
  1340.8 5.6 fusion.23
  1349.0 10.1 all-reduce.74
  1360.3 16.0 fusion.15
  1376.3 213.9 %all-reduce.88.cloned.1.call-done = (bf16[3,1024,512]{1,2,0:T(8,128)(2,1)}, bf16[1024,2,1408]{2,0,1:T(8,128)(2,1)}, bf16[512,1024]{1,0:T(8,128)(2,1)}, bf16[1408,1024]{1,0:T(8,128)(2,1)}) async-done(((bf16[3,1024,512]{1,2,0:T(8,128)(2,1)}, bf16[1024,2,1408]{2,0,1:T(8,128)(2,1)}, bf16[512,1024]{1,0:T(8,128)(2,1)}, bf16[1408,1024]{1,0:T(8,128)(2,1)}), (bf16[3,1024,512]{1,2,0:T(8,128)(2,1)}, ...) | async-done | bytes 12845072 | tf_op jit(solution)/shard_map/psum | solution.py:205
  1590.3 5.5 copy.30
  1597.3 12.8 copy.31
  (517 shorter events, 316.9 us)
Async XLA Ops:
  7.2 30.9 %all-gather.10.cloned.1.call-start = ((), (), s32[]{:S(2)}) async-start(), calls=%async_computation.4 | async-start | bytes 9437184 | tf_op jit(solution)/shard_map/all_gather | solution.py:56
  12.3 6.5 copy-start.72
  12.3 6.8 copy-start.83
  12.3 234.7 %all-gather.12.cloned.1.call-start = ((), (), s32[]{:S(2)}) async-start(), calls=%async_computation.5 | async-start | bytes 3145728 | tf_op jit(solution)/shard_map/all_gather | solution.py:57
  13.5 391.8 %all-reduce.82.cloned.1.call-start = ((), (), s32[]{:S(2)}) async-start(), calls=%async_computation.6 | async-start | bytes 8388608 | tf_op jit(solution)/shard_map/psum | solution.py:103
  15.6 22.5 %copy-start.37 = (f32[2048]{0:T(1024)}, f32[2048]{0:T(1024)S(1)}, u32[]{:S(2)}) copy-start(f32[2048]{0:T(1024)S(1)} %convert_element_type.164) | copy-start | bytes 24580
  18.8 31.8 %copy-start.47 = (f32[4,256]{1,0:T(4,128)}, f32[4,256]{1,0:T(4,128)S(1)}, u32[]{:S(2)}) copy-start(f32[4,256]{1,0:T(4,128)S(1)} %pad_convert_fusion) | copy-start | bytes 12292
  18.8 31.8 %copy-start.50 = (f32[512]{0:T(512)}, f32[512]{0:T(512)S(1)}, u32[]{:S(2)}) copy-start(f32[512]{0:T(512)S(1)} %broadcast_subtract_fusion) | copy-start | bytes 6148
  19.0 19.1 %copy-start.78 = (f32[4]{0:T(128)}, f32[4]{0:T(128)S(1)}, u32[]{:S(2)}) copy-start(f32[4]{0:T(128)S(1)} %get-tuple-element.374) | copy-start | bytes 52
  19.0 19.1 %copy-start.80 = (f32[4]{0:T(128)}, f32[4]{0:T(128)S(1)}, u32[]{:S(2)}) copy-start(f32[4]{0:T(128)S(1)} %get-tuple-element.375) | copy-start | bytes 52
  20.7 17.4 %copy-start.39 = (f32[1,2,4,128]{3,1,2,0:T(2,128)}, f32[1,2,4,128]{3,1,2,0:T(2,128)S(1)}, u32[]{:S(2)}) copy-start(f32[1,2,4,128]{3,1,2,0:T(2,128)S(1)} %copy.38) | copy-start | bytes 12292
  53.3 116.5 %copy-start.8 = (f32[4,256,512]{2,1,0:T(8,128)}, f32[4,256,512]{2,1,0:T(8,128)S(1)}, u32[]{:S(2)}) copy-start(f32[4,256,512]{2,1,0:T(8,128)S(1)} %get-tuple-element.436) | copy-start | bytes 6291460
  142.9 27.6 %copy-start.42 = (f32[4,2,512]{2,1,0:T(2,128)S(1)}, f32[4,2,512]{2,1,0:T(2,128)}, u32[]{:S(2)}) copy-start(f32[4,2,512]{2,1,0:T(2,128)} %get-tuple-element.510) | copy-start | bytes 49156
  142.9 27.6 %copy-start.67 = (f32[4,1,512]{2,1,0:T(1,128)S(1)}, f32[4,1,512]{2,1,0:T(1,128)}, u32[]{:S(2)}) copy-start(f32[4,1,512]{2,1,0:T(1,128)} %get-tuple-element.488) | copy-start | bytes 24580
  142.9 27.6 %copy-start.68 = (f32[4,1,512]{2,1,0:T(1,128)S(1)}, f32[4,1,512]{2,1,0:T(1,128)}, u32[]{:S(2)}) copy-start(f32[4,1,512]{2,1,0:T(1,128)} %get-tuple-element.489) | copy-start | bytes 24580
  142.9 27.6 %copy-start.69 = (f32[4,1,512]{2,1,0:T(1,128)S(1)}, f32[4,1,512]{2,1,0:T(1,128)}, u32[]{:S(2)}) copy-start(f32[4,1,512]{2,1,0:T(1,128)} %get-tuple-element.490) | copy-start | bytes 24580
  142.9 27.6 %copy-start.70 = (f32[4,1,512]{2,1,0:T(1,128)S(1)}, f32[4,1,512]{2,1,0:T(1,128)}, u32[]{:S(2)}) copy-start(f32[4,1,512]{2,1,0:T(1,128)} %get-tuple-element.491) | copy-start | bytes 24580
  142.9 27.7 %copy-start.41 = (f32[4,2,512]{2,1,0:T(2,128)S(1)}, f32[4,2,512]{2,1,0:T(2,128)}, u32[]{:S(2)}) copy-start(f32[4,2,512]{2,1,0:T(2,128)} %get-tuple-element.511) | copy-start | bytes 49156
  153.2 22.7 %copy-start.31 = (f32[4,15,512]{2,1,0:T(8,128)S(1)}, f32[4,15,512]{2,1,0:T(8,128)}, u32[]{:S(2)}) copy-start(f32[4,15,512]{2,1,0:T(8,128)} %slice.552) | copy-start | bytes 368644
  153.2 22.7 %copy-start.34 = (f32[4,15,512]{2,1,0:T(8,128)S(1)}, f32[4,15,512]{2,1,0:T(8,128)}, u32[]{:S(2)}) copy-start(f32[4,15,512]{2,1,0:T(8,128)} %slice.585) | copy-start | bytes 368644
  168.4 8.8 copy-start.65
  199.7 11.4 copy-start.19
  199.7 14.7 copy-start.54
  203.1 15.8 copy-start.15
  211.1 17.2 %copy-start.71 = (f32[4,4]{1,0:T(4,128)S(1)}, f32[4,4]{1,0:T(4,128)}, u32[]{:S(2)}) copy-start(f32[4,4]{1,0:T(4,128)} %reshape.146) | copy-start | bytes 196
  211.1 17.6 %copy-start.81 = (f32[4]{0:T(128)S(1)}, f32[4]{0:T(128)}, u32[]{:S(2)}) copy-start(f32[4]{0:T(128)} %copy-done.80) | copy-start | bytes 52
  228.8 16.0 copy-start.74
  253.0 176.5 %all-gather.14.cloned.1.call-start = ((), (), s32[]{:S(2)}) async-start(), calls=%async_computation.7 | async-start | bytes 17301504 | tf_op jit(solution)/shard_map/all_gather | solution.py:58
  261.3 187.4 %all-gather.16.cloned.1.call-start = ((), (), s32[]{:S(2)}) async-start(), calls=%async_computation.8 | async-start | bytes 8650752 | tf_op jit(solution)/shard_map/all_gather | solution.py:59
  266.0 371.9 %all-reduce.84.cloned.1.call-start = ((), (), s32[]{:S(2)}) async-start(), calls=%async_computation.9 | async-start | bytes 8388608 | tf_op jit(solution)/shard_map/psum | solution.py:123
  405.3 5.9 copy-start.2
  481.7 570.2 %reduce-scatter.7.cloned.1.call-start = ((), (), s32[]{:S(2)}) async-start(), calls=%async_computation.11 | async-start | bytes 3145728 | tf_op jit(solution)/shard_map/reduce_scatter | solution.py:188
  638.0 8.8 copy-start.1
  638.0 8.8 copy-start.3
  638.0 8.8 copy-start.11
  659.1 392.8 %reduce-scatter.11.cloned.1.call-start = ((), (), s32[]{:S(2)}) async-start(), calls=%async_computation.13 | async-start | bytes 8650752 | tf_op jit(solution)/shard_map/reduce_scatter | solution.py:194
  722.0 329.9 %reduce-scatter.5.cloned.1.call-start = ((), (), s32[]{:S(2)}) async-start(), calls=%async_computation.10 | async-start | bytes 9437184 | tf_op jit(solution)/shard_map/reduce_scatter | solution.py:185
  722.3 6.5 copy-start.7
  835.0 31.4 %copy-start.43 = (f32[4,2,512]{2,1,0:T(2,128)S(1)}, f32[4,2,512]{2,1,0:T(2,128)}, u32[]{:S(2)}) copy-start(f32[4,2,512]{2,1,0:T(2,128)} %slice.662) | copy-start | bytes 49156
  835.0 31.4 %copy-start.44 = (f32[4,2,512]{2,1,0:T(2,128)S(1)}, f32[4,2,512]{2,1,0:T(2,128)}, u32[]{:S(2)}) copy-start(f32[4,2,512]{2,1,0:T(2,128)} %slice.658) | copy-start | bytes 49156
  835.0 31.4 %copy-start.45 = (f32[4,2,512]{2,1,0:T(2,128)S(1)}, f32[4,2,512]{2,1,0:T(2,128)}, u32[]{:S(2)}) copy-start(f32[4,2,512]{2,1,0:T(2,128)} %slice.660) | copy-start | bytes 49156
  835.0 31.4 %copy-start.46 = (f32[4,2,512]{2,1,0:T(2,128)S(1)}, f32[4,2,512]{2,1,0:T(2,128)}, u32[]{:S(2)}) copy-start(f32[4,2,512]{2,1,0:T(2,128)} %slice.659) | copy-start | bytes 49156
  835.0 31.5 %copy-start.35 = (f32[2,8,512]{2,1,0:T(8,128)S(1)}, f32[2,8,512]{2,1,0:T(8,128)}, u32[]{:S(2)}) copy-start(f32[2,8,512]{2,1,0:T(8,128)} %get-tuple-element.534) | copy-start | bytes 98308
  835.0 31.5 %copy-start.36 = (f32[2,8,512]{2,1,0:T(8,128)S(1)}, f32[2,8,512]{2,1,0:T(8,128)}, u32[]{:S(2)}) copy-start(f32[2,8,512]{2,1,0:T(8,128)} %get-tuple-element.535) | copy-start | bytes 98308
  848.0 22.7 %copy-start.32 = (f32[4,15,512]{2,1,0:T(8,128)S(1)}, f32[4,15,512]{2,1,0:T(8,128)}, u32[]{:S(2)}) copy-start(f32[4,15,512]{2,1,0:T(8,128)} %slice.639) | copy-start | bytes 368644
  848.0 22.7 %copy-start.33 = (f32[4,15,512]{2,1,0:T(8,128)S(1)}, f32[4,15,512]{2,1,0:T(8,128)}, u32[]{:S(2)}) copy-start(f32[4,15,512]{2,1,0:T(8,128)} %slice.672) | copy-start | bytes 368644
  855.9 14.3 copy-start.66
  855.9 14.6 copy-start.64
  873.2 9.9 copy-start.58
  881.0 10.5 copy-start.56
  888.5 12.4 copy-start.55
  914.3 6.1 copy-start.20
  927.6 24.2 %copy-start.18 = (f32[4,128,512]{2,1,0:T(8,128)S(1)}, f32[4,128,512]{2,1,0:T(8,128)}, u32[]{:S(2)}) copy-start(f32[4,128,512]{2,1,0:T(8,128)} %add.577) | copy-start | bytes 3145732
  955.1 37.0 %copy-start.79 = (f32[4]{0:T(128)S(1)}, f32[4]{0:T(128)}, u32[]{:S(2)}) copy-start(f32[4]{0:T(128)} %copy-done.78) | copy-start | bytes 52
  955.1 37.1 %copy-start.48 = (f32[4,256]{1,0:T(4,128)S(1)}, f32[4,256]{1,0:T(4,128)}, u32[]{:S(2)}) copy-start(f32[4,256]{1,0:T(4,128)} %copy-done.47) | copy-start | bytes 12292
  955.1 37.1 %copy-start.51 = (f32[512]{0:T(512)S(1)}, f32[512]{0:T(512)}, u32[]{:S(2)}) copy-start(f32[512]{0:T(512)} %copy-done.50) | copy-start | bytes 6148
  955.1 37.1 %copy-start.52 = (f32[4,1,512]{2,1,0:T(1,128)S(1)}, f32[4,1,512]{2,1,0:T(1,128)}, u32[]{:S(2)}) copy-start(f32[4,1,512]{2,1,0:T(1,128)} %broadcast_in_dim.10) | copy-start | bytes 24580
  955.1 37.1 %copy-start.73 = (f32[512]{0:T(512)S(1)}, f32[512]{0:T(512)}, u32[]{:S(2)}) copy-start(f32[512]{0:T(512)} %param.24) | copy-start | bytes 6148
  1008.0 44.0 %reduce-scatter.9.cloned.1.call-start = ((), (), s32[]{:S(2)}) async-start(), calls=%async_computation.12 | async-start | bytes 17301504 | tf_op jit(solution)/shard_map/reduce_scatter | solution.py:191
  1026.4 314.4 %all-reduce.86.cloned.1.call-start = ((), (), s32[]{:S(2)}) async-start(), calls=%async_computation.14 | async-start | bytes 16777216 | tf_op jit(solution)/shard_map/psum | solution.py:112
  1051.8 538.4 %all-reduce.88.cloned.1.call-start = ((), (), s32[]{:S(2)}) async-start(), calls=%async_computation.15 | async-start | bytes 25690112 | tf_op jit(solution)/shard_map/psum | solution.py:205
  1052.0 288.8 %copy-start.38 = (f32[2048]{0:T(1024)S(1)}, f32[2048]{0:T(1024)}, u32[]{:S(2)}) copy-start(f32[2048]{0:T(1024)} %copy-done.37) | copy-start | bytes 24580
  1340.8 5.6 copy-start.75
  1597.3 12.8 copy-start.24
  (34 other events, 111.5 us)
Sparse Core Ops, SparseCore 0:
  12.4 19.4 all-gather.9
  33.4 11.7 all-gather.11
  253.1 152.2 all-reduce.81
  407.4 22.0 all-gather.13
  431.5 17.1 all-gather.15
  481.8 156.1 all-reduce.83
  659.3 8.5 reduce-scatter.6
  722.1 12.7 reduce-scatter.10
  1008.1 11.8 reduce-scatter.4
  1026.5 17.4 reduce-scatter.8
  1051.9 288.7 all-reduce.85
  1345.1 245.0 all-reduce.87
where the time goes:
time: 1640 us; the launch traced here: 1620 us
  waiting for transfers between devices  794 us (48%)
  local copies, waits for them, and re-layouts  394 us (24%)
  other arithmetic  185 us (11%)
  matrix products  141 us (9%)
  blocking collectives  88.5 us (5%)
  between operations  17.3 us (1%)
    psum x1, waiting for transfers between devices, local(): lax.psum(jnp.dot(act, w_down_all, preferred_element_type=FLOAT).astype(jn...  272 us
    psum x1, waiting for transfers between devices, local(): lax.psum(pieces[0].astype(jnp.bfloat16), 'ctx').astype(jnp.float32)  214 us
    psum x1, waiting for transfers between devices, local(): lax.psum(jnp.einsum('wtf,dwf->td', grad_glu, w_glu_all, preferred_element...  156 us
    slice x57, local copies, waits for them, and re-layouts, local(): lax.associative_scan(link, (ahead, grad_from_norm), axis=1, reverse=True)  153 us
    psum x1, waiting for transfers between devices, local(): lax.psum(jnp.dot(gated, w_out_all, preferred_element_type=FLOAT).astype(j...  137 us
    slice x52, local copies, waits for them, and re-layouts, local(): reach, local_state = lax.associative_scan(link, (mult, update), axis=1)  101 us
    mul x27, other arithmetic, link(): return (earlier[0] * later[0], later[0] * earlier[1] + later[1])  43.6 us
    pad x28, local copies, waits for them, and re-layouts, local(): lax.associative_scan(link, (ahead, grad_from_norm), axis=1, reverse=True)  38.6 us
  transfers between devices with their start and end apart: 12, of which 6 were waited for; matrix products, arithmetic and copies ran while one was open for 39% of the time, Pallas kernels for 0%

commit v1 on v0

v1 whole, which is shorter than its diff:
```python
import functools

import jax
import jax.numpy as jnp
from jax import lax
from jax.experimental import pallas as pl
from jax.experimental.pallas import tpu as pltpu
from jax.sharding import PartitionSpec as P

EPS = 1e-06
FLOAT = jnp.float32
HALF = jnp.bfloat16
MESH = pl.DeviceIdType.MESH
GROUP = 8
BLOCK = 128
MIB = 1 << 20


def rms_scale(values):
    return lax.rsqrt(jnp.mean(values * values, -1, keepdims=True) + EPS)


def silu_slope(values):
    sig = jax.nn.sigmoid(values)
    return sig * (1.0 + values * (1.0 - sig))


def greet(peers):
    barrier = pltpu.get_barrier_semaphore()
    for peer in peers:
        pl.semaphore_signal(barrier, inc=1, device_id=peer, device_id_type=MESH)
    pl.semaphore_wait(barrier, len(peers))


def others(axis, count):
    mine = lax.axis_index(axis)
    return [{axis: lax.rem(mine + step, count)} for step in range(1, count)]


def share(slots, axis, count, send, recv):
    mine = lax.axis_index(axis)
    copies = [
        pltpu.make_async_remote_copy(
            src_ref=slots.at[mine],
            dst_ref=slots.at[mine],
            send_sem=send.at[step],
            recv_sem=recv.at[step],
            device_id=peer,
            device_id_type=MESH,
        )
        for step, peer in enumerate(others(axis, count))
    ]
    for copy in copies:
        copy.start()
    for copy in copies:
        copy.wait()


def lane_sums(values):
    part = values[:, :BLOCK]
    for start in range(BLOCK, values.shape[1], BLOCK):
        part = part + values[:, start : start + BLOCK]
    return jnp.sum(part.T, 0, keepdims=True)


def columns(row):
    return jnp.broadcast_to(row, (BLOCK, BLOCK)).T


def widen(values, chan):
    return jnp.concatenate([values] * (chan // BLOCK), -1)


def scan_forward(
    n_ctx, n_tp, width,
    proj, keep, gain, lower,
    gated, state, scale, carry_out,
    local, reach, ends, squares, ctx_send, ctx_recv, tp_send, tp_recv,
):
    n_seq, length, chan = state.shape
    greet(others("ctx", n_ctx) + others("tp", n_tp))
    low = lower[...].reshape(1, 1, chan)
    row = lax.broadcasted_iota(jnp.int32, (n_seq, GROUP, chan), 1)

    def step(index, carry):
        prod, total = carry
        rows = pl.ds(pl.multiple_of(index * GROUP, GROUP), GROUP)
        inp = proj[0, :, rows, :]
        decay = low + (1.0 - low) * jax.nn.sigmoid(proj[1, :, rows, :])
        add = inp * jax.nn.sigmoid(inp) * (1.0 - decay)
        mult = decay * keep[:, rows, :]
        for hop in (1, 2, 4):
            inside = row >= hop
            add = jnp.where(inside, mult * pltpu.roll(add, hop, 1) + add, add)
            mult = jnp.where(inside, mult * pltpu.roll(mult, hop, 1), mult)
        add = add + mult * total
        mult = mult * prod
        local[:, rows, :] = add
        reach[:, rows, :] = mult
        return mult[:, GROUP - 1 :, :], add[:, GROUP - 1 :, :]

    start = (jnp.ones((n_seq, 1, chan), FLOAT), jnp.zeros((n_seq, 1, chan), FLOAT))
    prod, total = lax.fori_loop(0, length // GROUP, step, start)
    here = lax.axis_index("ctx")
    ends[here, 0] = prod.reshape(n_seq, chan)
    ends[here, 1] = total.reshape(n_seq, chan)
    share(ends, "ctx", n_ctx, ctx_send, ctx_recv)
    carry = jnp.zeros((n_seq, chan), FLOAT)
    for place in range(n_ctx - 1):
        carry = jnp.where(place < here, ends[place, 1] + ends[place, 0] * carry, carry)
    carry_out[...] = carry
    mine = lax.axis_index("tp")
    for seq in range(n_seq):
        for start in range(0, length, BLOCK):
            rows = slice(start, start + BLOCK)
            value = local[seq, rows, :] + reach[seq, rows, :] * carry[seq : seq + 1]
            state[seq, rows, :] = value
            squares[mine, seq : seq + 1, rows] = lane_sums(value * value)
    share(squares, "tp", n_tp, tp_send, tp_recv)
    total = squares[0]
    for place in range(1, n_tp):
        total = total + squares[place]
    rate = lax.rsqrt(total / width + EPS)
    scale[...] = rate
    for seq in range(n_seq):
        for start in range(0, length, BLOCK):
            rows = slice(start, start + BLOCK)
            gate = proj[2, seq, rows, :]
            unit = state[seq, rows, :] * widen(columns(rate[seq : seq + 1, rows]), chan)
            gated[seq, rows, :] = (unit * gain[...] * (gate * jax.nn.sigmoid(gate))).astype(HALF)


def run_scan_forward(proj, keep, gain, lower, n_ctx, n_tp, width):
    _, n_seq, length, chan = proj.shape
    vmem = pl.BlockSpec(memory_space=pltpu.VMEM)
    return pl.pallas_call(
        functools.partial(scan_forward, n_ctx, n_tp, width),
        name="scan_forward",
        out_shape=(
            jax.ShapeDtypeStruct((n_seq, length, chan), HALF),
            jax.ShapeDtypeStruct((n_seq, length, chan), FLOAT),
            jax.ShapeDtypeStruct((n_seq, length), FLOAT),
            jax.ShapeDtypeStruct((n_seq, chan), FLOAT),
        ),
        in_specs=[vmem] * 4,
        out_specs=[vmem] * 4,
        scratch_shapes=[
            pltpu.VMEM((n_seq, length, chan), FLOAT),
            pltpu.VMEM((n_seq, length, chan), FLOAT),
            pltpu.VMEM((n_ctx, 2, n_seq, chan), FLOAT),
            pltpu.VMEM((n_tp, n_seq, length), FLOAT),
            pltpu.SemaphoreType.DMA((n_ctx,)),
            pltpu.SemaphoreType.DMA((n_ctx,)),
            pltpu.SemaphoreType.DMA((n_tp,)),
            pltpu.SemaphoreType.DMA((n_tp,)),
        ],
        compiler_params=pltpu.CompilerParams(
            collective_id=0, has_side_effects=True, vmem_limit_bytes=40 * MIB
        ),
    )(proj, keep, gain, lower)


def scan_backward(
    n_ctx, n_tp, width,
    proj, keep, gain, lower, state, scale, carry_in, grad_gated,
    grad_proj, grad_gain, grad_lower,
    near, reach, rate_wide, cross_wide, ends, cross, ctx_send, ctx_recv, tp_send, tp_recv,
):
    n_seq, length, chan = state.shape
    greet(others("ctx", n_ctx) + others("tp", n_tp))
    low = lower[...].reshape(1, 1, chan)
    mine = lax.axis_index("tp")
    gain_total = jnp.zeros((8, chan), FLOAT)
    for seq in range(n_seq):
        for start in range(0, length, BLOCK):
            rows = slice(start, start + BLOCK)
            rate = columns(scale[seq : seq + 1, rows])
            rate_wide[seq, rows, :] = rate
            gate = proj[2, seq, rows, :]
            sig = jax.nn.sigmoid(gate)
            value = state[seq, rows, :]
            into = grad_gated[seq, rows, :]
            by_unit = into * value * widen(rate, chan)
            into_swish = into * (gate * sig)
            slope = sig * (1.0 + gate * (1.0 - sig))
            grad_proj[2, seq, rows, :] = (by_unit * gain[...] * slope).astype(HALF)
            gain_total = gain_total + jnp.sum((by_unit * (gate * sig)).reshape(-1, 8, chan), 0)
            grad_unit = into_swish * gain[...]
            near[seq, rows, :] = grad_unit
            cross[mine, seq : seq + 1, rows] = lane_sums(grad_unit * value)
    grad_gain[...] = jnp.sum(gain_total, 0, keepdims=True)
    share(cross, "tp", n_tp, tp_send, tp_recv)
    total = cross[0]
    for place in range(1, n_tp):
        total = total + cross[place]
    rate = scale[...]
    total = total * (rate * rate * rate) / width
    for seq in range(n_seq):
        for start in range(0, length, BLOCK):
            rows = slice(start, start + BLOCK)
            cross_wide[seq, rows, :] = columns(total[seq : seq + 1, rows])

    row = lax.broadcasted_iota(jnp.int32, (n_seq, GROUP, chan), 1)

    def back(index, carry):
        prod, above = carry
        rows = pl.ds(pl.multiple_of((length // GROUP - 1 - index) * GROUP, GROUP), GROUP)
        decay = low + (1.0 - low) * jax.nn.sigmoid(proj[1, :, rows, :])
        mult = decay * keep[:, rows, :]
        direct = (
            widen(rate_wide[:, rows, :], chan) * near[:, rows, :]
            - widen(cross_wide[:, rows, :], chan) * state[:, rows, :]
        )
        add = mult * direct
        for hop in (1, 2, 4):
            inside = row < GROUP - hop
            add = jnp.where(inside, mult * pltpu.roll(add, GROUP - hop, 1) + add, add)
            mult = jnp.where(inside, mult * pltpu.roll(mult, GROUP - hop, 1), mult)
        add = add + mult * above
        mult = mult * prod
        inside = row < GROUP - 1
        near[:, rows, :] = direct + jnp.where(inside, pltpu.roll(add, GROUP - 1, 1), above)
        reach[:, rows, :] = jnp.where(inside, pltpu.roll(mult, GROUP - 1, 1), prod)
        return mult[:, :1, :], add[:, :1, :]

    start = (jnp.ones((n_seq, 1, chan), FLOAT), jnp.zeros((n_seq, 1, chan), FLOAT))
    prod, total = lax.fori_loop(0, length // GROUP, back, start)
    here = lax.axis_index("ctx")
    ends[here, 0] = prod.reshape(n_seq, chan)
    ends[here, 1] = total.reshape(n_seq, chan)
    share(ends, "ctx", n_ctx, ctx_send, ctx_recv)
    carry = jnp.zeros((n_seq, chan), FLOAT)
    for place in range(n_ctx - 1, 0, -1):
        carry = jnp.where(place > here, ends[place, 1] + ends[place, 0] * carry, carry)
    carry = carry.reshape(n_seq, 1, chan)
    wide = 2 * GROUP
    first = lax.broadcasted_iota(jnp.int32, (n_seq, wide, chan), 1) == 0

    def finish(index, held):
        before, low_total = held
        rows = pl.ds(pl.multiple_of(index * wide, wide), wide)
        inp = proj[0, :, rows, :]
        sig = jax.nn.sigmoid(inp)
        silu = inp * sig
        fsig = jax.nn.sigmoid(proj[1, :, rows, :])
        rest = 1.0 - fsig
        decay = low + (1.0 - low) * fsig
        grad_state = near[:, rows, :] + reach[:, rows, :] * carry
        value = state[:, rows, :]
        prev = jnp.where(first, before, pltpu.roll(value, 1, 1))
        grad_decay = grad_state * (prev * keep[:, rows, :] - silu)
        grad_proj[0, :, rows, :] = (
            grad_state * (1.0 - decay) * (sig * (1.0 + inp * (1.0 - sig)))
        ).astype(HALF)
        grad_proj[1, :, rows, :] = (grad_decay * (1.0 - low) * fsig * rest).astype(HALF)
        return value[:, wide - 1 :, :], low_total + grad_decay * rest

    held = (carry_in[...].reshape(n_seq, 1, chan), jnp.zeros((n_seq, wide, chan), FLOAT))
    _, low_total = lax.fori_loop(0, length // wide, finish, held)
    grad_lower[...] = jnp.sum(jnp.sum(low_total, 0), 0, keepdims=True)


def run_scan_backward(
    proj, keep, gain, lower, state, scale, carry, grad_gated, n_ctx, n_tp, width
):
    _, n_seq, length, chan = proj.shape
    vmem = pl.BlockSpec(memory_space=pltpu.VMEM)
    return pl.pallas_call(
        functools.partial(scan_backward, n_ctx, n_tp, width),
        name="scan_backward",
        out_shape=(
            jax.ShapeDtypeStruct((3, n_seq, length, chan), HALF),
            jax.ShapeDtypeStruct((1, chan), FLOAT),
            jax.ShapeDtypeStruct((1, chan), FLOAT),
        ),
        in_specs=[vmem] * 8,
        out_specs=[vmem] * 3,
        scratch_shapes=[
            pltpu.VMEM((n_seq, length, chan), FLOAT),
            pltpu.VMEM((n_seq, length, chan), FLOAT),
            pltpu.VMEM((n_seq, length, BLOCK), FLOAT),
            pltpu.VMEM((n_seq, length, BLOCK), FLOAT),
            pltpu.VMEM((n_ctx, 2, n_seq, chan), FLOAT),
            pltpu.VMEM((n_tp, n_seq, length), FLOAT),
            pltpu.SemaphoreType.DMA((n_ctx,)),
            pltpu.SemaphoreType.DMA((n_ctx,)),
            pltpu.SemaphoreType.DMA((n_tp,)),
            pltpu.SemaphoreType.DMA((n_tp,)),
        ],
        compiler_params=pltpu.CompilerParams(
            collective_id=1, has_side_effects=True, vmem_limit_bytes=40 * MIB
        ),
    )(proj, keep, gain, lower, state, scale, carry, grad_gated)


def gather_fsdp(part, dim, count):
    if count != 2:
        return lax.all_gather(part, "fsdp", axis=dim, tiled=True)
    other = lax.ppermute(part, "fsdp", [(0, 1), (1, 0)])
    first = lax.axis_index("fsdp") == 0
    return jnp.concatenate(
        [jnp.where(first, part, other), jnp.where(first, other, part)], dim
    )


def keep_flags(segment_ids, count):
    last = lax.ppermute(
        segment_ids[:, -1:].astype(FLOAT), "ctx", [(place, place + 1) for place in range(count - 1)]
    )
    seg = segment_ids.astype(FLOAT)
    before = jnp.concatenate([last, seg[:, :-1]], 1)
    token = lax.broadcasted_iota(jnp.int32, seg.shape, 1)
    start = (token == 0) & (lax.axis_index("ctx") == 0)
    return jnp.where(start, 0.0, (seg == before).astype(FLOAT))


def local(
    sizes,
    tokens, segment_ids, w_in, w_out, w_glu, w_down, gain_one, gain_two, gate_gain, lower, cotangent,
):
    n_fsdp, n_ctx, n_tp = sizes
    n_seq, length, width = tokens.shape
    rows = n_seq * length
    chan = w_in.shape[2]
    gain_a = gather_fsdp(gain_one.astype(HALF)[None], 1, n_fsdp).astype(FLOAT)
    gain_b = gather_fsdp(gain_two.astype(HALF)[None], 1, n_fsdp).astype(FLOAT)
    w_in_all = gather_fsdp(w_in.astype(HALF), 1, n_fsdp)
    w_out_all = gather_fsdp(w_out.astype(HALF), 1, n_fsdp)
    w_glu_all = gather_fsdp(w_glu.astype(HALF), 0, n_fsdp)
    w_down_all = gather_fsdp(w_down.astype(HALF), 1, n_fsdp)
    keep = keep_flags(segment_ids, n_ctx)[..., None]
    gain_gate = gate_gain[None]
    low = lower[None]
    flat = tokens.reshape(rows, width).astype(FLOAT)
    scale_one = rms_scale(flat)
    normed = (flat * scale_one * gain_a).astype(HALF)
    proj = jnp.einsum("td,wdc->wtc", normed, w_in_all, preferred_element_type=FLOAT)
    proj = proj.reshape(3, n_seq, length, chan)
    gated, state, gate_scale, carry = run_scan_forward(
        proj, keep, gain_gate, low, n_ctx, n_tp, width
    )
    gated = gated.reshape(rows, chan)
    mixed = lax.psum(
        jnp.dot(gated, w_out_all, preferred_element_type=FLOAT).astype(HALF), "tp"
    ).astype(FLOAT)
    resid = flat + mixed
    scale_two = rms_scale(resid)
    normed_two = (resid * scale_two * gain_b).astype(HALF)
    glu = jnp.einsum("td,dwf->wtf", normed_two, w_glu_all, preferred_element_type=FLOAT)
    silu_glu = jax.nn.silu(glu[0])
    act = (silu_glu * glu[1]).astype(HALF)
    down = lax.psum(
        jnp.dot(act, w_down_all, preferred_element_type=FLOAT).astype(HALF), "tp"
    ).astype(FLOAT)
    output = (resid + down).astype(HALF).reshape(n_seq, length, width)
    grad_y_half = cotangent.reshape(rows, width)
    grad_y = grad_y_half.astype(FLOAT)
    grad_act = jnp.einsum("te,fe->tf", grad_y_half, w_down_all, preferred_element_type=FLOAT)
    grad_w_down = jnp.einsum("tf,te->fe", act, grad_y_half, preferred_element_type=FLOAT)
    grad_gate_pre = grad_act * glu[1] * silu_slope(glu[0])
    grad_up_pre = grad_act * silu_glu
    grad_glu = jnp.stack([grad_gate_pre, grad_up_pre]).astype(HALF)
    grad_normed_two = lax.psum(
        jnp.einsum("wtf,dwf->td", grad_glu, w_glu_all, preferred_element_type=FLOAT).astype(HALF),
        "tp",
    ).astype(FLOAT)
    grad_w_glu = jnp.einsum("td,wtf->dwf", normed_two, grad_glu, preferred_element_type=FLOAT)
    grad_gain_two = jnp.sum(grad_normed_two * resid * scale_two, 0)
    inner_two = gain_b * grad_normed_two
    grad_resid = (
        grad_y
        + scale_two * inner_two
        - resid * scale_two**3 * jnp.mean(inner_two * resid, -1, keepdims=True)
    )
    grad_mixed = grad_resid.astype(HALF)
    grad_gated = jnp.einsum(
        "te,ce->tc", grad_mixed, w_out_all, preferred_element_type=FLOAT
    ).reshape(n_seq, length, chan)
    grad_w_out = jnp.einsum("tc,te->ce", gated, grad_mixed, preferred_element_type=FLOAT)
    grad_proj, grad_gate_gain, grad_lower = run_scan_backward(
        proj, keep, gain_gate, low, state, gate_scale, carry, grad_gated, n_ctx, n_tp, width
    )
    grad_proj = grad_proj.reshape(3, rows, chan)
    grad_normed = lax.psum(
        jnp.einsum("wtc,wdc->td", grad_proj, w_in_all, preferred_element_type=FLOAT).astype(HALF),
        "tp",
    ).astype(FLOAT)
    grad_w_in = jnp.einsum("td,wtc->wdc", normed, grad_proj, preferred_element_type=FLOAT)
    grad_gain_one = jnp.sum(grad_normed * flat * scale_one, 0)
    inner_one = gain_a * grad_normed
    grad_tokens = (
        grad_resid
        + scale_one * inner_one
        - flat * scale_one**3 * jnp.mean(inner_one * flat, -1, keepdims=True)
    )
    pieces = [
        lax.psum(
            lax.psum_scatter(
                value.astype(HALF), "fsdp", scatter_dimension=dim, tiled=True
            ),
            "ctx",
        ).astype(FLOAT)
        for value, dim in (
            (grad_w_in, 1),
            (grad_w_out, 1),
            (grad_w_glu, 0),
            (grad_w_down, 1),
            (grad_gain_one, 0),
            (grad_gain_two, 0),
        )
    ]
    channel = lax.psum((grad_gate_gain[0], grad_lower[0]), ("fsdp", "ctx"))
    return (
        output,
        grad_tokens.reshape(n_seq, length, width),
        *pieces,
        channel[0],
        channel[1],
    )


def solution(mesh):
    sizes = tuple(mesh.shape[axis] for axis in ("fsdp", "ctx", "tp"))
    return jax.shard_map(
        functools.partial(local, sizes),
        mesh=mesh,
        in_specs=(
            P("fsdp", "ctx", None),
            P("fsdp", "ctx"),
            P(None, "fsdp", "tp"),
            P("tp", "fsdp"),
            P("fsdp", None, "tp"),
            P("tp", "fsdp"),
            P("fsdp"),
            P("fsdp"),
            P("tp"),
            P("tp"),
            P("fsdp", "ctx", None),
        ),
        out_specs=(
            P("fsdp", "ctx", None),
            P("fsdp", "ctx", None),
            P(None, "fsdp", "tp"),
            P("tp", "fsdp"),
            P("fsdp", None, "tp"),
            P("tp", "fsdp"),
            P("fsdp"),
            P("fsdp"),
            P("tp"),
            P("tp"),
        ),
        check_vma=False,
    )
```

time: 1640 us -> 1170 us (0.71)
  local copies, waits for them, and re-layouts: 394 us -> 62.3 us
  other arithmetic: 185 us -> 93.9 us
  blocking collectives: 88.5 us -> 27 us
  Pallas kernels: 0 us -> 35.5 us
    slice x111 -> x0, local copies, waits for them, and re-layouts: 256 us -> none  [the longest x57 153 us: local(): lax.associative_scan(link, (ahead, grad_from_norm), axis=1, reverse=True)]
    pad x56 -> x0, local copies, waits for them, and re-layouts: 58.8 us -> none  [the longest x28 38.6 us: local(): lax.associative_scan(link, (ahead, grad_from_norm), axis=1, reverse=True)]
    mul x31 -> x0, other arithmetic: 47.2 us -> none  [the longest x27 43.6 us: link(): return (earlier[0] * later[0], later[0] * earlier[1] + later[1])]
    pallas_call x0 -> x2, Pallas kernels: none -> 35.5 us  [the longest x1 20.1 us: run_scan_backward(): pl.pallas_call(functools.partial(scan_backward, n_ctx, n_tp, width), name...]
    rev x6 -> x0, local copies, waits for them, and re-layouts: 35.2 us -> none  [the longest x2 33.4 us: local(): lax.associative_scan(link, (ahead, grad_from_norm), axis=1, reverse=True)]
    all_gather x5 -> x0, blocking collectives: 27.7 us -> none  [the longest x3 24 us: entering(): pieces = jax.tree.map(lambda part: lax.all_gather(part, axis), value)]
    add x31 -> x0, other arithmetic: 23.5 us -> none  [the longest x16 17.3 us: local(): lax.associative_scan(link, (ahead, grad_from_norm), axis=1, reverse=True)]
    psum x4 -> x2, blocking collectives: 46.8 us -> 24.5 us  [the longest x1 14.1 us: local(): channel = lax.psum((grad_gate_gain[0], grad_lower[0]), ('fsdp', 'ctx'))]
  transfers between devices with their start and end apart: 12 -> 15, of which waited for: 6 -> 4; matrix products, arithmetic and copies ran while one was open for 39% -> 14% of each run, Pallas kernels for 0% -> 3%
where the time goes in v1:
time: 1170 us; the launch traced here: 1160 us
  waiting for transfers between devices  783 us (67%)
  matrix products  135 us (12%)
  other arithmetic  93.9 us (8%)
  local copies, waits for them, and re-layouts  62.3 us (5%)
  Pallas kernels  35.5 us (3%)
  blocking collectives  27 us (2%)
  between operations  15.7 us (1%)
    psum x1, waiting for transfers between devices, local(): lax.psum(jnp.dot(act, w_down_all, preferred_element_type=FLOAT).astype(HA...  276 us
    psum x1, waiting for transfers between devices, local(): lax.psum(lax.psum_scatter(value.astype(HALF), 'fsdp', scatter_dimension=d...  214 us
    psum x1, waiting for transfers between devices, local(): lax.psum(jnp.einsum('wtf,dwf->td', grad_glu, w_glu_all, preferred_element...  154 us
    psum x1, waiting for transfers between devices, local(): lax.psum(jnp.dot(gated, w_out_all, preferred_element_type=FLOAT).astype(H...  138 us
    unnamed x76, local copies, waits for them, and re-layouts  55.5 us
  transfers between devices with their start and end apart: 15, of which 4 were waited for; matrix products, arithmetic and copies ran while one was open for 14% of the time, Pallas kernels for 3%

profile of v1, /device:TPU:0, one launch (start us, length us, event | category | flops | bytes accessed | tf_op | source)
XLA Modules:
  0.0 1159.2 jit_solution(16371918838959621410)
XLA Ops:
  7.3 5.5 copy.45
  12.8 0.5 collective-permute-start
  13.4 0.5 collective-permute-start.5
  14.0 4.4 collective-permute-start.2
  18.4 1.1 convert_element_type.153
  19.5 0.2 collective-permute-start.3
  19.7 3.1 fusion.14
  22.8 0.6 add_rsqrt_fusion.1
  23.4 15.8 %copy.48 = bf16[1024,2,1408]{0,2,1:T(8,128)(2,1)} copy(f32[1024,2,1408]{2,1,0:T(2,128)} %param.15) | data formatting | bytes 17301504 | tf_op args[4]
  39.2 4.7 convert_element_type.161
  43.9 0.4 collective-permute-start.4
  44.4 0.2 copy.47.keep
  44.6 0.3 collective-permute-start.6
  45.0 3.2 fusion.18
  48.2 2.8 broadcast_select_fusion.7
  51.0 3.3 broadcast_select_fusion.3
  54.3 1.8 copy-done.16
  56.1 0.9 copy-done.18
  56.9 8.6 fusion.46
  65.6 6.6 copy.46
  72.1 2.8 copy-done
  74.9 15.4 %scan_forward.1 = (bf16[4,256,512]{2,1,0:T(8,128)(2,1)S(1)}, f32[4,256,512]{2,1,0:T(8,128)S(1)}, f32[4,256]{1,0:T(4,128)S(1)}, f32[4,512]{1,0:T(4,128)S(1)}) custom-call(f32[3,4,256,512]{3,2,1,0:T(8,128)S(1)} %bitcast.135, f32[4,256,1]{2,1,0:T(8,128)S(1)} %copy.47.keep, f32[1,512]{1,0:T(1,128)S(1)} %bitcast.140, f32[1,512]{1,0:T(1,128)S(1)} %bitcast.142), custom_call_target="tpu_custom_call" | custom-call | tf_op jit(solution)/shard_map/scan_forward/pallas_call | solution.py:136
  90.4 1.0 copy-done.2
  91.3 5.9 convolution_convert_fusion.3
  97.3 0.3 all-reduce.14.cloned.1.call-start
  97.6 6.5 broadcast_select_fusion.5
  104.1 9.5 broadcast_select_fusion.1
  113.6 137.9 %all-reduce.12.cloned.1.call-done = bf16[1024,2048]{1,0:T(8,128)(2,1)} async-done(((bf16[1024,2048]{1,0:T(8,128)(2,1)}), bf16[1024,2048]{1,0:T(8,128)(2,1)}) %all-reduce.12.cloned.1.call-update) | async-done | bytes 4194320 | tf_op jit(solution)/shard_map/psum | solution.py:343
  251.5 5.0 multiply_reduce_fusion
  256.5 0.9 copy-done.11
  257.4 4.0 multiply_convert_fusion
  261.4 17.3 %fusion.22 = f32[2,1024,1408]{1,2,0:T(8,128)} fusion(bf16[1024,2,1408]{0,2,1:T(8,128)(2,1)} %get-tuple-element.77, bf16[1024,2,1408]{0,2,1:T(8,128)(2,1)S(1)} %bitcast.149, bf16[1024,2048]{1,0:T(8,128)(2,1)} %multiply_convert_fusion), kind=kOutput, calls=%fused_computation.40 | convolution fusion | flops 11834228736 | bytes 27262976 | tf_op jit(solution)/shard_map/td,dwf->wtf/dot_general | solution.py:349
  278.7 13.9 %fusion.45 = (bf16[1,1024,1408]{1,2,0:T(8,128)(2,1)S(1)}, bf16[1,1024,1408]{1,2,0:T(8,128)(2,1)}) fusion(f32[2,1024,1408]{1,2,0:T(8,128)} %fusion.22, bf16[1024,2048]{1,0:T(8,128)(2,1)} %bitcast.151, bf16[1408,1024]{1,0:T(8,128)(2,1)} %get-tuple-element.81, bf16[1408,1024]{1,0:T(8,128)(2,1)} %get-tuple-element.80), kind=kOutput, calls=%fused_computation.80 | convolution fusion | flops 5935857664 | bytes 27262976 | tf_op jit(solution)/shard_map/te,fe->tf/dot_general | solution.py:358
  292.6 1.5 copy-done.31
  294.1 17.6 %bitcast_convert_fusion.2 = bf16[1024,2048]{1,0:T(8,128)(2,1)} fusion(bf16[1024,2,1408]{0,2,1:T(8,128)(2,1)} %get-tuple-element.77, bf16[1024,2,1408]{0,2,1:T(8,128)(2,1)} %get-tuple-element.76, bf16[1,1024,1408]{1,2,0:T(8,128)(2,1)} %get-tuple-element.75, bf16[1,1024,1408]{1,2,0:T(8,128)(2,1)S(1)} %get-tuple-element.74), kind=kOutput, calls=%fused_computation.22 | convolution fusion | flops 11839209472 | bytes 21495808 | tf_op jit(solution)/shard_map/wtf,dwf->td/dot_general | solution.py:364
  311.8 154.1 %all-reduce.14.cloned.1.call-done = bf16[1024,2048]{1,0:T(8,128)(2,1)} async-done(((bf16[1024,2048]{1,0:T(8,128)(2,1)}), bf16[1024,2048]{1,0:T(8,128)(2,1)}) %all-reduce.14.cloned.1.call-update) | async-done | bytes 4194320 | tf_op jit(solution)/shard_map/psum | solution.py:363
  465.9 15.1 %fusion.11 = (bf16[2048]{0:T(1024)(128)(2,1)S(1)}, f32[1024]{0:T(1024)S(1)}) fusion(bf16[1024,2048]{1,0:T(8,128)(2,1)} %all-reduce.14.cloned.1.call-done, bf16[1024,2048]{1,0:T(8,128)(2,1)} %all-reduce.12.cloned.1.call-done, bf16[4,256,2048]{2,1,0:T(8,128)(2,1)} %param.11, f32[1024]{0:T(1024)S(1)} %get-tuple-element.89, f32[2048]{0:T(1024)S(1)} %maximum_convert_fusion.1), kind=kLoop, calls=%fused_computation.18 | loop fusion | flops 20968448 | bytes 12603392 | tf_op jit(solution)/shard_map/reduce_sum | solution.py:368
  481.0 5.2 fusion.8
  486.2 3.4 copy-done.13
  489.6 3.8 convolution_convert_fusion.4
  493.4 11.9 %convolution_convert_fusion.1 = bf16[1408,2048]{1,0:T(8,128)(2,1)} fusion(bf16[1024,2048]{1,0:T(8,128)(2,1)} %bitcast.152, f32[2,1024,1408]{1,2,0:T(8,128)} %fusion.22), kind=kOutput, calls=%fused_computation.37 | convolution fusion | flops 5917114368 | bytes 21495808 | tf_op jit(solution)/shard_map/tf,te->fe/dot_general | solution.py:359
  505.4 6.5 fusion.50
  511.9 3.2 copy-done.1
  515.1 20.1 %scan_backward.1 = (bf16[3,4,256,512]{3,2,1,0:T(8,128)(2,1)S(1)}, f32[1,512]{1,0:T(1,128)S(1)}, f32[1,512]{1,0:T(1,128)S(1)}) custom-call(f32[3,4,256,512]{3,2,1,0:T(8,128)S(1)} %bitcast.136, f32[4,256,1]{2,1,0:T(8,128)S(1)} %copy.47.keep, f32[1,512]{1,0:T(1,128)S(1)} %bitcast.141, f32[1,512]{1,0:T(1,128)S(1)} %bitcast.143, ...), custom_call_target="tpu_custom_call" | custom-call | tf_op jit(solution)/shard_map/scan_backward/pallas_call | solution.py:268
  535.2 1.6 copy-done.6
  536.8 9.0 fusion.23
  545.8 18.3 %convolution_convert_fusion = bf16[2048,2,1408]{2,0,1:T(8,128)(2,1)} fusion(bf16[1024,2048]{1,0:T(8,128)(2,1)} %multiply_convert_fusion, bf16[1,1024,1408]{1,2,0:T(8,128)(2,1)} %get-tuple-element.75, bf16[1,1024,1408]{1,2,0:T(8,128)(2,1)} %copy-done.31), kind=kOutput, calls=%fused_computation.2 | convolution fusion | flops 11828461568 | bytes 21495808 | tf_op jit(solution)/shard_map/td,wtf->dwf/dot_general | solution.py:367
  564.3 13.9 %convolution_convert_fusion.2 = bf16[1024,2048]{1,0:T(8,128)(2,1)} fusion(bf16[1408,1024]{1,0:T(8,128)(2,1)} %get-tuple-element.81, bf16[1408,1024]{1,0:T(8,128)(2,1)} %get-tuple-element.80, f32[2,1024,1408]{1,2,0:T(8,128)} %fusion.22), kind=kOutput, calls=%fused_computation.70 | convolution fusion | flops 5927862272 | bytes 21495808 | tf_op jit(solution)/shard_map/dot_general | solution.py:353
  578.2 8.3 bitcast_convert_fusion.1
  586.7 0.6 all-reduce.18.cloned.1.call-update
  587.3 0.6 dynamic-slice
  588.6 14.1 %all-reduce.2 = (f32[512]{0:T(512)}, f32[512]{0:T(512)}) all-reduce(f32[512]{0:T(512)S(1)} %bitcast.144, f32[512]{0:T(512)S(1)} %bitcast.145), channel_id=1, replica_groups=mesh['fsdp'=2,'ctx'=4,'tp'=4] {'fsdp','ctx'}, use_global_device_ids=true, to_apply=%region_22.23 | all-reduce | flops 1024 | bytes 8192 | tf_op jit(solution)/shard_map/psum | solution.py:412
  602.7 276.4 %all-reduce.16.cloned.1.call-done = (bf16[1024,2048]{1,0:T(8,128)(2,1)}, bf16[1024,2048]{1,0:T(8,128)(2,1)}) async-done(((bf16[1024,2048]{1,0:T(8,128)(2,1)}, bf16[1024,2048]{1,0:T(8,128)(2,1)}), (bf16[1024,2048]{1,0:T(8,128)(2,1)}, bf16[1024,2048]{1,0:T(8,128)(2,1)})) %all-reduce.16.cloned.1.call-update) | async-done | bytes 8388624 | tf_op jit(solution)/shard_map/psum | solution.py:352
  879.1 5.6 fusion.13
  884.7 2.5 all-reduce.6
  887.3 10.4 all-reduce.4
  897.7 0.6 convert_element_type.184
  898.3 0.6 convert_element_type.186
  898.9 16.1 %fusion.5 = (f32[1024,2048]{1,0:T(8,128)}, bf16[1024,2048]{1,0:T(8,128)(2,1)}) fusion(f32[1024,2048]{1,0:T(8,128)} %copy-done.13, bf16[1024,2048]{1,0:T(8,128)(2,1)} %get-tuple-element.65, bf16[4,256,2048]{2,1,0:T(8,128)(2,1)} %param.11, f32[1024]{0:T(1024)S(1)} %broadcast_multiply_fusion, f32[1024]{0:T(1024)S(1)} %multiply_multiply_fusion, ...), kind=kLoop, calls=%fused_computation.12 | loop fusion | flops 27262976 | bytes 37769216 | tf_op jit(solution)/shard_map/sub | solution.py:392
  915.0 213.7 %all-reduce.18.cloned.1.call-done = (bf16[3,1024,512]{1,2,0:T(8,128)(2,1)}, bf16[1024,2,1408]{2,0,1:T(8,128)(2,1)}, bf16[512,1024]{1,0:T(8,128)(2,1)}, bf16[1408,1024]{1,0:T(8,128)(2,1)}) async-done(((bf16[3,1024,512]{1,2,0:T(8,128)(2,1)}, bf16[1024,2,1408]{2,0,1:T(8,128)(2,1)}, bf16[512,1024]{1,0:T(8,128)(2,1)}, bf16[1408,1024]{1,0:T(8,128)(2,1)}), (bf16[3,1024,512]{1,2,0:T(8,128)(2,1)}, ...) | async-done | bytes 12845072 | tf_op jit(solution)/shard_map/psum | solution.py:397
  1128.7 12.8 %copy.57 = f32[1024,2,1408]{2,1,0:T(2,128)} copy(bf16[1024,2,1408]{2,0,1:T(8,128)(2,1)} %get-tuple-element.69) | data formatting | bytes 17301504
  1141.5 3.7 copy.56
  1145.2 5.2 convert_element_type.182
  1150.3 1.6 convert_element_type.176
  (104 shorter events, 1.1 us)
Async XLA Ops:
  7.2 6.1 copy-start.28
  7.2 6.2 copy-start.29
  7.2 6.7 copy-start.26
  7.2 11.2 copy-start.15
  7.2 244.3 %all-reduce.12.cloned.1.call-start = ((), (), s32[]{:S(2)}) async-start(), calls=%async_computation.4 | async-start | bytes 8388608 | tf_op jit(solution)/shard_map/psum | solution.py:343
  12.8 38.3 %collective-permute-start = (bf16[3,1024,512]{1,2,0:T(8,128)(2,1)}, bf16[3,1024,512]{1,2,0:T(8,128)(2,1)}, u32[]{:S(2)}, u32[]{:S(2)}) collective-permute-start(bf16[3,1024,512]{1,2,0:T(8,128)(2,1)} %copy.45), channel_id=1, source_target_pairs={{0,16},{16,0},{1,17},{17,1},{2,18},{18,2},{3,19},{19,3},{4,20},{20... | collective-permute-start | bytes 9437192 | tf_op jit(solution)/shard_map/ppermute | solution.py:299
  13.2 31.4 %collective-permute-start.1 = (bf16[1,1024]{1,0:T(2,128)(2,1)S(1)}, bf16[1,1024]{1,0:T(2,128)(2,1)S(1)}, u32[]{:S(2)}, u32[]{:S(2)}) collective-permute-start(bf16[1,1024]{1,0:T(2,128)(2,1)S(1)} %broadcast_in_dim.23), channel_id=1, source_target_pairs={{0,16},{16,0},{1,17},{17,1},{2,18},{18,2},{3,19},{19,3},{4,20},{20... | collective-permute-start | bytes 6152 | tf_op jit(solution)/shard_map/ppermute | solution.py:299
  13.4 31.5 %collective-permute-start.5 = (bf16[1,1024]{1,0:T(2,128)(2,1)S(1)}, bf16[1,1024]{1,0:T(2,128)(2,1)S(1)}, u32[]{:S(2)}, u32[]{:S(2)}) collective-permute-start(bf16[1,1024]{1,0:T(2,128)(2,1)S(1)} %broadcast_in_dim.28), channel_id=1, source_target_pairs={{0,16},{16,0},{1,17},{17,1},{2,18},{18,2},{3,19},{19,3},{4,20},{20... | collective-permute-start | bytes 6152 | tf_op jit(solution)/shard_map/ppermute | solution.py:299
  14.0 29.9 %collective-permute-start.2 = (f32[4,1]{1,0:T(4,128)S(1)}, f32[4,1]{1,0:T(4,128)S(1)}, u32[]{:S(2)}, u32[]{:S(2)}) collective-permute-start(f32[4,1]{1,0:T(4,128)S(1)} %slice_convert_fusion), channel_id=1, source_target_pairs={{0,4},{4,8},{8,12},{1,5},{5,9},{9,13},{2,6},{6,10},{10,14},{3,7},{... | collective-permute-start | bytes 56 | tf_op jit(solution)/shard_map/ppermute | solution.py:307
  19.5 28.6 %collective-permute-start.3 = (bf16[512,1024]{1,0:T(8,128)(2,1)}, bf16[512,1024]{1,0:T(8,128)(2,1)}, u32[]{:S(2)}, u32[]{:S(2)}) collective-permute-start(bf16[512,1024]{1,0:T(8,128)(2,1)} %convert_element_type.153), channel_id=1, source_target_pairs={{0,16},{16,0},{1,17},{17,1},{2,18},{18,2},{3,19},{19,3},{4,20},{20... | collective-permute-start | bytes 3145736 | tf_op jit(solution)/shard_map/ppermute | solution.py:299
  23.4 21.5 %copy-start.24 = (f32[1,2,4,128]{3,1,2,0:T(2,128)}, f32[1,2,4,128]{3,1,2,0:T(2,128)S(1)}, u32[]{:S(2)}) copy-start(f32[1,2,4,128]{3,1,2,0:T(2,128)S(1)} %copy.66) | copy-start | bytes 12292
  43.9 60.2 %collective-permute-start.4 = (bf16[1024,2,1408]{0,2,1:T(8,128)(2,1)}, bf16[1024,2,1408]{0,2,1:T(8,128)(2,1)}, u32[]{:S(2)}, u32[]{:S(2)}) collective-permute-start(bf16[1024,2,1408]{0,2,1:T(8,128)(2,1)} %copy.48), channel_id=1, source_target_pairs={{0,16},{16,0},{1,17},{17,1},{2,18},{18,2},{3,19},{19,3},{4,20},{20... | collective-permute-start | bytes 17301512 | tf_op jit(solution)/shard_map/ppermute | solution.py:299
  44.6 53.0 %collective-permute-start.6 = (bf16[1408,1024]{1,0:T(8,128)(2,1)}, bf16[1408,1024]{1,0:T(8,128)(2,1)}, u32[]{:S(2)}, u32[]{:S(2)}) collective-permute-start(bf16[1408,1024]{1,0:T(8,128)(2,1)} %convert_element_type.161), channel_id=1, source_target_pairs={{0,16},{16,0},{1,17},{17,1},{2,18},{18,2},{3,19},{19,3},{4,20},{20... | collective-permute-start | bytes 8650760 | tf_op jit(solution)/shard_map/ppermute | solution.py:299
  44.9 6.1 copy-start.22
  54.3 1.8 copy-start.16
  54.3 2.6 copy-start.18
  65.6 6.6 copy-start.4
  65.6 6.6 copy-start.5
  72.1 2.8 copy-start
  90.4 1.0 copy-start.2
  97.3 368.6 %all-reduce.14.cloned.1.call-start = ((), (), s32[]{:S(2)}) async-start(), calls=%async_computation.5 | async-start | bytes 8388608 | tf_op jit(solution)/shard_map/psum | solution.py:363
  251.5 5.0 copy-start.8
  251.5 5.9 copy-start.11
  251.5 9.9 slice-start
  257.4 4.0 slice-start.1
  292.6 1.5 copy-start.31
  311.8 274.8 %reduce-scatter.7.cloned.1.call-start = ((), (), s32[]{:S(2)}) async-start(), calls=%async_computation.7 | async-start | bytes 3145728 | tf_op jit(solution)/shard_map/reduce_scatter | solution.py:398
  465.9 15.1 %copy-start.9 = (bf16[4,256,2048]{2,1,0:T(8,128)(2,1)S(1)}, bf16[4,256,2048]{2,1,0:T(8,128)(2,1)}, u32[]{:S(2)}) copy-start(bf16[4,256,2048]{2,1,0:T(8,128)(2,1)} %param.11) | copy-start | bytes 12582916
  465.9 15.1 %copy-start.12 = (bf16[1024,2048]{1,0:T(8,128)(2,1)S(1)}, bf16[1024,2048]{1,0:T(8,128)(2,1)}, u32[]{:S(2)}) copy-start(bf16[1024,2048]{1,0:T(8,128)(2,1)} %all-reduce.12.cloned.1.call-done) | copy-start | bytes 12582916
  465.9 15.1 %copy-start.14 = (bf16[1024,2048]{1,0:T(8,128)(2,1)S(1)}, bf16[1024,2048]{1,0:T(8,128)(2,1)}, u32[]{:S(2)}) copy-start(bf16[1024,2048]{1,0:T(8,128)(2,1)} %all-reduce.14.cloned.1.call-done) | copy-start | bytes 12582916
  481.0 8.6 copy-start.3
  486.2 3.4 copy-start.13
  493.4 93.2 %reduce-scatter.11.cloned.1.call-start = ((), (), s32[]{:S(2)}) async-start(), calls=%async_computation.9 | async-start | bytes 8650752 | tf_op jit(solution)/shard_map/reduce_scatter | solution.py:398
  505.3 81.3 %reduce-scatter.5.cloned.1.call-start = ((), (), s32[]{:S(2)}) async-start(), calls=%async_computation.6 | async-start | bytes 9437184 | tf_op jit(solution)/shard_map/reduce_scatter | solution.py:398
  505.4 31.4 %copy-start.10 = (bf16[4,256,2048]{2,1,0:T(8,128)(2,1)S(1)}, bf16[4,256,2048]{2,1,0:T(8,128)(2,1)}, u32[]{:S(2)}) copy-start(bf16[4,256,2048]{2,1,0:T(8,128)(2,1)} %param.11) | copy-start | bytes 12582916
  505.4 31.4 %copy-start.23 = (f32[2048]{0:T(1024)S(1)}, f32[2048]{0:T(1024)}, u32[]{:S(2)}) copy-start(f32[2048]{0:T(1024)} %copy-done.22) | copy-start | bytes 24580
  511.9 24.9 %copy-start.27 = (f32[4,256]{1,0:T(4,128)S(1)}, f32[4,256]{1,0:T(4,128)}, u32[]{:S(2)}) copy-start(f32[4,256]{1,0:T(4,128)} %get-tuple-element.86) | copy-start | bytes 12292
  511.9 3.2 copy-start.1
  535.2 1.6 copy-start.6
  545.8 40.9 %reduce-scatter.9.cloned.1.call-start = ((), (), s32[]{:S(2)}) async-start(), calls=%async_computation.8 | async-start | bytes 17301504 | tf_op jit(solution)/shard_map/reduce_scatter | solution.py:398
  564.2 314.9 %all-reduce.16.cloned.1.call-start = ((), (), s32[]{:S(2)}) async-start(), calls=%async_computation.10 | async-start | bytes 16777216 | tf_op jit(solution)/shard_map/psum | solution.py:352
  564.2 13.9 %copy-start.7 = (bf16[3,4,256,512]{3,2,1,0:T(8,128)(2,1)S(1)}, bf16[3,4,256,512]{3,2,1,0:T(8,128)(2,1)}, u32[]{:S(2)}) copy-start(bf16[3,4,256,512]{3,2,1,0:T(8,128)(2,1)} %copy-done.6) | copy-start | bytes 9437188
  564.3 13.9 %copy-start.17 = (bf16[3,1024,512]{1,2,0:T(8,128)(2,1)S(1)}, bf16[3,1024,512]{1,2,0:T(8,128)(2,1)}, u32[]{:S(2)}) copy-start(bf16[3,1024,512]{1,2,0:T(8,128)(2,1)} %copy-done.16) | copy-start | bytes 9437188
  564.3 13.9 %copy-start.19 = (bf16[3,1024,512]{1,2,0:T(8,128)(2,1)S(1)}, bf16[3,1024,512]{1,2,0:T(8,128)(2,1)}, u32[]{:S(2)}) copy-start(bf16[3,1024,512]{1,2,0:T(8,128)(2,1)} %copy-done.18) | copy-start | bytes 9437188
  586.5 542.2 %all-reduce.18.cloned.1.call-start = ((), (), s32[]{:S(2)}) async-start(), calls=%async_computation.11 | async-start | bytes 25690112 | tf_op jit(solution)/shard_map/psum | solution.py:397
  586.7 0.7 copy-start.30
  586.7 1.9 copy-start.25
  1128.7 12.8 %copy-start.20 = (bf16[3,1024,512]{1,2,0:T(8,128)(2,1)S(1)}, bf16[3,1024,512]{1,2,0:T(8,128)(2,1)}, u32[]{:S(2)}) copy-start(bf16[3,1024,512]{1,2,0:T(8,128)(2,1)} %get-tuple-element.68) | copy-start | bytes 9437188
  1145.2 5.2 copy-start.21
Sparse Core Ops, SparseCore 0:
  97.4 154.0 all-reduce.11
  311.9 153.9 all-reduce.13
  493.5 8.5 reduce-scatter.6
  505.5 14.4 reduce-scatter.10
  545.9 12.8 reduce-scatter.4
  564.3 18.5 reduce-scatter.8
  586.6 292.4 all-reduce.15
  883.6 245.0 all-reduce.17

commit v2 on v1

--- a/solution.py
+++ b/solution.py
@@ -293,6 +293,598 @@
     )(proj, keep, gain, lower, state, scale, carry, grad_gated)
 
 
+CHUNK = 256
+PIECES = 4
+TILE = 256
+
+
+def dot(lhs, rhs):
+    return jnp.dot(lhs, rhs, preferred_element_type=FLOAT)
+
+
+def dot_nt(lhs, rhs):
+    return lax.dot_general(lhs, rhs, (((1,), (1,)), ((), ())), preferred_element_type=FLOAT)
+
+
+class Line:
+    def __init__(self, held, cross, total, sems):
+        self.held, self.cross, self.total, self.sems = held, cross, total, sems
+        place = lax.axis_index("tp")
+        self.inner = (place == 1) | (place == 2)
+        self.side = place + 1 - 2 * lax.rem(place, 2)
+        self.facing = 3 - place
+
+    def slot(self, job):
+        slots = self.held.shape[0]
+        return job if slots == self.total.shape[0] else lax.rem(job, slots)
+
+    def copy(self, source, target, send, recv, place):
+        return pltpu.make_async_remote_copy(
+            src_ref=source,
+            dst_ref=target,
+            send_sem=send,
+            recv_sem=recv,
+            device_id={"tp": place},
+            device_id_type=MESH,
+        )
+
+    def inward(self, job, q):
+        send, recv, _, _ = self.sems
+        return self.copy(
+            self.held.at[self.slot(job), q], self.total.at[job, q],
+            send.at[job, q], recv.at[job, q], self.side,
+        )
+
+    def outward(self, job, q):
+        send, recv, _, _ = self.sems
+        return self.copy(
+            self.total.at[job, q], self.total.at[job, q],
+            send.at[job, q], recv.at[job, q], self.side,
+        )
+
+    def across(self, job, q):
+        _, _, send, recv = self.sems
+        return self.copy(
+            self.held.at[self.slot(job), q], self.cross.at[self.slot(job), q],
+            send.at[job, q], recv.at[job, q], self.facing,
+        )
+
+    def offer(self, job, q):
+        @pl.when(jnp.logical_not(self.inner))
+        def _():
+            self.inward(job, q).start()
+
+    def tick(self, job, step):
+        slot = self.slot(job)
+
+        @pl.when(self.inner)
+        def _():
+            if step < PIECES:
+                self.inward(job, step).wait_recv()
+                value = self.held[slot, step].astype(FLOAT) + self.total[job, step].astype(FLOAT)
+                self.held[slot, step] = value.astype(HALF)
+                self.across(job, step).start()
+            if step > 0:
+                q = step - 1
+                self.across(job, q).wait_recv()
+                value = self.held[slot, q].astype(FLOAT) + self.cross[slot, q].astype(FLOAT)
+                self.total[job, q] = value.astype(HALF)
+                self.outward(job, q).start()
+
+    def relay(self, job):
+        for step in range(PIECES + 1):
+            self.tick(job, step)
+
+    def arrive(self, job):
+        @pl.when(jnp.logical_not(self.inner))
+        def _():
+            @pl.loop(0, PIECES)
+            def _(q):
+                self.outward(job, q).wait_recv()
+
+    def release(self, job):
+        @pl.when(self.inner)
+        def _():
+            @pl.loop(0, PIECES)
+            def _(q):
+                self.across(job, q).wait_send()
+
+        @pl.when(jnp.logical_not(self.inner))
+        def _():
+            @pl.loop(0, PIECES)
+            def _(q):
+                self.inward(job, q).wait_send()
+
+    def settle(self, job):
+        @pl.when(self.inner)
+        def _():
+            @pl.loop(0, PIECES)
+            def _(q):
+                self.outward(job, q).wait_send()
+
+
+def pull(parts, wholes, dims, n_fsdp, own_sem, send_sem, recv_sem):
+    if n_fsdp != 2:
+        copies = [
+            pltpu.make_async_copy(part, whole, own_sem.at[index])
+            for index, (part, whole) in enumerate(zip(parts, wholes))
+        ]
+        for copy in copies:
+            copy.start()
+        return lambda index: copies[index].wait()
+    mine = lax.axis_index("fsdp")
+    near, far = [], []
+    for index, (part, whole, dim) in enumerate(zip(parts, wholes, dims)):
+        size = part.shape[dim]
+        at = pl.ds(pl.multiple_of(mine * size, size), size)
+        place = whole.at[at] if dim == 0 else whole.at[:, at]
+        near.append(pltpu.make_async_copy(part, place, own_sem.at[index]))
+        far.append(
+            pltpu.make_async_remote_copy(
+                src_ref=part,
+                dst_ref=place,
+                send_sem=send_sem.at[index],
+                recv_sem=recv_sem.at[index],
+                device_id={"fsdp": 1 - mine},
+                device_id_type=MESH,
+            )
+        )
+    for one, two in zip(near, far):
+        two.start()
+        one.start()
+
+    def wait(index):
+        near[index].wait()
+        far[index].wait()
+
+    return wait
+
+
+def row_blocks(count, size, body):
+    @pl.loop(0, count // size)
+    def _(index):
+        body(pl.ds(pl.multiple_of(index * size, size), size))
+
+
+def line_peers():
+    place = lax.axis_index("tp")
+    return [{"tp": place + 1 - 2 * lax.rem(place, 2)}, {"tp": 3 - place}]
+
+
+def joined(ref, c, rows):
+    return jnp.concatenate([ref[c, q, rows, :].astype(FLOAT) for q in range(PIECES)], -1)
+
+
+def middle(
+    n_fsdp,
+    gated, tokens, cotangent, gain, wo_part, wg_part, wu_part, wd_part,
+    mixed_out, normed_out, act_out, grad_glu_out, down_out, grad_resid_out, grad_mixed_out,
+    grad_gated_out, grad_gain_out,
+    wo, wg, wu, wd, x_all, dy_all, held, crossed, total, normed, act, grad_glu, down,
+    grad_resid, grad_mixed, grad_gated, gain_total,
+    own_sem, send_sem, recv_sem, load_sem, store_sem, *line_sems,
+):
+    n_chunks, _, _, piece = held.shape
+    units = wd.shape[0]
+    width = wd.shape[1]
+    peers = line_peers()
+    if n_fsdp == 2:
+        peers.append({"fsdp": 1 - lax.axis_index("fsdp")})
+    greet(peers)
+    ready = pull(
+        (wo_part, wg_part, wu_part, wd_part), (wo, wg, wu, wd), (1, 0, 0, 1),
+        n_fsdp, own_sem, send_sem, recv_sem,
+    )
+    loads = [
+        pltpu.make_async_copy(tokens, x_all, load_sem.at[0]),
+        pltpu.make_async_copy(cotangent, dy_all, load_sem.at[1]),
+    ]
+    for load in loads:
+        load.start()
+    line = Line(held, crossed, total, line_sems)
+
+    def chunk_rows(c):
+        return pl.ds(pl.multiple_of(c * CHUNK, CHUNK), CHUNK)
+
+    def stores(c, wanted=None):
+        rows = chunk_rows(c)
+        pairs = [
+            (normed, normed_out.at[rows]),
+            (act, act_out.at[rows]),
+            (grad_glu.at[0], grad_glu_out.at[0, rows]),
+            (grad_glu.at[1], grad_glu_out.at[1, rows]),
+            (down, down_out.at[rows]),
+            (grad_resid, grad_resid_out.at[rows]),
+            (grad_mixed, grad_mixed_out.at[rows]),
+            (grad_gated, grad_gated_out.at[rows]),
+        ]
+        pairs += [
+            (total.at[c, q], mixed_out.at[rows, pl.ds(q * piece, piece)]) for q in range(PIECES)
+        ]
+        return [
+            pltpu.make_async_copy(source, target, store_sem.at[index])
+            for index, (source, target) in enumerate(pairs)
+            if wanted is None or index in wanted
+        ]
+
+    FORWARD = (0, 1, 2, 3, 4, 8, 9, 10, 11)
+    BACKWARD = (5, 6, 7)
+
+    ready(0)
+
+    @pl.loop(0, n_chunks)
+    def _(c):
+        lhs = gated[chunk_rows(c), :]
+
+        @pl.loop(0, PIECES)
+        def _(q):
+            for half in range(piece // TILE):
+                cols = pl.ds(pl.multiple_of(q * piece + half * TILE, TILE), TILE)
+                held[c, q, :, half * TILE : (half + 1) * TILE] = dot(lhs, wo[:, cols]).astype(HALF)
+            line.offer(c, q)
+
+    for load in loads:
+        load.wait()
+    line.relay(0)
+    for index in (1, 2, 3):
+        ready(index)
+
+    @pl.loop(0, n_chunks)
+    def _(c):
+        line.arrive(c)
+        line.tick(c + 1, 0)
+
+        @pl.when(c > 0)
+        def _():
+            for store in stores(c - 1, FORWARD):
+                store.wait()
+
+        def norm(rows):
+            at = pl.ds(pl.multiple_of(c * CHUNK + rows.start, 16), rows.size)
+            resid = x_all[at, :].astype(FLOAT) + joined(total, c, rows)
+            normed[rows, :] = (resid * rms_scale(resid) * gain[...]).astype(HALF)
+
+        row_blocks(CHUNK, 16, norm)
+
+        def unit(cols):
+            glu_gate = dot(normed[...], wg[:, cols])
+            glu_up = dot(normed[...], wu[:, cols])
+            grad_act = dot_nt(dy_all[chunk_rows(c), :], wd[cols, :])
+            sig = jax.nn.sigmoid(glu_gate)
+            silu = glu_gate * sig
+            act[:, cols] = (silu * glu_up).astype(HALF)
+            slope = sig * (1.0 + glu_gate * (1.0 - sig))
+            grad_glu[0, :, cols] = (grad_act * glu_up * slope).astype(HALF)
+            grad_glu[1, :, cols] = (grad_act * silu).astype(HALF)
+
+        def units_from(start, stop):
+            @pl.loop(start, stop)
+            def _(index):
+                unit(pl.ds(pl.multiple_of(index * TILE, TILE), TILE))
+
+        half_way = units // TILE // 2
+        units_from(0, half_way)
+        line.tick(c + 1, 1)
+        units_from(half_way, units // TILE)
+        if units % TILE:
+            unit(pl.ds(units - units % TILE, units % TILE))
+        line.tick(c + 1, 2)
+        line.release(c)
+
+        @pl.loop(0, PIECES)
+        def _(q):
+            @pl.when(q == PIECES // 2)
+            def _():
+                line.tick(c + 1, 3)
+
+            for half in range(piece // TILE):
+                at = pl.ds(pl.multiple_of(q * piece + half * TILE, TILE), TILE)
+                value = dot_nt(grad_glu[0], wg[at, :]) + dot_nt(grad_glu[1], wu[at, :])
+                held[c, q, :, half * TILE : (half + 1) * TILE] = value.astype(HALF)
+            line.offer(n_chunks + c, q)
+
+        line.tick(c + 1, 4)
+
+        @pl.loop(0, width // TILE)
+        def _(index):
+            cols = pl.ds(pl.multiple_of(index * TILE, TILE), TILE)
+            down[:, cols] = dot(act[...], wd[:, cols]).astype(HALF)
+
+        for store in stores(c, FORWARD):
+            store.start()
+
+    gain_total[...] = jnp.zeros_like(gain_total)
+
+    @pl.loop(0, n_chunks)
+    def _(c):
+        @pl.when(c > 0)
+        def _():
+            line.relay(n_chunks + c)
+
+        line.arrive(n_chunks + c)
+
+        @pl.when(c > 0)
+        def _():
+            for store in stores(c - 1, BACKWARD):
+                store.wait()
+
+        def norm_back(rows):
+            at = pl.ds(pl.multiple_of(c * CHUNK + rows.start, 16), rows.size)
+            resid = x_all[at, :].astype(FLOAT) + joined(total, c, rows)
+            rate = rms_scale(resid)
+            grad = joined(total, n_chunks + c, rows)
+            by_gain = grad * (resid * rate)
+            gain_total[...] += by_gain[:8] + by_gain[8:]
+            inner = gain[...] * grad
+            mean = jnp.mean(inner * resid, -1, keepdims=True)
+            value = dy_all[at, :].astype(FLOAT) + rate * inner - resid * (rate * rate * rate * mean)
+            grad_resid[rows, :] = value
+            grad_mixed[rows, :] = value.astype(HALF)
+
+        row_blocks(CHUNK, 16, norm_back)
+        for start in range(0, grad_gated.shape[1], TILE):
+            grad_gated[:, start : start + TILE] = dot_nt(
+                grad_mixed[...], wo[start : start + TILE, :]
+            )
+        for store in stores(c, BACKWARD):
+            store.start()
+
+    grad_gain_out[...] = jnp.sum(gain_total[...], 0, keepdims=True)
+    for store in stores(n_chunks - 1):
+        store.wait()
+
+    @pl.loop(0, n_chunks)
+    def _(c):
+        line.settle(c)
+        line.settle(n_chunks + c)
+        line.release(n_chunks + c)
+
+
+def run_middle(gated, tokens, cotangent, gain, parts, n_fsdp):
+    rows, chan = gated.shape
+    width = tokens.shape[1]
+    wg = parts[1]
+    units = wg.shape[1]
+    n_chunks = rows // CHUNK
+    piece = width // PIECES
+    vmem = pl.BlockSpec(memory_space=pltpu.VMEM)
+    hbm = pl.BlockSpec(memory_space=pl.ANY)
+    sems = pltpu.SemaphoreType.DMA((2 * n_chunks, PIECES))
+    return pl.pallas_call(
+        functools.partial(middle, n_fsdp),
+        name="middle",
+        out_shape=(
+            jax.ShapeDtypeStruct((rows, width), HALF),
+            jax.ShapeDtypeStruct((rows, width), HALF),
+            jax.ShapeDtypeStruct((rows, units), HALF),
+            jax.ShapeDtypeStruct((2, rows, units), HALF),
+            jax.ShapeDtypeStruct((rows, width), HALF),
+            jax.ShapeDtypeStruct((rows, width), FLOAT),
+            jax.ShapeDtypeStruct((rows, width), HALF),
+            jax.ShapeDtypeStruct((rows, chan), FLOAT),
+            jax.ShapeDtypeStruct((1, width), FLOAT),
+        ),
+        in_specs=[vmem, hbm, hbm, vmem, hbm, hbm, hbm, hbm],
+        out_specs=[hbm] * 8 + [vmem],
+        scratch_shapes=[
+            pltpu.VMEM((chan, width), HALF),
+            pltpu.VMEM((width, units), HALF),
+            pltpu.VMEM((width, units), HALF),
+            pltpu.VMEM((units, width), HALF),
+            pltpu.VMEM((rows, width), HALF),
+            pltpu.VMEM((rows, width), HALF),
+            pltpu.VMEM((n_chunks, PIECES, CHUNK, piece), HALF),
+            pltpu.VMEM((n_chunks, PIECES, CHUNK, piece), HALF),
+            pltpu.VMEM((2 * n_chunks, PIECES, CHUNK, piece), HALF),
+            pltpu.VMEM((CHUNK, width), HALF),
+            pltpu.VMEM((CHUNK, units), HALF),
+            pltpu.VMEM((2, CHUNK, units), HALF),
+            pltpu.VMEM((CHUNK, width), HALF),
+            pltpu.VMEM((CHUNK, width), FLOAT),
+            pltpu.VMEM((CHUNK, width), HALF),
+            pltpu.VMEM((CHUNK, chan), FLOAT),
+            pltpu.VMEM((8, width), FLOAT),
+            pltpu.SemaphoreType.DMA((4,)),
+            pltpu.SemaphoreType.DMA((4,)),
+            pltpu.SemaphoreType.DMA((4,)),
+            pltpu.SemaphoreType.DMA((2,)),
+            pltpu.SemaphoreType.DMA((12,)),
+        ]
+        + [sems] * 4,
+        compiler_params=pltpu.CompilerParams(
+            collective_id=2, has_side_effects=True, vmem_limit_bytes=63 * MIB
+        ),
+        cost_estimate=pl.CostEstimate(
+            flops=16 * rows * width * units, bytes_accessed=400 * MIB, transcendentals=0
+        ),
+    )(gated, tokens, cotangent, gain, *parts)
+
+
+def tail(
+    n_fsdp, n_ctx,
+    grad_proj, gain, vectors, w_in, down, grad_resid, tokens, mixed,
+    grad_tokens_out, output_out, vectors_out,
+    w_all, resid_all, x_all, mixed_all, held, crossed, total, gain_total, over_ctx, over_fsdp,
+    load_sem, down_sem, store_sem, ctx_send, ctx_recv, fsdp_send, fsdp_recv, *line_sems,
+):
+    rows, width = x_all.shape
+    n_chunks = rows // CHUNK
+    piece = width // PIECES
+    greet(line_peers() + others("ctx", n_ctx) + others("fsdp", n_fsdp))
+    loads = [
+        pltpu.make_async_copy(source, target, load_sem.at[index])
+        for index, (source, target) in enumerate(
+            [(w_in, w_all), (grad_resid, resid_all), (tokens, x_all), (mixed, mixed_all)]
+        )
+    ]
+    for load in loads:
+        load.start()
+
+    def chunk_rows(c):
+        return pl.ds(pl.multiple_of(c * CHUNK, CHUNK), CHUNK)
+
+    def down_load(c, q):
+        cols = pl.ds(pl.multiple_of(q * piece, piece), piece)
+        return pltpu.make_async_copy(
+            down.at[chunk_rows(c), cols], held.at[n_chunks + c, q], down_sem.at[c, q]
+        )
+
+    def every(body):
+        @pl.loop(0, n_chunks)
+        def _(c):
+            @pl.loop(0, PIECES)
+            def _(q):
+                body(c, q)
+
+    every(lambda c, q: down_load(c, q).start())
+    line = Line(held, crossed, total, line_sems)
+    loads[0].wait()
+
+    def term(c, q):
+        for half in range(piece // TILE):
+            at = pl.ds(pl.multiple_of(q * piece + half * TILE, TILE), TILE)
+            value = dot_nt(grad_proj[0, chunk_rows(c), :], w_all[0, at, :])
+            for gate in (1, 2):
+                value = value + dot_nt(grad_proj[gate, chunk_rows(c), :], w_all[gate, at, :])
+            held[c, q, :, half * TILE : (half + 1) * TILE] = value.astype(HALF)
+        line.offer(c, q)
+
+    every(term)
+
+    def hand_on(c, q):
+        down_load(c, q).wait()
+        line.offer(n_chunks + c, q)
+
+    every(hand_on)
+    for load in loads[1:]:
+        load.wait()
+    gain_total[...] = jnp.zeros_like(gain_total)
+    line.relay(0)
+
+    def token_store(c):
+        at = chunk_rows(c)
+        return pltpu.make_async_copy(resid_all.at[at], grad_tokens_out.at[at], store_sem.at[0, c])
+
+    def output_store(c):
+        at = chunk_rows(c)
+        return pltpu.make_async_copy(mixed_all.at[at], output_out.at[at], store_sem.at[1, c])
+
+    @pl.loop(0, n_chunks)
+    def _(c):
+        line.arrive(c)
+        for quarter in range(PIECES):
+            line.tick(c + 1, quarter)
+
+            @pl.loop(0, CHUNK // PIECES // 16)
+            def _(index):
+                start = quarter * (CHUNK // PIECES) + index * 16
+                rows = pl.ds(pl.multiple_of(start, 16), 16)
+                at = pl.ds(pl.multiple_of(c * CHUNK + start, 16), 16)
+                value = x_all[at, :].astype(FLOAT)
+                rate = rms_scale(value)
+                grad = joined(total, c, rows)
+                by_gain = grad * (value * rate)
+                gain_total[...] += by_gain[:8] + by_gain[8:]
+                inner = gain[...] * grad
+                mean = jnp.mean(inner * value, -1, keepdims=True)
+                resid_all[at, :] = (
+                    resid_all[at, :] + rate * inner - value * (rate * rate * rate * mean)
+                )
+
+        line.tick(c + 1, PIECES)
+        token_store(c).start()
+
+    here = lax.axis_index("ctx")
+    over_ctx[here, :, width:] = vectors[...]
+    over_ctx[here, :, :width] = jnp.sum(gain_total[...], 0, keepdims=True)
+    share(over_ctx, "ctx", n_ctx, ctx_send, ctx_recv)
+    value = over_ctx[0]
+    for place in range(1, n_ctx):
+        value = value + over_ctx[place]
+    over_fsdp[lax.axis_index("fsdp")] = value
+    share(over_fsdp, "fsdp", n_fsdp, fsdp_send, fsdp_recv)
+    value = over_fsdp[0]
+    for place in range(1, n_fsdp):
+        value = value + over_fsdp[place]
+    vectors_out[...] = value
+
+    @pl.loop(0, n_chunks)
+    def _(c):
+        job = n_chunks + c
+        line.arrive(job)
+
+        @pl.when(c + 1 < n_chunks)
+        def _():
+            line.relay(job + 1)
+
+        @pl.loop(0, CHUNK // 16)
+        def _(index):
+            rows = pl.ds(pl.multiple_of(index * 16, 16), 16)
+            at = pl.ds(pl.multiple_of(c * CHUNK + index * 16, 16), 16)
+            value = x_all[at, :].astype(FLOAT) + mixed_all[at, :].astype(FLOAT)
+            mixed_all[at, :] = (value + joined(total, job, rows)).astype(HALF)
+
+        output_store(c).start()
+
+    for c in range(n_chunks):
+        token_store(c).wait()
+        output_store(c).wait()
+
+    @pl.loop(0, 2 * n_chunks)
+    def _(job):
+        line.settle(job)
+        line.release(job)
+
+
+def run_tail(grad_proj, gain, vectors, w_in, down, grad_resid, tokens, mixed, n_fsdp, n_ctx):
+    _, rows, chan = grad_proj.shape
+    width = tokens.shape[1]
+    n_chunks = rows // CHUNK
+    piece = width // PIECES
+    size = width + vectors.shape[1]
+    vmem = pl.BlockSpec(memory_space=pltpu.VMEM)
+    hbm = pl.BlockSpec(memory_space=pl.ANY)
+    slots = pltpu.VMEM((2 * n_chunks, PIECES, CHUNK, piece), HALF)
+    sems = pltpu.SemaphoreType.DMA((2 * n_chunks, PIECES))
+    return pl.pallas_call(
+        functools.partial(tail, n_fsdp, n_ctx),
+        name="tail",
+        out_shape=(
+            jax.ShapeDtypeStruct((rows, width), FLOAT),
+            jax.ShapeDtypeStruct((rows, width), HALF),
+            jax.ShapeDtypeStruct((1, size), FLOAT),
+        ),
+        in_specs=[vmem] * 3 + [hbm] * 5,
+        out_specs=[hbm, hbm, vmem],
+        scratch_shapes=[
+            pltpu.VMEM((3, width, chan), HALF),
+            pltpu.VMEM((rows, width), FLOAT),
+            pltpu.VMEM((rows, width), HALF),
+            pltpu.VMEM((rows, width), HALF),
+            slots,
+            slots,
+            slots,
+            pltpu.VMEM((8, width), FLOAT),
+            pltpu.VMEM((n_ctx, 1, size), FLOAT),
+            pltpu.VMEM((n_fsdp, 1, size), FLOAT),
+            pltpu.SemaphoreType.DMA((4,)),
+            pltpu.SemaphoreType.DMA((n_chunks, PIECES)),
+            pltpu.SemaphoreType.DMA((2, n_chunks)),
+            pltpu.SemaphoreType.DMA((n_ctx,)),
+            pltpu.SemaphoreType.DMA((n_ctx,)),
+            pltpu.SemaphoreType.DMA((n_fsdp,)),
+            pltpu.SemaphoreType.DMA((n_fsdp,)),
+        ]
+        + [sems] * 4,
+        compiler_params=pltpu.CompilerParams(
+            collective_id=3, has_side_effects=True, vmem_limit_bytes=63 * MIB
+        ),
+        cost_estimate=pl.CostEstimate(
+            flops=6 * rows * width * chan, bytes_accessed=700 * MIB, transcendentals=0
+        ),
+    )(grad_proj, gain, vectors, w_in, down, grad_resid, tokens, mixed)
+
+
 def gather_fsdp(part, dim, count):
     if count != 2:
         return lax.all_gather(part, "fsdp", axis=dim, tiled=True)
@@ -325,9 +917,9 @@
     gain_a = gather_fsdp(gain_one.astype(HALF)[None], 1, n_fsdp).astype(FLOAT)
     gain_b = gather_fsdp(gain_two.astype(HALF)[None], 1, n_fsdp).astype(FLOAT)
     w_in_all = gather_fsdp(w_in.astype(HALF), 1, n_fsdp)
-    w_out_all = gather_fsdp(w_out.astype(HALF), 1, n_fsdp)
-    w_glu_all = gather_fsdp(w_glu.astype(HALF), 0, n_fsdp)
-    w_down_all = gather_fsdp(w_down.astype(HALF), 1, n_fsdp)
+    parts = (w_out.astype(HALF), w_glu[:, 0].astype(HALF), w_glu[:, 1].astype(HALF), w_down.astype(HALF))
+    if n_fsdp != 2:
+        parts = tuple(gather_fsdp(part, dim, n_fsdp) for part, dim in zip(parts, (1, 0, 0, 1)))
     keep = keep_flags(segment_ids, n_ctx)[..., None]
     gain_gate = gate_gain[None]
     low = lower[None]
@@ -340,59 +932,24 @@
         proj, keep, gain_gate, low, n_ctx, n_tp, width
     )
     gated = gated.reshape(rows, chan)
-    mixed = lax.psum(
-        jnp.dot(gated, w_out_all, preferred_element_type=FLOAT).astype(HALF), "tp"
-    ).astype(FLOAT)
-    resid = flat + mixed
-    scale_two = rms_scale(resid)
-    normed_two = (resid * scale_two * gain_b).astype(HALF)
-    glu = jnp.einsum("td,dwf->wtf", normed_two, w_glu_all, preferred_element_type=FLOAT)
-    silu_glu = jax.nn.silu(glu[0])
-    act = (silu_glu * glu[1]).astype(HALF)
-    down = lax.psum(
-        jnp.dot(act, w_down_all, preferred_element_type=FLOAT).astype(HALF), "tp"
-    ).astype(FLOAT)
-    output = (resid + down).astype(HALF).reshape(n_seq, length, width)
     grad_y_half = cotangent.reshape(rows, width)
-    grad_y = grad_y_half.astype(FLOAT)
-    grad_act = jnp.einsum("te,fe->tf", grad_y_half, w_down_all, preferred_element_type=FLOAT)
+    (
+        mixed, normed_two, act, grad_glu, down, grad_resid, grad_mixed, grad_gated, grad_gain_two
+    ) = run_middle(gated, tokens.reshape(rows, width), grad_y_half, gain_b, parts, n_fsdp)
     grad_w_down = jnp.einsum("tf,te->fe", act, grad_y_half, preferred_element_type=FLOAT)
-    grad_gate_pre = grad_act * glu[1] * silu_slope(glu[0])
-    grad_up_pre = grad_act * silu_glu
-    grad_glu = jnp.stack([grad_gate_pre, grad_up_pre]).astype(HALF)
-    grad_normed_two = lax.psum(
-        jnp.einsum("wtf,dwf->td", grad_glu, w_glu_all, preferred_element_type=FLOAT).astype(HALF),
-        "tp",
-    ).astype(FLOAT)
     grad_w_glu = jnp.einsum("td,wtf->dwf", normed_two, grad_glu, preferred_element_type=FLOAT)
-    grad_gain_two = jnp.sum(grad_normed_two * resid * scale_two, 0)
-    inner_two = gain_b * grad_normed_two
-    grad_resid = (
-        grad_y
-        + scale_two * inner_two
-        - resid * scale_two**3 * jnp.mean(inner_two * resid, -1, keepdims=True)
-    )
-    grad_mixed = grad_resid.astype(HALF)
-    grad_gated = jnp.einsum(
-        "te,ce->tc", grad_mixed, w_out_all, preferred_element_type=FLOAT
-    ).reshape(n_seq, length, chan)
+    grad_gated = grad_gated.reshape(n_seq, length, chan)
     grad_w_out = jnp.einsum("tc,te->ce", gated, grad_mixed, preferred_element_type=FLOAT)
     grad_proj, grad_gate_gain, grad_lower = run_scan_backward(
         proj, keep, gain_gate, low, state, gate_scale, carry, grad_gated, n_ctx, n_tp, width
     )
     grad_proj = grad_proj.reshape(3, rows, chan)
-    grad_normed = lax.psum(
-        jnp.einsum("wtc,wdc->td", grad_proj, w_in_all, preferred_element_type=FLOAT).astype(HALF),
-        "tp",
-    ).astype(FLOAT)
+    vectors = jnp.concatenate([grad_gain_two, grad_gate_gain, grad_lower], 1)
+    grad_tokens, output, vectors = run_tail(
+        grad_proj, gain_a, vectors, w_in_all, down, grad_resid,
+        tokens.reshape(rows, width), mixed, n_fsdp, n_ctx,
+    )
     grad_w_in = jnp.einsum("td,wtc->wdc", normed, grad_proj, preferred_element_type=FLOAT)
-    grad_gain_one = jnp.sum(grad_normed * flat * scale_one, 0)
-    inner_one = gain_a * grad_normed
-    grad_tokens = (
-        grad_resid
-        + scale_one * inner_one
-        - flat * scale_one**3 * jnp.mean(inner_one * flat, -1, keepdims=True)
-    )
     pieces = [
         lax.psum(
             lax.psum_scatter(
@@ -405,17 +962,18 @@
             (grad_w_out, 1),
             (grad_w_glu, 0),
             (grad_w_down, 1),
-            (grad_gain_one, 0),
-            (grad_gain_two, 0),
         )
     ]
-    channel = lax.psum((grad_gate_gain[0], grad_lower[0]), ("fsdp", "ctx"))
+    part = gain_one.shape[0]
+    begin = lax.axis_index("fsdp") * part
     return (
-        output,
+        output.reshape(n_seq, length, width),
         grad_tokens.reshape(n_seq, length, width),
         *pieces,
-        channel[0],
-        channel[1],
+        lax.dynamic_slice(vectors[0], (begin,), (part,)),
+        lax.dynamic_slice(vectors[0], (width + begin,), (part,)),
+        vectors[0, 2 * width : 2 * width + chan],
+        vectors[0, 2 * width + chan :],
     )
 
 

time: 1170 us -> 700 us (0.60)
  waiting for transfers between devices: 783 us -> 35.1 us
  Pallas kernels: 35.5 us -> 496 us
  matrix products: 135 us -> 53.1 us
  other arithmetic: 93.9 us -> 30.1 us
  blocking collectives: 27 us -> 0 us
    psum x3 -> x0, waiting for transfers between devices: 568 us -> none  [the longest x1 276 us: local(): lax.psum(jnp.dot(act, w_down_all, preferred_element_type=FLOAT).astype(HA...]
    pallas_call x0 -> x2, Pallas kernels: none -> 462 us  [the longest x1 236 us: run_middle(): pl.pallas_call(functools.partial(middle, n_fsdp), name='middle', out_shap...]
    psum x1, waiting for transfers between devices: 214 us -> 16 us  [local(): lax.psum(lax.psum_scatter(value.astype(HALF), 'fsdp', scatter_dimension=d...]
    dot_general x7 -> x0, matrix products: 83.4 us -> none  [the longest x1 17.6 us: local(): jnp.einsum('wtf,dwf->td', grad_glu, w_glu_all, preferred_element_type=FLOAT)]
    psum x2 -> x0, blocking collectives: 24.5 us -> none  [the longest x1 14.1 us: local(): channel = lax.psum((grad_gate_gain[0], grad_lower[0]), ('fsdp', 'ctx'))]
    sub x2 -> x0, other arithmetic: 21.2 us -> none  [the longest x1 16.1 us: local(): grad_resid + scale_one * inner_one]
    reduce_sum x2 -> x0, other arithmetic: 20.7 us -> none  [the longest x1 15.1 us: local(): grad_gain_two = jnp.sum(grad_normed_two * resid * scale_two, 0)]
    reduce_scatter x4, waiting for transfers between devices: 0.07 us -> 19.1 us  [local(): lax.psum_scatter(value.astype(HALF), 'fsdp', scatter_dimension=dim, tiled...]
  transfers between devices with their start and end apart: 15 -> 9, of which waited for: 4 -> 2; matrix products, arithmetic and copies ran while one was open for 14% -> 9% of each run, Pallas kernels for 3% -> 35%
where the time goes in v2:
time: 700 us; the launch traced here: 692 us
  Pallas kernels  496 us (71%)
  local copies, waits for them, and re-layouts  57.6 us (8%)
  matrix products  53.1 us (8%)
  waiting for transfers between devices  35.1 us (5%)
  other arithmetic  30.1 us (4%)
  between operations  14.5 us (2%)
    pallas_call x1, Pallas kernels, run_middle(): pl.pallas_call(functools.partial(middle, n_fsdp), name='middle', out_shap...  236 us
    pallas_call x1, Pallas kernels, run_tail(): pl.pallas_call(functools.partial(tail, n_fsdp, n_ctx), name='tail', out_s...  226 us
    unnamed x54, local copies, waits for them, and re-layouts  45.2 us
    reduce_scatter x4, waiting for transfers between devices, local(): lax.psum_scatter(value.astype(HALF), 'fsdp', scatter_dimension=dim, tiled...  19.1 us
    pallas_call x1, Pallas kernels, run_scan_backward(): pl.pallas_call(functools.partial(scan_backward, n_ctx, n_tp, width), name...  18.6 us
    dot_general x1, matrix products, local(): jnp.einsum('td,wtf->dwf', normed_two, grad_glu, preferred_element_type=FL...  18.3 us
    psum x1, waiting for transfers between devices, local(): lax.psum(lax.psum_scatter(value.astype(HALF), 'fsdp', scatter_dimension=d...  16 us
    pallas_call x1, Pallas kernels, run_scan_forward(): pl.pallas_call(functools.partial(scan_forward, n_ctx, n_tp, width), name=...  15.4 us
  transfers between devices with their start and end apart: 9, of which 2 were waited for; matrix products, arithmetic and copies ran while one was open for 9% of the time, Pallas kernels for 35%

profile of v2, /device:TPU:0, one launch (start us, length us, event | category | flops | bytes accessed | tf_op | source)
XLA Modules:
  0.0 692.3 jit_solution(11884104924051532476)
XLA Ops:
  7.2 0.0 reduce-scatter.7.cloned.1.call-start
  7.3 4.9 convert_element_type.78
  12.1 0.5 collective-permute-start
  12.6 0.1 collective-permute-start.3
  12.7 0.5 collective-permute-start.1
  13.2 0.1 slice_convert_fusion
  13.3 4.4 collective-permute-start.2
  17.7 3.1 fusion
  20.9 1.1 convert_element_type.89.wo_part
  22.0 4.9 copy.44
  26.9 4.7 convert_element_type.92.wd_part
  31.7 3.0 slice_bitcast_fusion
  34.6 0.1 select_bitcast_fusion
  34.7 0.2 copy.32.keep
  35.0 0.6 maximum_convert_fusion.gain
  35.6 4.4 broadcast_select_fusion.1
  40.1 1.6 copy-done.11
  41.7 1.0 copy-done.13
  42.8 9.1 %fusion.14 = f32[3,1024,512]{1,2,0:T(8,128)} fusion(bf16[1024,2048]{1,0:T(8,128)(2,1)S(1)} %bitcast.62, f32[2048]{0:T(1024)S(1)} %maximum_convert_fusion.2, f32[1024]{0:T(1024)S(1)} %bitcast.70, bf16[3,1024,512]{2,1,0:T(8,128)(2,1)S(1)} %get-tuple-element.77, bf16[3,1024,512]{2,1,0:T(8,128)(2,1)S(1)} %get-tuple-element.76), kind=kOutput, calls=%fused_computation.25 | convolution fusion | flops 6463422464 | bytes 16789504 | tf_op jit(solution)/shard_map/td,wdc->wtc/dot_general | solution.py:929
  51.9 6.6 copy.29
  58.5 2.8 copy-done
  61.3 15.4 %scan_forward.1 = (bf16[4,256,512]{2,1,0:T(8,128)(2,1)S(1)}, f32[4,256,512]{2,1,0:T(8,128)S(1)}, f32[4,256]{1,0:T(4,128)S(1)}, f32[4,512]{1,0:T(4,128)S(1)}) custom-call(f32[3,4,256,512]{3,2,1,0:T(8,128)S(1)} %bitcast.50, f32[4,256,1]{2,1,0:T(8,128)S(1)} %copy.32.keep, f32[1,512]{1,0:T(1,128)S(1)} %bitcast.54, f32[1,512]{1,0:T(1,128)S(1)} %bitcast.56), custom_call_target="tpu_custom_call" | custom-call | tf_op jit(solution)/shard_map/scan_forward/pallas_call | solution.py:136
  76.7 0.0 copy-start.3
  76.7 1.3 copy-done.3
  78.0 1.0 copy-done.8
  79.0 235.8 %middle.1 = (bf16[1024,2048]{1,0:T(8,128)(2,1)}, bf16[1024,2048]{1,0:T(8,128)(2,1)}, bf16[1024,1408]{1,0:T(8,128)(2,1)}, bf16[2,1024,1408]{2,1,0:T(8,128)(2,1)},...) custom-call(bf16[1024,512]{1,0:T(8,128)(2,1)} %bitcast.58, ...), custom_call_target="tpu_custom_call" | custom-call | flops 47244640256 | bytes 419430400 | tf_op jit(solution)/shard_map/middle/pallas_call | solution.py:653
  314.8 6.2 convolution_convert_fusion.2
  321.0 0.0 reduce-scatter.7.cloned.1.call-update
  321.0 0.0 reduce-scatter.11.cloned.1.call-start
  321.1 10.4 %convolution_convert_fusion.1 = bf16[1408,2048]{1,0:T(8,128)(2,1)} fusion(bf16[1024,1408]{1,0:T(8,128)(2,1)} %get-tuple-element.46, bf16[1024,2048]{1,0:T(8,128)(2,1)} %bitcast.74), kind=kOutput, calls=%fused_computation.9 | convolution fusion | flops 5908463616 | bytes 12845056 | tf_op jit(solution)/shard_map/tf,te->fe/dot_general | solution.py:939
  331.5 0.0 reduce-scatter.11.cloned.1.call-update
  331.5 0.3 reduce-scatter.5.cloned.1.call-start
  331.8 1.3 copy-done.4
  333.1 2.8 copy-done.1
  335.9 1.6 copy-done.5
  337.5 18.6 %scan_backward.1 = (bf16[3,4,256,512]{3,2,1,0:T(8,128)(2,1)S(1)}, f32[1,512]{1,0:T(1,128)S(1)}, f32[1,512]{1,0:T(1,128)S(1)}) custom-call(f32[3,4,256,512]{3,2,1,0:T(8,128)S(1)} %bitcast.51, f32[4,256,1]{2,1,0:T(8,128)S(1)} %copy.32.keep, f32[1,512]{1,0:T(1,128)S(1)} %bitcast.55, f32[1,512]{1,0:T(1,128)S(1)} %bitcast.57, f32[4,256,512]{2,1,0:T(8,128)S(1)} %copy-done.4, ...), custom_call_target="tpu_custom_call" | custom-call | tf_op jit(solution)/shard_map/scan_backward/pallas_call | solution.py:268
  356.1 1.7 copy-done.2
  357.8 9.0 %fusion.3 = bf16[3,2048,512]{1,2,0:T(8,128)(2,1)} fusion(bf16[3,4,256,512]{3,2,1,0:T(8,128)(2,1)S(1)} %get-tuple-element.34, bf16[4,256,2048]{2,1,0:T(8,128)(2,1)S(1)} %copy-done.10, f32[2048]{0:T(1024)S(1)} %maximum_convert_fusion.2, f32[4,256]{1,0:T(4,128)S(1)} %get-tuple-element.88), kind=kOutput, calls=%fused_computation.10 | convolution fusion | flops 6453985280 | bytes 13643776 | tf_op jit(solution)/shard_map/td,wtc->wdc/dot_general | solution.py:952
  366.7 0.0 reduce-scatter.5.cloned.1.call-update
  366.7 0.0 reduce-scatter.9.cloned.1.call-start
  366.8 18.3 %convolution_convert_fusion = bf16[2048,2,1408]{2,0,1:T(8,128)(2,1)} fusion(bf16[2,1024,1408]{2,1,0:T(8,128)(2,1)} %get-tuple-element.45, bf16[1024,2048]{1,0:T(8,128)(2,1)} %get-tuple-element.44), kind=kOutput, calls=%fused_computation.2 | convolution fusion | flops 11816927232 | bytes 21495808 | tf_op jit(solution)/shard_map/td,wtf->dwf/dot_general | solution.py:940
  385.1 0.0 reduce-scatter.9.cloned.1.call-update
  385.1 0.3 all-reduce.3.cloned.1.call-start
  385.4 0.0 reduce-scatter.7.cloned.1.call-done
  385.4 0.0 reduce-scatter.11.cloned.1.call-done
  385.5 0.0 reduce-scatter.5.cloned.1.call-done
  385.5 19.0 %reduce-scatter.9.cloned.1.call-done = bf16[1024,2,1408]{2,0,1:T(8,128)(2,1)} async-done(((bf16[2048,2,1408]{2,0,1:T(8,128)(2,1)}), bf16[1024,2,1408]{2,0,1:T(8,128)(2,1)}) %reduce-scatter.9.cloned.1.call-update) | async-done | bytes 5767184 | tf_op jit(solution)/shard_map/reduce_scatter | solution.py:955
  404.5 0.0 all-reduce.3.cloned.1.call-update
  404.5 0.6 maximum_convert_fusion.1.gain
  405.1 0.1 copy-done.19
  405.2 0.6 pad_maximum_fusion.1.vectors
  405.8 0.6 copy-done.12
  406.4 5.0 pad_maximum_fusion.w_in
  411.4 226.1 %tail.1 = (f32[1024,2048]{1,0:T(8,128)}, bf16[1024,2048]{1,0:T(8,128)(2,1)}, f32[1,5120]{1,0:T(1,128)}) custom-call(bf16[3,1024,512]{2,1,0:T(8,128)(2,1)} %bitcast.52, f32[1,2048]{1,0:T(1,128)} %maximum_convert_fusion.1.gain, f32[1,3072]{1,0:T(1,128)} %pad_maximum_fusion.1.vectors, bf16[3,2048,512]{2,1,0:T(8,128)(2,1)} %pad_maximum_fusion.w_in, ...), custom_call_target="tpu_custom_call" | custom-call | flops 6442450944 | bytes 734003200 | tf_op jit(solution)/shard_map/tail/pallas_call | solution.py:849
  637.5 1.3 constant_dynamic-slice_fusion
  638.8 1.3 fusion.20
  640.1 16.0 %all-reduce.3.cloned.1.call-done = (bf16[3,1024,512]{1,2,0:T(8,128)(2,1)}, bf16[1024,2,1408]{2,0,1:T(8,128)(2,1)}, bf16[512,1024]{1,0:T(8,128)(2,1)}, bf16[1408,1024]{1,0:T(8,128)(2,1)}) async-done(((bf16[3,1024,512]{1,2,0:T(8,128)(2,1)}, bf16[1024,2,1408]{2,0,1:T(8,128)(2,1)}, bf16[512,1024]{1,0:T(8,128)(2,1)}, bf16[1408,1024]{1,0:T(8,128)(2,1)}), (bf16[3,1024,512]{1,2,0:T(8,128)(2,1)}, ...) | async-done | bytes 12845072 | tf_op jit(solution)/shard_map/psum | solution.py:954
  656.0 5.5 copy.35
  661.5 1.6 convert_element_type.99
  663.1 13.4 %copy.36 = f32[1024,2,1408]{2,1,0:T(2,128)} copy(bf16[1024,2,1408]{2,0,1:T(8,128)(2,1)} %get-tuple-element.69) | data formatting | bytes 17301504
  676.4 3.3 convert_element_type.103
  679.7 0.2 copy-done.14
  679.9 2.0 copy.51
  682.0 3.4 copy.52
  (50 shorter events, 0.2 us)
Async XLA Ops:
  7.2 5.4 copy-start.20
  7.2 5.5 copy-start.21
  7.2 6.0 copy-start.18
  7.2 378.2 %reduce-scatter.7.cloned.1.call-start = ((), (), s32[]{:S(2)}) async-start(), calls=%async_computation.5 | async-start | bytes 3145728 | tf_op jit(solution)/shard_map/reduce_scatter | solution.py:955
  12.1 8.8 %copy-start.16 = (f32[512,1024]{1,0:T(8,128)S(1)}, f32[512,1024]{1,0:T(8,128)}, u32[]{:S(2)}) copy-start(f32[512,1024]{1,0:T(8,128)} %param.14) | copy-start | bytes 6291460
  12.1 23.5 %collective-permute-start = (bf16[3,1024,512]{2,1,0:T(8,128)(2,1)}, bf16[3,1024,512]{2,1,0:T(8,128)(2,1)}, u32[]{:S(2)}, u32[]{:S(2)}) collective-permute-start(bf16[3,1024,512]{2,1,0:T(8,128)(2,1)} %convert_element_type.78), channel_id=1, source_target_pairs={{0,16},{16,0},{1,17},{17,1},{2,18},{18,2},{3,19},{19,3},{4,20},{20... | collective-permute-start | bytes 9437192 | tf_op jit(solution)/shard_map/ppermute | solution.py:891
  12.6 22.4 %collective-permute-start.3 = (bf16[1,1024]{1,0:T(2,128)(2,1)S(1)}, bf16[1,1024]{1,0:T(2,128)(2,1)S(1)}, u32[]{:S(2)}, u32[]{:S(2)}) collective-permute-start(bf16[1,1024]{1,0:T(2,128)(2,1)S(1)} %broadcast_in_dim.25), channel_id=1, source_target_pairs={{0,16},{16,0},{1,17},{17,1},{2,18},{18,2},{3,19},{19,3},{4,20},{20... | collective-permute-start | bytes 6152 | tf_op jit(solution)/shard_map/ppermute | solution.py:891
  12.7 22.2 %collective-permute-start.1 = (bf16[1,1024]{1,0:T(2,128)(2,1)S(1)}, bf16[1,1024]{1,0:T(2,128)(2,1)S(1)}, u32[]{:S(2)}, u32[]{:S(2)}) collective-permute-start(bf16[1,1024]{1,0:T(2,128)(2,1)S(1)} %broadcast_in_dim.20), channel_id=1, source_target_pairs={{0,16},{16,0},{1,17},{17,1},{2,18},{18,2},{3,19},{19,3},{4,20},{20... | collective-permute-start | bytes 6152 | tf_op jit(solution)/shard_map/ppermute | solution.py:891
  13.3 21.3 %collective-permute-start.2 = (f32[4,1]{1,0:T(4,128)S(1)}, f32[4,1]{1,0:T(4,128)S(1)}, u32[]{:S(2)}, u32[]{:S(2)}) collective-permute-start(f32[4,1]{1,0:T(4,128)S(1)} %slice_convert_fusion), channel_id=1, source_target_pairs={{0,4},{4,8},{8,12},{1,5},{5,9},{9,13},{2,6},{6,10},{10,14},{3,7},{... | collective-permute-start | bytes 56 | tf_op jit(solution)/shard_map/ppermute | solution.py:899
  35.6 7.1 %copy-start.9 = (bf16[4,256,2048]{2,1,0:T(8,128)(2,1)S(1)}, bf16[4,256,2048]{2,1,0:T(8,128)(2,1)}, u32[]{:S(2)}) copy-start(bf16[4,256,2048]{2,1,0:T(8,128)(2,1)} %param.11) | copy-start | bytes 12582916
  40.1 1.7 copy-start.11
  40.1 2.7 copy-start.13
  51.9 6.6 copy-start.6
  51.9 6.6 copy-start.7
  58.5 2.8 copy-start
  76.7 1.3 copy-start.3
  78.0 1.0 copy-start.8
  321.0 64.4 %reduce-scatter.11.cloned.1.call-start = ((), (), s32[]{:S(2)}) async-start(), calls=%async_computation.7 | async-start | bytes 8650752 | tf_op jit(solution)/shard_map/reduce_scatter | solution.py:955
  331.5 1.6 copy-start.4
  331.5 53.9 %reduce-scatter.5.cloned.1.call-start = ((), (), s32[]{:S(2)}) async-start(), calls=%async_computation.4 | async-start | bytes 9437184 | tf_op jit(solution)/shard_map/reduce_scatter | solution.py:955
  333.1 2.8 copy-start.1
  335.9 1.6 copy-start.5
  337.5 20.3 %copy-start.10 = (bf16[4,256,2048]{2,1,0:T(8,128)(2,1)S(1)}, bf16[4,256,2048]{2,1,0:T(8,128)(2,1)}, u32[]{:S(2)}) copy-start(bf16[4,256,2048]{2,1,0:T(8,128)(2,1)} %param.11) | copy-start | bytes 12582916
  356.1 1.7 copy-start.2
  366.7 37.8 %reduce-scatter.9.cloned.1.call-start = ((), (), s32[]{:S(2)}) async-start(), calls=%async_computation.6 | async-start | bytes 17301504 | tf_op jit(solution)/shard_map/reduce_scatter | solution.py:955
  385.1 270.9 %all-reduce.3.cloned.1.call-start = ((), (), s32[]{:S(2)}) async-start(), calls=%async_computation.8 | async-start | bytes 25690112 | tf_op jit(solution)/shard_map/psum | solution.py:954
  404.5 0.7 copy-start.19
  404.5 1.9 copy-start.12
  656.0 5.5 copy-start.17
  661.5 20.5 %slice-start = ((s8[8388608]{0:T(1024)(128)(4,1)}), s8[4194304]{0:T(1024)(128)(4,1)S(1)}, s32[]{:S(2)}) async-start(s8[8388608]{0:T(1024)(128)(4,1)} %bitcast.63), calls=%async_computation.9 | async-start | bytes 8388608
  663.0 13.4 %copy-start.15 = (bf16[1408,1024]{1,0:T(8,128)(2,1)S(1)}, bf16[1408,1024]{1,0:T(8,128)(2,1)}, u32[]{:S(2)}) copy-start(bf16[1408,1024]{1,0:T(8,128)(2,1)} %get-tuple-element.71) | copy-start | bytes 8650756
  663.0 18.9 %slice-start.1 = ((s8[8388608]{0:T(1024)(128)(4,1)}), s8[4194304]{0:T(1024)(128)(4,1)S(1)}, s32[]{:S(2)}) async-start(s8[8388608]{0:T(1024)(128)(4,1)} %bitcast.63), calls=%async_computation.10 | async-start | bytes 8388608
  676.4 3.5 copy-start.14
Sparse Core Ops, SparseCore 0:
  321.1 8.3 reduce-scatter.6
  332.5 14.9 reduce-scatter.10
  366.9 13.3 reduce-scatter.4
  385.2 19.2 reduce-scatter.8
  408.8 247.1 all-reduce.2

commit v3 on v2

v3 whole, which is shorter than its diff:
```python
import functools

import jax
import jax.numpy as jnp
from jax import lax
from jax.experimental import pallas as pl
from jax.experimental.pallas import tpu as pltpu
from jax.sharding import PartitionSpec as P

EPS = 1e-06
FLOAT = jnp.float32
HALF = jnp.bfloat16
MESH = pl.DeviceIdType.MESH
GROUP = 8
BLOCK = 128
MIB = 1 << 20


def rms_scale(values):
    return lax.rsqrt(jnp.mean(values * values, -1, keepdims=True) + EPS)


def silu_slope(values):
    sig = jax.nn.sigmoid(values)
    return sig * (1.0 + values * (1.0 - sig))


def greet(peers):
    barrier = pltpu.get_barrier_semaphore()
    for peer in peers:
        pl.semaphore_signal(barrier, inc=1, device_id=peer, device_id_type=MESH)
    pl.semaphore_wait(barrier, len(peers))


def others(axis, count):
    mine = lax.axis_index(axis)
    return [{axis: lax.rem(mine + step, count)} for step in range(1, count)]


def share(slots, axis, count, send, recv):
    mine = lax.axis_index(axis)
    copies = [
        pltpu.make_async_remote_copy(
            src_ref=slots.at[mine],
            dst_ref=slots.at[mine],
            send_sem=send.at[step],
            recv_sem=recv.at[step],
            device_id=peer,
            device_id_type=MESH,
        )
        for step, peer in enumerate(others(axis, count))
    ]
    for copy in copies:
        copy.start()
    for copy in copies:
        copy.wait()


def lane_sums(values):
    part = values[:, :BLOCK]
    for start in range(BLOCK, values.shape[1], BLOCK):
        part = part + values[:, start : start + BLOCK]
    return jnp.sum(part.T, 0, keepdims=True)


def columns(row):
    return jnp.broadcast_to(row, (BLOCK, BLOCK)).T


def widen(values, chan):
    return jnp.concatenate([values] * (chan // BLOCK), -1)


def scan_forward(
    n_ctx, n_tp, width,
    proj, keep, gain, lower,
    gated, state, scale, carry_out,
    local, reach, ends, squares, ctx_send, ctx_recv, tp_send, tp_recv,
):
    n_seq, length, chan = state.shape
    greet(others("ctx", n_ctx) + others("tp", n_tp))
    low = lower[...].reshape(1, 1, chan)
    row = lax.broadcasted_iota(jnp.int32, (n_seq, GROUP, chan), 1)

    def step(index, carry):
        prod, total = carry
        rows = pl.ds(pl.multiple_of(index * GROUP, GROUP), GROUP)
        inp = proj[0, :, rows, :]
        decay = low + (1.0 - low) * jax.nn.sigmoid(proj[1, :, rows, :])
        add = inp * jax.nn.sigmoid(inp) * (1.0 - decay)
        mult = decay * keep[:, rows, :]
        for hop in (1, 2, 4):
            inside = row >= hop
            add = jnp.where(inside, mult * pltpu.roll(add, hop, 1) + add, add)
            mult = jnp.where(inside, mult * pltpu.roll(mult, hop, 1), mult)
        add = add + mult * total
        mult = mult * prod
        local[:, rows, :] = add
        reach[:, rows, :] = mult
        return mult[:, GROUP - 1 :, :], add[:, GROUP - 1 :, :]

    start = (jnp.ones((n_seq, 1, chan), FLOAT), jnp.zeros((n_seq, 1, chan), FLOAT))
    prod, total = lax.fori_loop(0, length // GROUP, step, start)
    here = lax.axis_index("ctx")
    ends[here, 0] = prod.reshape(n_seq, chan)
    ends[here, 1] = total.reshape(n_seq, chan)
    share(ends, "ctx", n_ctx, ctx_send, ctx_recv)
    carry = jnp.zeros((n_seq, chan), FLOAT)
    for place in range(n_ctx - 1):
        carry = jnp.where(place < here, ends[place, 1] + ends[place, 0] * carry, carry)
    carry_out[...] = carry
    mine = lax.axis_index("tp")
    for seq in range(n_seq):
        for start in range(0, length, BLOCK):
            rows = slice(start, start + BLOCK)
            value = local[seq, rows, :] + reach[seq, rows, :] * carry[seq : seq + 1]
            state[seq, rows, :] = value
            squares[mine, seq : seq + 1, rows] = lane_sums(value * value)
    share(squares, "tp", n_tp, tp_send, tp_recv)
    total = squares[0]
    for place in range(1, n_tp):
        total = total + squares[place]
    rate = lax.rsqrt(total / width + EPS)
    scale[...] = rate
    for seq in range(n_seq):
        for start in range(0, length, BLOCK):
            rows = slice(start, start + BLOCK)
            gate = proj[2, seq, rows, :]
            unit = state[seq, rows, :] * widen(columns(rate[seq : seq + 1, rows]), chan)
            gated[seq, rows, :] = (unit * gain[...] * (gate * jax.nn.sigmoid(gate))).astype(HALF)


def run_scan_forward(proj, keep, gain, lower, n_ctx, n_tp, width):
    _, n_seq, length, chan = proj.shape
    vmem = pl.BlockSpec(memory_space=pltpu.VMEM)
    return pl.pallas_call(
        functools.partial(scan_forward, n_ctx, n_tp, width),
        name="scan_forward",
        out_shape=(
            jax.ShapeDtypeStruct((n_seq, length, chan), HALF),
            jax.ShapeDtypeStruct((n_seq, length, chan), FLOAT),
            jax.ShapeDtypeStruct((n_seq, length), FLOAT),
            jax.ShapeDtypeStruct((n_seq, chan), FLOAT),
        ),
        in_specs=[vmem] * 4,
        out_specs=[vmem] * 4,
        scratch_shapes=[
            pltpu.VMEM((n_seq, length, chan), FLOAT),
            pltpu.VMEM((n_seq, length, chan), FLOAT),
            pltpu.VMEM((n_ctx, 2, n_seq, chan), FLOAT),
            pltpu.VMEM((n_tp, n_seq, length), FLOAT),
            pltpu.SemaphoreType.DMA((n_ctx,)),
            pltpu.SemaphoreType.DMA((n_ctx,)),
            pltpu.SemaphoreType.DMA((n_tp,)),
            pltpu.SemaphoreType.DMA((n_tp,)),
        ],
        compiler_params=pltpu.CompilerParams(
            collective_id=0, has_side_effects=True, vmem_limit_bytes=40 * MIB
        ),
    )(proj, keep, gain, lower)


PIECES = 4
TILE = 256
WIDE = 512


def bands(count, size):
    return [(start, min(size, count - start)) for start in range(0, count, size)]


def dot(lhs, rhs):
    return jnp.dot(lhs, rhs, preferred_element_type=FLOAT)


def dot_nt(lhs, rhs):
    return lax.dot_general(lhs, rhs, (((1,), (1,)), ((), ())), preferred_element_type=FLOAT)


class Line:
    def __init__(self, held, cross, total, sems):
        self.held, self.cross, self.total, self.sems = held, cross, total, sems
        place = lax.axis_index("tp")
        self.inner = (place == 1) | (place == 2)
        self.side = place + 1 - 2 * lax.rem(place, 2)
        self.facing = 3 - place

    def slot(self, job, ref):
        slots = ref.shape[0]
        if slots == self.total.shape[0]:
            return job
        return job % slots if isinstance(job, int) else lax.rem(job, slots)

    def copy(self, source, target, send, recv, place):
        return pltpu.make_async_remote_copy(
            src_ref=source,
            dst_ref=target,
            send_sem=send,
            recv_sem=recv,
            device_id={"tp": place},
            device_id_type=MESH,
        )

    def inward(self, job, q):
        send, recv, _, _ = self.sems
        return self.copy(
            self.held.at[self.slot(job, self.held), q], self.total.at[job, q],
            send.at[job, q], recv.at[job, q], self.side,
        )

    def outward(self, job, q):
        send, recv, _, _ = self.sems
        return self.copy(
            self.total.at[job, q], self.total.at[job, q],
            send.at[job, q], recv.at[job, q], self.side,
        )

    def across(self, job, q):
        _, _, send, recv = self.sems
        return self.copy(
            self.held.at[self.slot(job, self.held), q], self.cross.at[self.slot(job, self.cross), q],
            send.at[job, q], recv.at[job, q], self.facing,
        )

    def offer(self, job, q):
        @pl.when(jnp.logical_not(self.inner))
        def _():
            self.inward(job, q).start()

    def tick(self, job, step):
        slot, cross_slot = self.slot(job, self.held), self.slot(job, self.cross)

        @pl.when(self.inner)
        def _():
            if step < PIECES:
                self.inward(job, step).wait_recv()
                value = self.held[slot, step].astype(FLOAT) + self.total[job, step].astype(FLOAT)
                self.held[slot, step] = value.astype(HALF)
                self.across(job, step).start()
            if step > 0:
                q = step - 1
                self.across(job, q).wait_recv()
                value = self.held[slot, q].astype(FLOAT) + self.cross[cross_slot, q].astype(FLOAT)
                self.total[job, q] = value.astype(HALF)
                self.outward(job, q).start()

    def relay(self, job):
        for step in range(PIECES + 1):
            self.tick(job, step)

    def arrive(self, job):
        @pl.when(jnp.logical_not(self.inner))
        def _():
            @pl.loop(0, PIECES)
            def _(q):
                self.outward(job, q).wait_recv()

    def release(self, job):
        @pl.when(self.inner)
        def _():
            @pl.loop(0, PIECES)
            def _(q):
                self.across(job, q).wait_send()

        @pl.when(jnp.logical_not(self.inner))
        def _():
            @pl.loop(0, PIECES)
            def _(q):
                self.inward(job, q).wait_send()

    def settle(self, job):
        @pl.when(self.inner)
        def _():
            @pl.loop(0, PIECES)
            def _(q):
                self.outward(job, q).wait_send()


def pull(parts, wholes, dims, n_fsdp, own_sem, send_sem, recv_sem):
    if n_fsdp != 2:
        copies = [
            pltpu.make_async_copy(part, whole, own_sem.at[index])
            for index, (part, whole) in enumerate(zip(parts, wholes))
        ]
        for copy in copies:
            copy.start()
        return lambda index: copies[index].wait()
    mine = lax.axis_index("fsdp")
    near, far = [], []
    for index, (part, whole, dim) in enumerate(zip(parts, wholes, dims)):
        size = part.shape[dim]
        at = pl.ds(pl.multiple_of(mine * size, size), size)
        place = whole.at[at] if dim == 0 else whole.at[:, at]
        near.append(pltpu.make_async_copy(part, place, own_sem.at[index]))
        far.append(
            pltpu.make_async_remote_copy(
                src_ref=part,
                dst_ref=place,
                send_sem=send_sem.at[index],
                recv_sem=recv_sem.at[index],
                device_id={"fsdp": 1 - mine},
                device_id_type=MESH,
            )
        )
    for one, two in zip(near, far):
        two.start()
        one.start()

    def wait(index):
        near[index].wait()
        far[index].wait()

    return wait


def span(start, size, unit):
    return pl.ds(pl.multiple_of(start, unit), size)


def row_blocks(count, size, body):
    @pl.loop(0, count // size)
    def _(index):
        body(pl.ds(pl.multiple_of(index * size, size), size))


def line_peers():
    place = lax.axis_index("tp")
    return [{"tp": place + 1 - 2 * lax.rem(place, 2)}, {"tp": 3 - place}]


def joined(ref, c, rows):
    return jnp.concatenate([ref[c, q, rows, :].astype(FLOAT) for q in range(PIECES)], -1)


def halves(n_fsdp, store_sem, send_sem, recv_sem, spare, inbox):
    mine = lax.axis_index("fsdp")
    pending = {}

    def send(index, view):
        slot = index % 2
        return pltpu.make_async_remote_copy(
            src_ref=view(spare.at[slot]),
            dst_ref=view(inbox.at[slot]),
            send_sem=send_sem.at[slot],
            recv_sem=recv_sem.at[slot],
            device_id={"fsdp": 1 - mine},
            device_id_type=MESH,
        )

    def item(index, view, compute_other, compute_own, other_place, target):
        slot = index % 2
        if index - 2 in pending:
            pending.pop(index - 2)()
        compute_other(view(spare.at[slot]))
        if n_fsdp == 2:
            copy = send(index, view)
            copy.start()
            pending[index] = lambda: send(index, view).wait_send()
        else:
            def store():
                return pltpu.make_async_copy(view(spare.at[slot]), other_place(), store_sem.at[slot])

            store().start()
            pending[index] = lambda: store().wait()
        compute_own(target)
        if n_fsdp == 2:
            send(index, view).wait_recv()
            extra = view(inbox.at[slot])

            def add(rows):
                value = target[rows, :].astype(FLOAT) + extra[rows, :].astype(FLOAT)
                target[rows, :] = value.astype(HALF)

            row_blocks(target.shape[0], 16, add)

    def finish():
        for wait in pending.values():
            wait()

    return item, finish


class Square:
    def __init__(self, index, buffers, at, place, send, recv, store_sem):
        self.buffers, self.at, self.place_of = buffers, at, place
        self.send, self.recv, self.index, self.store_sem = send, recv, index, store_sem

    @property
    def tile(self):
        return self.buffers[0].at[self.at]

    @property
    def half(self):
        return self.buffers[1].at[self.at]

    @property
    def quarter(self):
        return self.buffers[2].at[self.at]

    def geometry(self):
        here = lax.axis_index("ctx")
        low, high = lax.rem(here, 2), here // 2
        near, far = here + 1 - 2 * low, here + 2 - 4 * high
        bits = (low, high) if self.index % 2 == 0 else (high, low)
        peers = (near, far) if self.index % 2 == 0 else (far, near)
        wide, thin = self.half.shape[1], self.quarter.shape[1]
        begin = bits[0] * wide
        return (
            peers,
            span(begin, wide, BLOCK),
            span((1 - bits[0]) * wide, wide, BLOCK),
            span(begin + bits[1] * thin, thin, BLOCK),
            span(begin + (1 - bits[1]) * thin, thin, BLOCK),
        )

    def round(self, number):
        peers, mine, yours, my_part, your_part = self.geometry()
        source, target, peer = (
            (self.tile.at[:, yours], self.half, 0),
            (self.tile.at[:, your_part], self.quarter, 1),
            (self.tile.at[:, my_part], self.place_of().at[:, my_part], 1),
            (self.place_of().at[:, mine], self.place_of().at[:, mine], 0),
        )[number]
        return pltpu.make_async_remote_copy(
            src_ref=source,
            dst_ref=target,
            send_sem=self.send.at[self.index, number],
            recv_sem=self.recv.at[self.index, number],
            device_id={"ctx": peers[peer]},
            device_id_type=MESH,
        )

    def add(self, cols, extra):
        def body(rows):
            value = self.tile[rows, cols].astype(FLOAT) + extra[rows, :].astype(FLOAT)
            self.tile[rows, cols] = value.astype(HALF)

        row_blocks(self.tile.shape[0], 16, body)

    def store(self):
        return pltpu.make_async_copy(self.tile, self.place_of(), self.store_sem.at[self.index])

    def store_part(self):
        part = self.geometry()[3]
        return pltpu.make_async_copy(
            self.tile.at[:, part], self.place_of().at[:, part], self.store_sem.at[self.index]
        )

    def advance(self, number):
        if number > 0:
            self.round(number - 1).wait_recv()
        if number == 1:
            self.add(self.geometry()[1], self.half)
        if number == 2:
            self.add(self.geometry()[3], self.quarter)
            self.store_part().start()
        if number == 3:
            self.store_part().wait()
        if number < 4:
            self.round(number).start()

    def settle(self):
        for number in range(4):
            self.round(number).wait_send()


def fill(target, left, right, first):
    for start, size in bands(target.shape[1], WIDE):
        cols = pl.ds(pl.multiple_of(first + start, BLOCK), size)
        target[:, start : start + size] = dot(left, right[:, cols]).astype(HALF)


def middle(
    n_fsdp, CHUNK,
    gated, tokens, cotangent, gain, wo_part, wg_part, wu_part, wd_part,
    mixed_out, normed_out, act_out, grad_glu_out, grad_resid_out, grad_mixed_out,
    grad_gated_out, w_glu_out, w_down_out, grad_gain_out,
    wo, wg, wu, wd, x_all, dy_all, held, crossed, total, normed, act, grad_glu,
    grad_resid, grad_mixed, grad_gated, gain_total, spare, own, inbox,
    weight_sem, weight_send, weight_recv, again_sem, own_sem, send_sem, recv_sem, load_sem, store_sem, *line_sems,
):
    n_chunks, _, _, piece = held.shape
    units = wd.shape[0]
    width = wd.shape[1]
    peers = line_peers()
    if n_fsdp == 2:
        peers.append({"fsdp": 1 - lax.axis_index("fsdp")})
    greet(peers)
    ready = pull(
        (wo_part, wg_part, wu_part, wd_part), (wo, wg, wu, wd), (1, 0, 0, 1),
        n_fsdp, own_sem, send_sem, recv_sem,
    )
    loads = [
        pltpu.make_async_copy(tokens, x_all, load_sem.at[0]),
        pltpu.make_async_copy(cotangent, dy_all, load_sem.at[1]),
    ]
    for load in loads:
        load.start()
    line = Line(held, crossed, total, line_sems)

    def chunk_rows(c):
        return pl.ds(pl.multiple_of(c * CHUNK, CHUNK), CHUNK)

    def stores(c, wanted=None):
        rows = chunk_rows(c)
        pairs = [
            (normed, normed_out.at[rows]),
            (act, act_out.at[rows]),
            (grad_glu.at[0], grad_glu_out.at[0, rows]),
            (grad_glu.at[1], grad_glu_out.at[1, rows]),
            (grad_resid, grad_resid_out.at[rows]),
            (grad_mixed, grad_mixed_out.at[rows]),
            (grad_gated, grad_gated_out.at[rows]),
        ]
        pairs += [
            (total.at[c, q], mixed_out.at[rows, pl.ds(q * piece, piece)]) for q in range(PIECES)
        ]
        return [
            pltpu.make_async_copy(source, target, store_sem.at[index])
            for index, (source, target) in enumerate(pairs)
            if wanted is None or index in wanted
        ]

    FORWARD = (0, 1, 2, 3, 7, 8, 9, 10)
    BACKWARD = (4, 5, 6)

    ready(0)

    @pl.loop(0, n_chunks)
    def _(c):
        lhs = gated[chunk_rows(c), :]

        @pl.loop(0, PIECES)
        def _(q):
            cols = pl.ds(pl.multiple_of(q * piece, piece), piece)
            held[c, q] = dot(lhs, wo[:, cols]).astype(HALF)
            line.offer(c, q)

    for load in loads:
        load.wait()
    line.relay(0)
    for index in (1, 2, 3):
        ready(index)
    w_down_store = pltpu.make_async_copy(wd, w_down_out, again_sem.at[3])
    w_down_store.start()

    @pl.loop(0, n_chunks)
    def _(c):
        line.arrive(c)
        line.tick(c + 1, 0)

        @pl.when(c > 0)
        def _():
            for store in stores(c - 1, FORWARD):
                store.wait()

        def norm(rows):
            at = pl.ds(pl.multiple_of(c * CHUNK + rows.start, 16), rows.size)
            resid = x_all[at, :].astype(FLOAT) + joined(total, c, rows)
            normed[rows, :] = (resid * rms_scale(resid) * gain[...]).astype(HALF)

        row_blocks(CHUNK, 16, norm)

        def unit(cols):
            glu_gate = dot(normed[...], wg[:, cols])
            glu_up = dot(normed[...], wu[:, cols])
            grad_act = dot_nt(dy_all[chunk_rows(c), :], wd[cols, :])
            sig = jax.nn.sigmoid(glu_gate)
            silu = glu_gate * sig
            act[:, cols] = (silu * glu_up).astype(HALF)
            slope = sig * (1.0 + glu_gate * (1.0 - sig))
            grad_glu[0, :, cols] = (grad_act * glu_up * slope).astype(HALF)
            grad_glu[1, :, cols] = (grad_act * silu).astype(HALF)

        for index, (start, size) in enumerate(bands(units, WIDE)):
            unit(slice(start, start + size))
            if index == 0:
                line.tick(c + 1, 1)
        line.tick(c + 1, 2)
        line.release(c)

        @pl.loop(0, PIECES)
        def _(q):
            @pl.when(q == PIECES // 2)
            def _():
                line.tick(c + 1, 3)

            at = pl.ds(pl.multiple_of(q * piece, piece), piece)
            value = dot_nt(grad_glu[0], wg[at, :]) + dot_nt(grad_glu[1], wu[at, :])
            held[c, q] = value.astype(HALF)
            line.offer(n_chunks + c, q)

        line.tick(c + 1, 4)

        for store in stores(c, FORWARD):
            store.start()

    for store in stores(n_chunks - 1, FORWARD):
        store.wait()
    rows = n_chunks * CHUNK
    w_down_store.wait()
    kept = [
        (grad_glu_out.at[0], wg.at[:rows]),
        (grad_glu_out.at[1], wu.at[:rows]),
        (normed_out, wd.at[:rows]),
    ]
    again = [
        pltpu.make_async_copy(source, target, again_sem.at[index])
        for index, (source, target) in enumerate(kept)
    ]
    for copy in again:
        copy.start()
    gain_total[...] = jnp.zeros_like(gain_total)
    item, finish = halves(n_fsdp, weight_sem, weight_send, weight_recv, spare, inbox)
    mine = lax.axis_index("fsdp") if n_fsdp == 2 else 1
    depth = width // 2
    whole = n_fsdp != 2
    per_part = depth // TILE
    own_stores = {}

    def weight_item(index):
        if index >= 2 * per_part:
            return
        part, k = divmod(index, per_part)
        right = (wg, wu)[part].at[:rows]
        slot = index % 2
        if index > 1:
            own_stores.pop(slot).wait()

        def compute(side):
            at = pl.ds(pl.multiple_of(side * depth + k * TILE, TILE), TILE)
            return lambda target: fill(target, wd[:rows, at].T, right, 0)

        at = slice(k * TILE + whole * depth, (k + 1) * TILE + whole * depth)
        item(
            index, lambda ref: ref, compute(1 - mine), compute(mine),
            lambda: w_glu_out.at[part, k * TILE : (k + 1) * TILE], own.at[slot],
        )
        store = pltpu.make_async_copy(own.at[slot], w_glu_out.at[part, at], weight_sem.at[2 + slot])
        store.start()
        own_stores[slot] = store

    def backward(c):
        line.arrive(n_chunks + c)
        if c > 0:
            for store in stores(c - 1, BACKWARD):
                store.wait()

        def norm_back(rows):
            at = pl.ds(pl.multiple_of(c * CHUNK + rows.start, 16), rows.size)
            resid = x_all[at, :].astype(FLOAT) + joined(total, c, rows)
            rate = rms_scale(resid)
            grad = joined(total, n_chunks + c, rows)
            by_gain = grad * (resid * rate)
            gain_total[...] += by_gain[:8] + by_gain[8:]
            inner = gain[...] * grad
            mean = jnp.mean(inner * resid, -1, keepdims=True)
            value = dy_all[at, :].astype(FLOAT) + rate * inner - resid * (rate * rate * rate * mean)
            grad_resid[rows, :] = value
            grad_mixed[rows, :] = value.astype(HALF)

        row_blocks(CHUNK, 16, norm_back)
        for start, size in bands(grad_gated.shape[1], WIDE):
            grad_gated[:, start : start + size] = dot_nt(
                grad_mixed[...], wo[start : start + size, :]
            )
        for store in stores(c, BACKWARD):
            store.start()

    for copy in again:
        copy.wait()
    count = 0
    for c in range(n_chunks):
        if c == n_chunks - 1:
            while count < 2 * per_part:
                weight_item(count)
                count += 1
        backward(c)
        if c + 1 < n_chunks:
            for step in range(PIECES + 1):
                if step % 2 == 0:
                    weight_item(count)
                    count += 1
                line.tick(n_chunks + c + 1, step)
    finish()
    for store in own_stores.values():
        store.wait()

    grad_gain_out[...] = jnp.sum(gain_total[...], 0, keepdims=True)
    for store in stores(n_chunks - 1, BACKWARD):
        store.wait()

    @pl.loop(0, n_chunks)
    def _(c):
        line.settle(c)
        line.settle(n_chunks + c)
        line.release(n_chunks + c)


def run_middle(gated, tokens, cotangent, gain, parts, n_fsdp, length):
    rows, chan = gated.shape
    width = tokens.shape[1]
    wg = parts[1]
    units = wg.shape[1]
    n_chunks = rows // length
    piece = width // PIECES
    vmem = pl.BlockSpec(memory_space=pltpu.VMEM)
    hbm = pl.BlockSpec(memory_space=pl.ANY)
    sems = pltpu.SemaphoreType.DMA((2 * n_chunks, PIECES))
    return pl.pallas_call(
        functools.partial(middle, n_fsdp, length),
        name="middle",
        out_shape=(
            jax.ShapeDtypeStruct((rows, width), HALF),
            jax.ShapeDtypeStruct((rows, width), HALF),
            jax.ShapeDtypeStruct((rows, units), HALF),
            jax.ShapeDtypeStruct((2, rows, units), HALF),
            jax.ShapeDtypeStruct((rows, width), FLOAT),
            jax.ShapeDtypeStruct((rows, width), HALF),
            jax.ShapeDtypeStruct((rows, chan), FLOAT),
            jax.ShapeDtypeStruct((2, width if n_fsdp != 2 else width // 2, units), HALF),
            jax.ShapeDtypeStruct((units, width), HALF),
            jax.ShapeDtypeStruct((1, width), FLOAT),
        ),
        in_specs=[vmem, hbm, hbm, vmem, hbm, hbm, hbm, hbm],
        out_specs=[hbm] * 9 + [vmem],
        scratch_shapes=[
            pltpu.VMEM((chan, width), HALF),
            pltpu.VMEM((width, units), HALF),
            pltpu.VMEM((width, units), HALF),
            pltpu.VMEM((units, width), HALF),
            pltpu.VMEM((rows, width), HALF),
            pltpu.VMEM((rows, width), HALF),
            pltpu.VMEM((n_chunks, PIECES, length, piece), HALF),
            pltpu.VMEM((n_chunks, PIECES, length, piece), HALF),
            pltpu.VMEM((2 * n_chunks, PIECES, length, piece), HALF),
            pltpu.VMEM((length, width), HALF),
            pltpu.VMEM((length, units), HALF),
            pltpu.VMEM((2, length, units), HALF),
            pltpu.VMEM((length, width), FLOAT),
            pltpu.VMEM((length, width), HALF),
            pltpu.VMEM((length, chan), FLOAT),
            pltpu.VMEM((8, width), FLOAT),
            pltpu.VMEM((2, TILE, units), HALF),
            pltpu.VMEM((2, TILE, units), HALF),
            pltpu.VMEM((2, TILE, units), HALF),
            pltpu.SemaphoreType.DMA((4,)),
            pltpu.SemaphoreType.DMA((2,)),
            pltpu.SemaphoreType.DMA((2,)),
            pltpu.SemaphoreType.DMA((4,)),
            pltpu.SemaphoreType.DMA((4,)),
            pltpu.SemaphoreType.DMA((4,)),
            pltpu.SemaphoreType.DMA((4,)),
            pltpu.SemaphoreType.DMA((2,)),
            pltpu.SemaphoreType.DMA((12,)),
        ]
        + [sems] * 4,
        compiler_params=pltpu.CompilerParams(
            collective_id=2, has_side_effects=True, vmem_limit_bytes=63 * MIB
        ),
        cost_estimate=pl.CostEstimate(
            flops=16 * rows * width * units, bytes_accessed=400 * MIB, transcendentals=0
        ),
    )(gated, tokens, cotangent, gain, *parts)


def scan_back(
    n_ctx, n_tp, width, pump,
    proj, keep, gain, lower, state, scale, carry_in, near,
    grad_proj, gain_out, lower_out,
    reach, rate_wide, cross_wide, ends, cross, ctx_sems, tp_sems,
):
    n_seq, length, chan = state.shape
    low = lower[...].reshape(1, 1, chan)
    mine = lax.axis_index("tp")
    gain_total = jnp.zeros((8, chan), FLOAT)
    for seq in range(n_seq):
        for start in range(0, length, BLOCK):
            rows = slice(start, start + BLOCK)
            rate = columns(scale[seq : seq + 1, rows])
            rate_wide[seq, rows, :] = rate
            gate = proj[2, seq, rows, :]
            sig = jax.nn.sigmoid(gate)
            swish = gate * sig
            value = state[seq, rows, :]
            into = near[seq, rows, :]
            by_unit = into * value * widen(rate, chan)
            slope = sig * (1.0 + gate * (1.0 - sig))
            grad_proj[seq, rows, 2 * chan :] = (by_unit * gain[...] * slope).astype(HALF)
            gain_total = gain_total + jnp.sum((by_unit * swish).reshape(-1, 8, chan), 0)
            grad_unit = into * swish * gain[...]
            near[seq, rows, :] = grad_unit
            cross[mine, seq : seq + 1, rows] = lane_sums(grad_unit * value)
    gain_out[...] = jnp.sum(gain_total, 0, keepdims=True)
    share(cross, "tp", n_tp, *tp_sems)
    pump()
    total = cross[0]
    for place in range(1, n_tp):
        total = total + cross[place]
    rate = scale[...]
    total = total * (rate * rate * rate) / width
    for seq in range(n_seq):
        for start in range(0, length, BLOCK):
            rows = slice(start, start + BLOCK)
            cross_wide[seq, rows, :] = columns(total[seq : seq + 1, rows])

    row = lax.broadcasted_iota(jnp.int32, (n_seq, GROUP, chan), 1)

    def back(index, carry):
        prod, above = carry
        rows = pl.ds(pl.multiple_of((length // GROUP - 1 - index) * GROUP, GROUP), GROUP)
        decay = low + (1.0 - low) * jax.nn.sigmoid(proj[1, :, rows, :])
        mult = decay * keep[:, rows, :]
        direct = (
            widen(rate_wide[:, rows, :], chan) * near[:, rows, :]
            - widen(cross_wide[:, rows, :], chan) * state[:, rows, :]
        )
        add = mult * direct
        for hop in (1, 2, 4):
            inside = row < GROUP - hop
            add = jnp.where(inside, mult * pltpu.roll(add, GROUP - hop, 1) + add, add)
            mult = jnp.where(inside, mult * pltpu.roll(mult, GROUP - hop, 1), mult)
        add = add + mult * above
        mult = mult * prod
        inside = row < GROUP - 1
        near[:, rows, :] = direct + jnp.where(inside, pltpu.roll(add, GROUP - 1, 1), above)
        reach[:, rows, :] = jnp.where(inside, pltpu.roll(mult, GROUP - 1, 1), prod)
        return mult[:, :1, :], add[:, :1, :]

    held = (jnp.ones((n_seq, 1, chan), FLOAT), jnp.zeros((n_seq, 1, chan), FLOAT))
    held = lax.fori_loop(0, length // GROUP, back, held)
    prod, total = held
    here = lax.axis_index("ctx")
    ends[here, 0] = prod.reshape(n_seq, chan)
    ends[here, 1] = total.reshape(n_seq, chan)
    pump()
    share(ends, "ctx", n_ctx, *ctx_sems)
    carry = jnp.zeros((n_seq, chan), FLOAT)
    for place in range(n_ctx - 1, 0, -1):
        carry = jnp.where(place > here, ends[place, 1] + ends[place, 0] * carry, carry)
    carry = carry.reshape(n_seq, 1, chan)
    wide = 2 * GROUP
    first = lax.broadcasted_iota(jnp.int32, (n_seq, wide, chan), 1) == 0

    def finish(index, held):
        before, low_total = held
        rows = pl.ds(pl.multiple_of(index * wide, wide), wide)
        inp = proj[0, :, rows, :]
        sig = jax.nn.sigmoid(inp)
        silu = inp * sig
        fsig = jax.nn.sigmoid(proj[1, :, rows, :])
        rest = 1.0 - fsig
        decay = low + (1.0 - low) * fsig
        grad_state = near[:, rows, :] + reach[:, rows, :] * carry
        value = state[:, rows, :]
        prev = jnp.where(first, before, pltpu.roll(value, 1, 1))
        grad_decay = grad_state * (prev * keep[:, rows, :] - silu)
        grad_proj[:, rows, :chan] = (
            grad_state * (1.0 - decay) * (sig * (1.0 + inp * (1.0 - sig)))
        ).astype(HALF)
        grad_proj[:, rows, chan : 2 * chan] = (
            grad_decay * (1.0 - low) * fsig * rest
        ).astype(HALF)
        return value[:, wide - 1 :, :], low_total + grad_decay * rest

    held = (carry_in[...].reshape(n_seq, 1, chan), jnp.zeros((n_seq, wide, chan), FLOAT))
    _, low_total = lax.fori_loop(0, length // wide, finish, held)
    lower_out[...] = jnp.sum(jnp.sum(low_total, 0), 0, keepdims=True)
    pump()


def tail(
    n_fsdp, n_ctx, n_tp,
    keep, gate_gain, lower, scale, carry_in, gain, gain_two_grad,
    proj, state, grad_gated, w_in, w_down, act, normed, grad_mixed, gated, cotangent,
    grad_resid, tokens, mixed,
    grad_tokens_out, output_out, vectors_out, w_in_out, w_out_out, w_down_out,
    grad_proj, held, crossed, total, spare, inbox,
    in_tile, in_half, in_quarter, out_tile, out_half, out_quarter, down_tile, down_half, down_quarter,
    gain_total, ends, cross, over_ctx, over_fsdp,
    load_sem, store_sem, end_send, end_recv, cross_send, cross_recv, ctx_send, ctx_recv,
    fsdp_send, fsdp_recv, part_sem, part_send, part_recv, square_send, square_recv, square_store,
    *line_sems,
):
    n_seq, length, wide = grad_proj.shape
    chan = wide // 3
    rows = n_seq * length
    width = gain.shape[1]
    units = w_down.shape[0]
    piece = width // PIECES
    n_chunks = n_seq
    whole = n_fsdp != 2
    greet(others("ctx", n_ctx) + others("tp", n_tp) + others("fsdp", n_fsdp))
    line = Line(held, crossed, total, line_sems)
    ticks = [(job, step) for job in range(2 * n_chunks) for step in range(PIECES + 1)]
    squares = []
    turn = [0]
    SPACE = 3

    def pump(count=1):
        for _ in range(count):
            if ticks:
                line.tick(*ticks.pop(0))
            for index, square in enumerate(squares):
                if square[1] < 5 and turn[0] >= square[2] + SPACE * square[1]:
                    square[0].advance(square[1])
                    square[1] += 1
            turn[0] += 1

    def start_loads(pairs, first=0):
        copies = [
            pltpu.make_async_copy(source, target, load_sem.at[first + index])
            for index, (source, target) in enumerate(pairs)
        ]
        for copy in copies:
            copy.start()
        return copies

    def chunk_rows(c):
        return pl.ds(c * length, length) if isinstance(c, int) else span(c * length, length, length)

    def down_terms(w_all, act_all):
        for copy in start_loads([(w_down, w_all), (act, act_all)]):
            copy.wait()

        for c in range(n_chunks):
            @pl.loop(0, PIECES)
            def _(q):
                cols = pl.ds(pl.multiple_of(q * piece, piece), piece)
                held[c, q] = dot(act_all[chunk_rows(c), :], w_all[:, cols]).astype(HALF)
                line.offer(c, q)

            if c == n_chunks - 1:
                pump()

    pl.run_scoped(
        down_terms, pltpu.VMEM((units, width), HALF), pltpu.VMEM((rows, units), HALF)
    )

    def back(proj_all, state_all, near, reach, rate_wide, cross_wide):
        for copy in start_loads([(proj, proj_all), (state, state_all), (grad_gated, near)]):
            copy.wait()
        gain_at = over_ctx.at[lax.axis_index("ctx"), :, 2 * width : 2 * width + chan]
        lower_at = over_ctx.at[lax.axis_index("ctx"), :, 2 * width + chan :]
        scan_back(
            n_ctx, n_tp, width, pump,
            proj_all, keep, gate_gain, lower, state_all, scale, carry_in, near,
            grad_proj, gain_at, lower_at,
            reach, rate_wide, cross_wide, ends, cross, (end_send, end_recv), (cross_send, cross_recv),
        )

    shape = (n_seq, length, chan)
    pl.run_scoped(
        back,
        pltpu.VMEM((3, *shape), FLOAT),
        pltpu.VMEM(shape, FLOAT),
        pltpu.VMEM(shape, FLOAT),
        pltpu.VMEM(shape, FLOAT),
        pltpu.VMEM((n_seq, length, BLOCK), FLOAT),
        pltpu.VMEM((n_seq, length, BLOCK), FLOAT),
    )

    def back_terms(w_all):
        for copy in start_loads(
            [(w_in.at[gate], w_all.at[:, gate * chan : (gate + 1) * chan]) for gate in range(3)]
        ):
            copy.wait()

        for c in range(n_chunks):
            @pl.loop(0, PIECES)
            def _(q):
                at = pl.ds(pl.multiple_of(q * piece, piece), piece)
                held[n_chunks + c, q] = dot_nt(grad_proj[c], w_all[at, :]).astype(HALF)
                line.offer(n_chunks + c, q)

            if c % 2 == 1:
                pump()

    pl.run_scoped(back_terms, pltpu.VMEM((width, wide), HALF))

    item, finish = halves(n_fsdp, part_sem, part_send, part_recv, spare, inbox)
    mine = 1 if whole else lax.axis_index("fsdp")
    depth = width // 2
    skip = whole * depth
    stores = []

    def weights(act_all, dy_all, normed_all, mixed_all, gated_all):
        copies = start_loads(
            [(act, act_all), (cotangent, dy_all), (normed, normed_all), (grad_mixed, mixed_all),
             (gated, gated_all)]
        )
        count = [0]

        def tile(view, compute, other_place, own_place, buffers, at):
            index = count[0]
            count[0] += 1
            square = Square(
                index, buffers, at, own_place, square_send, square_recv, square_store
            )
            item(index, view, compute(1 - mine), compute(mine), other_place, square.tile)
            if whole:
                square.store().start()
                stores.append(square)
            else:
                squares.append([square, 0, turn[0]])
            pump()

        copies[0].wait()
        copies[1].wait()
        for start, size in bands(units, TILE):
            left = act_all[:, start : start + size].T
            at = slice(start, start + size)

            def compute(side):
                return lambda target: fill(target, left, dy_all, side * depth)

            tile(
                lambda ref, size=size: ref.at[:size, :depth], compute,
                lambda at=at: w_down_out.at[at, :depth], lambda at=at: w_down_out.at[at, skip:],
                (down_tile, down_half, down_quarter), at,
            )
        copies[2].wait()
        flat_proj = grad_proj.reshape(rows, wide)
        for k in range(depth // TILE):
            def compute(side):
                at = pl.ds(pl.multiple_of(side * depth + k * TILE, TILE), TILE)
                return lambda target: fill(target, normed_all[:, at].T, flat_proj, 0)

            at = slice(k * TILE, (k + 1) * TILE)
            tile(
                lambda ref: ref, compute,
                lambda at=at: w_in_out.at[at],
                lambda k=k: w_in_out.at[k * TILE + skip : (k + 1) * TILE + skip],
                (in_tile, in_half, in_quarter), k,
            )
        copies[3].wait()
        copies[4].wait()
        for k in range(chan // TILE):
            at = slice(k * TILE, (k + 1) * TILE)
            left = gated_all[:, at].T

            def compute(side):
                return lambda target: fill(target, left, mixed_all, side * depth)

            tile(
                lambda ref: ref.at[:, :depth], compute,
                lambda at=at: w_out_out.at[at, :depth], lambda at=at: w_out_out.at[at, skip:],
                (out_tile, out_half, out_quarter), k,
            )

    pl.run_scoped(
        weights,
        pltpu.VMEM((rows, units), HALF),
        pltpu.VMEM((rows, width), HALF),
        pltpu.VMEM((rows, width), HALF),
        pltpu.VMEM((rows, width), HALF),
        pltpu.VMEM((rows, chan), HALF),
    )
    finish()

    def ends_of(resid_all, x_all, mixed_all):
        for copy in start_loads([(tokens, x_all), (mixed, mixed_all), (grad_resid, resid_all)]):
            copy.wait()
        gain_total[...] = jnp.zeros_like(gain_total)

        def token_store(c):
            at = chunk_rows(c)
            return pltpu.make_async_copy(
                resid_all.at[at], grad_tokens_out.at[at], store_sem.at[0, c]
            )

        def output_store(c):
            at = chunk_rows(c)
            return pltpu.make_async_copy(mixed_all.at[at], output_out.at[at], store_sem.at[1, c])

        def until(job):
            while ticks and ticks[0][0] <= job:
                pump()

        for c in range(n_chunks):
            until(c)
            line.arrive(c)

            @pl.loop(0, length // 16)
            def _(index):
                at = pl.ds(pl.multiple_of(c * length + index * 16, 16), 16)
                rows = pl.ds(pl.multiple_of(index * 16, 16), 16)
                value = x_all[at, :].astype(FLOAT) + mixed_all[at, :].astype(FLOAT)
                mixed_all[at, :] = (value + joined(total, c, rows)).astype(HALF)

            output_store(c).start()

        for c in range(n_chunks):
            until(n_chunks + c)
            line.arrive(n_chunks + c)
            for quarter in range(PIECES):
                pump()

                @pl.loop(0, length // PIECES // 16)
                def _(index):
                    start = quarter * (length // PIECES) + index * 16
                    rows = pl.ds(pl.multiple_of(start, 16), 16)
                    at = pl.ds(pl.multiple_of(c * length + start, 16), 16)
                    value = x_all[at, :].astype(FLOAT)
                    rate = rms_scale(value)
                    grad = joined(total, n_chunks + c, rows)
                    by_gain = grad * (value * rate)
                    gain_total[...] += by_gain[:8] + by_gain[8:]
                    inner = gain[...] * grad
                    mean = jnp.mean(inner * value, -1, keepdims=True)
                    resid_all[at, :] = (
                        resid_all[at, :] + rate * inner - value * (rate * rate * rate * mean)
                    )

            token_store(c).start()

        here = lax.axis_index("ctx")
        over_ctx[here, :, :width] = jnp.sum(gain_total[...], 0, keepdims=True)
        over_ctx[here, :, width : 2 * width] = gain_two_grad[...]
        share(over_ctx, "ctx", n_ctx, ctx_send, ctx_recv)
        value = over_ctx[0]
        for place in range(1, n_ctx):
            value = value + over_ctx[place]
        over_fsdp[lax.axis_index("fsdp")] = value
        share(over_fsdp, "fsdp", n_fsdp, fsdp_send, fsdp_recv)
        value = over_fsdp[0]
        for place in range(1, n_fsdp):
            value = value + over_fsdp[place]
        vectors_out[...] = value
        while any(square[1] < 5 for square in squares):
            pump()
        for c in range(n_chunks):
            token_store(c).wait()
            output_store(c).wait()

    pl.run_scoped(
        ends_of,
        pltpu.VMEM((rows, width), FLOAT),
        pltpu.VMEM((rows, width), HALF),
        pltpu.VMEM((rows, width), HALF),
    )
    for square in squares:
        square[0].settle()
    for square in stores:
        square.store().wait()

    @pl.loop(0, 2 * n_chunks)
    def _(job):
        line.settle(job)
        line.release(job)


def run_tail(small, large, n_fsdp, n_ctx, n_tp):
    grad_gated, w_down, tokens = large[2], large[4], large[11]
    n_seq, length, chan = grad_gated.shape
    rows, width = tokens.shape
    units = w_down.shape[0]
    piece = width // PIECES
    size = 2 * width + 2 * chan
    depth = width // 2
    spread = width if n_fsdp != 2 else depth
    vmem = pl.BlockSpec(memory_space=pltpu.VMEM)
    hbm = pl.BlockSpec(memory_space=pl.ANY)
    slots = pltpu.VMEM((2 * n_seq, PIECES, length, piece), HALF)
    sems = pltpu.SemaphoreType.DMA((2 * n_seq, PIECES))
    n_in, n_out = depth // TILE, chan // TILE
    n_squares = n_in + n_out + len(bands(units, TILE))
    wide = max(3 * chan, depth)

    def tiles(*shape):
        return [pltpu.VMEM((*shape[:-1], shape[-1] // cut), HALF) for cut in (1, 2, 4)]

    return pl.pallas_call(
        functools.partial(tail, n_fsdp, n_ctx, n_tp),
        name="tail",
        out_shape=(
            jax.ShapeDtypeStruct((rows, width), FLOAT),
            jax.ShapeDtypeStruct((rows, width), HALF),
            jax.ShapeDtypeStruct((1, size), FLOAT),
            jax.ShapeDtypeStruct((spread, 3 * chan), HALF),
            jax.ShapeDtypeStruct((chan, spread), HALF),
            jax.ShapeDtypeStruct((units, spread), HALF),
        ),
        in_specs=[vmem] * len(small) + [hbm] * len(large),
        out_specs=[hbm, hbm, vmem, hbm, hbm, hbm],
        scratch_shapes=[
            pltpu.VMEM((n_seq, length, 3 * chan), HALF),
            slots,
            pltpu.VMEM((2 * n_seq, PIECES, length, piece), HALF),
            slots,
            pltpu.VMEM((2, TILE, wide), HALF),
            pltpu.VMEM((2, TILE, wide), HALF),
            *tiles(n_in, TILE, 3 * chan),
            *tiles(n_out, TILE, depth),
            *tiles(units, depth),
            pltpu.VMEM((8, width), FLOAT),
            pltpu.VMEM((n_ctx, 2, n_seq, chan), FLOAT),
            pltpu.VMEM((n_tp, n_seq, length), FLOAT),
            pltpu.VMEM((n_ctx, 1, size), FLOAT),
            pltpu.VMEM((n_fsdp, 1, size), FLOAT),
            pltpu.SemaphoreType.DMA((6,)),
            pltpu.SemaphoreType.DMA((2, n_seq)),
            pltpu.SemaphoreType.DMA((n_ctx,)),
            pltpu.SemaphoreType.DMA((n_ctx,)),
            pltpu.SemaphoreType.DMA((n_tp,)),
            pltpu.SemaphoreType.DMA((n_tp,)),
            pltpu.SemaphoreType.DMA((n_ctx,)),
            pltpu.SemaphoreType.DMA((n_ctx,)),
            pltpu.SemaphoreType.DMA((n_fsdp,)),
            pltpu.SemaphoreType.DMA((n_fsdp,)),
            pltpu.SemaphoreType.DMA((2,)),
            pltpu.SemaphoreType.DMA((2,)),
            pltpu.SemaphoreType.DMA((2,)),
            pltpu.SemaphoreType.DMA((n_squares, 4)),
            pltpu.SemaphoreType.DMA((n_squares, 4)),
            pltpu.SemaphoreType.DMA((n_squares,)),
        ]
        + [sems] * 4,
        compiler_params=pltpu.CompilerParams(
            collective_id=3, has_side_effects=True, vmem_limit_bytes=63 * MIB
        ),
        cost_estimate=pl.CostEstimate(
            flops=10 * rows * width * units, bytes_accessed=700 * MIB, transcendentals=0
        ),
    )(*small, *large)


def gather_fsdp(part, dim, count):
    if count != 2:
        return lax.all_gather(part, "fsdp", axis=dim, tiled=True)
    other = lax.ppermute(part, "fsdp", [(0, 1), (1, 0)])
    first = lax.axis_index("fsdp") == 0
    return jnp.concatenate(
        [jnp.where(first, part, other), jnp.where(first, other, part)], dim
    )


def keep_flags(segment_ids, count):
    last = lax.ppermute(
        segment_ids[:, -1:].astype(FLOAT), "ctx", [(place, place + 1) for place in range(count - 1)]
    )
    seg = segment_ids.astype(FLOAT)
    before = jnp.concatenate([last, seg[:, :-1]], 1)
    token = lax.broadcasted_iota(jnp.int32, seg.shape, 1)
    start = (token == 0) & (lax.axis_index("ctx") == 0)
    return jnp.where(start, 0.0, (seg == before).astype(FLOAT))


def local(
    sizes,
    tokens, segment_ids, w_in, w_out, w_glu, w_down, gain_one, gain_two, gate_gain, lower, cotangent,
):
    n_fsdp, n_ctx, n_tp = sizes
    n_seq, length, width = tokens.shape
    rows = n_seq * length
    chan = w_in.shape[2]
    gain_a = gather_fsdp(gain_one.astype(HALF)[None], 1, n_fsdp).astype(FLOAT)
    gain_b = gather_fsdp(gain_two.astype(HALF)[None], 1, n_fsdp).astype(FLOAT)
    w_in_all = gather_fsdp(w_in.astype(HALF), 1, n_fsdp)
    parts = (w_out.astype(HALF), w_glu[:, 0].astype(HALF), w_glu[:, 1].astype(HALF), w_down.astype(HALF))
    if n_fsdp != 2:
        parts = tuple(gather_fsdp(part, dim, n_fsdp) for part, dim in zip(parts, (1, 0, 0, 1)))
    keep = keep_flags(segment_ids, n_ctx)[..., None]
    gain_gate = gate_gain[None]
    low = lower[None]
    flat = tokens.reshape(rows, width).astype(FLOAT)
    scale_one = rms_scale(flat)
    normed = (flat * scale_one * gain_a).astype(HALF)
    proj = jnp.einsum("td,wdc->wtc", normed, w_in_all, preferred_element_type=FLOAT)
    proj = proj.reshape(3, n_seq, length, chan)
    gated, state, gate_scale, carry = run_scan_forward(
        proj, keep, gain_gate, low, n_ctx, n_tp, width
    )
    gated = gated.reshape(rows, chan)
    x_half = tokens.reshape(rows, width)
    grad_y_half = cotangent.reshape(rows, width)
    (
        mixed, _, act, _, grad_resid, grad_mixed, grad_gated, grad_w_glu, w_down_all, grad_gain_two
    ) = run_middle(gated, x_half, grad_y_half, gain_b, parts, n_fsdp, length)
    if n_fsdp != 2:
        grad_w_glu = lax.psum_scatter(grad_w_glu, "fsdp", scatter_dimension=1, tiled=True)
    grad_w_glu = lax.psum(grad_w_glu, "ctx")
    grad_tokens, output, vectors, grad_w_in, grad_w_out, grad_w_down = run_tail(
        (keep, gain_gate, low, gate_scale, carry, gain_a, grad_gain_two),
        (
            proj, state, grad_gated.reshape(n_seq, length, chan), w_in_all, w_down_all, act, normed,
            grad_mixed, gated, grad_y_half, grad_resid, x_half, mixed,
        ),
        n_fsdp, n_ctx, n_tp,
    )
    if n_fsdp == 2:
        grad_w_in = jnp.moveaxis(grad_w_in.reshape(width // 2, 3, chan), 1, 0)
    else:
        grad_w_in, grad_w_out, grad_w_down = (
            lax.psum(lax.psum_scatter(value, "fsdp", scatter_dimension=dim, tiled=True), "ctx")
            for value, dim in (
                (jnp.moveaxis(grad_w_in.reshape(width, 3, chan), 1, 0), 1),
                (grad_w_out, 1),
                (grad_w_down, 1),
            )
        )
    part = gain_one.shape[0]
    begin = lax.axis_index("fsdp") * part
    return (
        output.reshape(n_seq, length, width),
        grad_tokens.reshape(n_seq, length, width),
        grad_w_in.astype(FLOAT),
        grad_w_out.astype(FLOAT),
        jnp.moveaxis(grad_w_glu, 0, 1).astype(FLOAT),
        grad_w_down.astype(FLOAT),
        lax.dynamic_slice(vectors[0], (begin,), (part,)),
        lax.dynamic_slice(vectors[0], (width + begin,), (part,)),
        vectors[0, 2 * width : 2 * width + chan],
        vectors[0, 2 * width + chan :],
    )


def solution(mesh):
    sizes = tuple(mesh.shape[axis] for axis in ("fsdp", "ctx", "tp"))
    return jax.shard_map(
        functools.partial(local, sizes),
        mesh=mesh,
        in_specs=(
            P("fsdp", "ctx", None),
            P("fsdp", "ctx"),
            P(None, "fsdp", "tp"),
            P("tp", "fsdp"),
            P("fsdp", None, "tp"),
            P("tp", "fsdp"),
            P("fsdp"),
            P("fsdp"),
            P("tp"),
            P("tp"),
            P("fsdp", "ctx", None),
        ),
        out_specs=(
            P("fsdp", "ctx", None),
            P("fsdp", "ctx", None),
            P(None, "fsdp", "tp"),
            P("tp", "fsdp"),
            P("fsdp", None, "tp"),
            P("tp", "fsdp"),
            P("fsdp"),
            P("fsdp"),
            P("tp"),
            P("tp"),
        ),
        check_vma=False,
    )
```

time: 700 us -> 727 us (1.039)
  Pallas kernels: 496 us -> 594 us
  matrix products: 53.1 us -> 8.65 us
  waiting for transfers between devices: 35.1 us -> 0.03 us
    pallas_call x3 -> x2, Pallas kernels: 480 us -> 579 us  [the longest x1 335 us: run_tail(): pl.pallas_call(functools.partial(tail, n_fsdp, n_ctx, n_tp), name='tail',...]
    dot_general x4 -> x0, matrix products: 43.9 us -> none  [the longest x1 18.3 us: local(): jnp.einsum('td,wtf->dwf', normed_two, grad_glu, preferred_element_type=FL...]
    reduce_scatter x4 -> x0, waiting for transfers between devices: 19.1 us -> none  [local(): lax.psum_scatter(value.astype(HALF), 'fsdp', scatter_dimension=dim, tiled...]
    psum x1, waiting for transfers between devices: 16 us -> 0.01 us  [local(): grad_w_glu = lax.psum(grad_w_glu, 'ctx')]
    unnamed x54 -> x46, local copies, waits for them, and re-layouts: 45.2 us -> 44.7 us
  transfers between devices with their start and end apart: 9 -> 5, of which waited for: 2 -> 0; matrix products, arithmetic and copies ran while one was open for 9% -> 6% of each run, Pallas kernels for 35% -> 47%
where the time goes in v3:
time: 727 us; the launch traced here: 719 us
  Pallas kernels  594 us (82%)
  local copies, waits for them, and re-layouts  61 us (8%)
  other arithmetic  34.2 us (5%)
  between operations  14.7 us (2%)
  matrix products  8.65 us (1%)
    pallas_call x1, Pallas kernels, run_tail(): pl.pallas_call(functools.partial(tail, n_fsdp, n_ctx, n_tp), name='tail',...  335 us
    pallas_call x1, Pallas kernels, run_middle(): pl.pallas_call(functools.partial(middle, n_fsdp, length), name='middle',...  244 us
    unnamed x46, local copies, waits for them, and re-layouts  44.7 us
    pallas_call x1, Pallas kernels, run_scan_forward(): pl.pallas_call(functools.partial(scan_forward, n_ctx, n_tp, width), name=...  15.4 us
  transfers between devices with their start and end apart: 5, of which 0 were waited for; matrix products, arithmetic and copies ran while one was open for 6% of the time, Pallas kernels for 47%

profile of v3, /device:TPU:0, one launch (start us, length us, event | category | flops | bytes accessed | tf_op | source)
XLA Modules:
  0.0 718.7 jit_solution(14713165494067470644)
XLA Ops:
  7.2 0.0 copy-start.18
  7.2 0.0 copy-start.19
  7.2 0.0 copy-start.16
  7.2 0.0 all-reduce.2.cloned.1.call-start
  7.3 4.9 convert_element_type.71
  12.1 0.5 collective-permute-start.1
  12.6 0.0 copy-done.18
  12.6 0.1 collective-permute-start.2
  12.7 0.0 copy-done.19
  12.7 0.5 collective-permute-start.3
  13.2 0.0 copy-done.16
  13.2 0.1 slice_convert_fusion
  13.3 4.4 collective-permute-start
  17.7 3.1 multiply_reduce_fusion
  20.9 4.9 copy.37
  25.8 0.0 copy-start.14
  25.8 4.8 convert_element_type.83.wd_part
  30.6 0.0 copy-done.14
  30.6 1.2 convert_element_type.80.wo_part
  31.8 3.0 slice_bitcast_fusion
  34.8 0.0 collective-permute-done
  34.8 0.1 select_bitcast_fusion
  34.9 0.2 copy.30.keep
  35.1 0.0 copy-start.1
  35.1 0.0 collective-permute-done.2
  35.1 0.0 collective-permute-done.3
  35.2 0.7 maximum_convert_fusion.1.gain
  35.9 3.2 multiply_convert_fusion.normed
  39.1 0.0 copy-start.11
  39.1 0.0 collective-permute-done.1
  39.1 5.8 broadcast_select_fusion.1
  44.9 0.0 copy-start.8
  44.9 0.0 copy-start.10
  44.9 0.0 copy-done.11
  44.9 1.6 copy-done.8
  46.5 1.0 copy-done.10
  47.6 8.7 %fusion.2 = f32[3,1024,512]{1,2,0:T(8,128)} fusion(bf16[1024,2048]{1,0:T(8,128)(2,1)S(1)} %multiply_convert_fusion.normed, bf16[3,1024,512]{2,1,0:T(8,128)(2,1)S(1)} %get-tuple-element.71, bf16[3,1024,512]{2,1,0:T(8,128)(2,1)S(1)} %get-tuple-element.70), kind=kOutput, calls=%fused_computation.10 | convolution fusion | flops 6455033856 | bytes 16777216 | tf_op jit(solution)/shard_map/td,wdc->wtc/dot_general | solution.py:1269
  56.2 6.6 copy.27
  62.8 0.0 copy-done.1
  62.8 0.0 copy-done.2
  62.8 0.0 copy-start
  62.8 2.8 copy-done
  65.6 15.4 %scan_forward.1 = (bf16[4,256,512]{2,1,0:T(8,128)(2,1)S(1)}, f32[4,256,512]{2,1,0:T(8,128)S(1)}, f32[4,256]{1,0:T(4,128)S(1)}, f32[4,512]{1,0:T(4,128)S(1)}) custom-call(f32[3,4,256,512]{3,2,1,0:T(8,128)S(1)} %bitcast.36, f32[4,256,1]{2,1,0:T(8,128)S(1)} %copy.30.keep, f32[1,512]{1,0:T(1,128)S(1)} %bitcast.38, f32[1,512]{1,0:T(1,128)S(1)} %bitcast.40), custom_call_target="tpu_custom_call" | custom-call | tf_op jit(solution)/shard_map/scan_forward/pallas_call | solution.py:136
  81.0 0.0 copy-start.4
  81.0 1.3 copy-done.4
  82.4 1.1 copy-done.5
  83.4 0.6 copy-done.6
  84.0 0.6 copy-done.7
  84.6 243.6 %middle.1 = (bf16[1024,2048]{1,0:T(8,128)(2,1)}, bf16[1024,2048]{1,0:T(8,128)(2,1)}, bf16[1024,1408]{1,0:T(8,128)(2,1)}, bf16[2,1024,1408]{2,1,0:T(8,128)(2,1)},...) custom-call(bf16[1024,512]{1,0:T(8,128)(2,1)} %bitcast.41, ...), custom_call_target="tpu_custom_call" | custom-call | flops 47244640256 | bytes 419430400 | tf_op jit(solution)/shard_map/middle/pallas_call | solution.py:710
  328.2 0.0 copy-start.9
  328.2 0.0 all-reduce.2.cloned.1.call-update
  328.3 0.6 maximum_convert_fusion.gain
  328.9 1.2 copy-done.9
  330.1 5.0 pad_maximum_fusion.w_in
  335.1 335.5 %tail.1 = (f32[1024,2048]{1,0:T(8,128)}, bf16[1024,2048]{1,0:T(8,128)(2,1)}, f32[1,5120]{1,0:T(1,128)}, bf16[1024,1536]{1,0:T(8,128)(2,1)}, bf16[512,1024]{1,0:T(8,128)(2,1)}, /*index=5*/bf16[1408,1024]{1,0:T(8,128)(2,1)}) custom-call(f32[4,256,1]{2,1,0:T(8,128)} %copy-done.1, f32[1,512]{1,0:T(1,128)} %bitcast.37, f32[1,512]{1,0:T(1,128)} %bitcast.39, ...), custom_call_target="tpu_custom_call" | custom-call | flops 29527900160 | bytes 734003200 | tf_op jit(solution)/shard_map/tail/pallas_call | solution.py:1173
  670.6 5.4 copy.31
  676.0 6.7 copy.32
  682.7 3.3 convert_element_type.90
  686.0 1.6 convert_element_type.87
  687.5 0.6 constant_dynamic-slice_fusion
  688.1 0.6 fusion.7
  688.7 12.8 %copy.33 = f32[1024,2,1408]{2,1,0:T(2,128)} copy(bf16[1024,2,1408]{2,0,1:T(8,128)(2,1)} %all-reduce.2.cloned.1.call-done) | data formatting | bytes 17301504
  701.5 2.0 copy.41
  703.5 7.9 %copy.42 = f32[4,256,2048]{2,1,0:T(8,128)} copy(f32[4,256,2048]{2,1,0:T(8,128)} %bitcast.46) | data formatting | bytes 16777216
  (25 shorter events, 0.1 us)
Async XLA Ops:
  7.2 5.4 copy-start.18
  7.2 5.5 copy-start.19
  7.2 6.0 copy-start.16
  7.2 681.5 %all-reduce.2.cloned.1.call-start = ((), (), s32[]{:S(2)}) async-start(), calls=%async_computation | async-start | bytes 11534336 | tf_op jit(solution)/shard_map/psum | solution.py:1282
  12.1 27.0 %collective-permute-start.1 = (bf16[3,1024,512]{2,1,0:T(8,128)(2,1)}, bf16[3,1024,512]{2,1,0:T(8,128)(2,1)}, u32[]{:S(2)}, u32[]{:S(2)}) collective-permute-start(bf16[3,1024,512]{2,1,0:T(8,128)(2,1)} %convert_element_type.71), channel_id=1, source_target_pairs={{0,16},{16,0},{1,17},{17,1},{2,18},{18,2},{3,19},{19,3},{4,20},{20... | collective-permute-start | bytes 9437192 | tf_op jit(solution)/shard_map/ppermute | solution.py:1231
  12.6 22.5 %collective-permute-start.2 = (bf16[1,1024]{1,0:T(2,128)(2,1)S(1)}, bf16[1,1024]{1,0:T(2,128)(2,1)S(1)}, u32[]{:S(2)}, u32[]{:S(2)}) collective-permute-start(bf16[1,1024]{1,0:T(2,128)(2,1)S(1)} %broadcast_in_dim.24), channel_id=1, source_target_pairs={{0,16},{16,0},{1,17},{17,1},{2,18},{18,2},{3,19},{19,3},{4,20},{20... | collective-permute-start | bytes 6152 | tf_op jit(solution)/shard_map/ppermute | solution.py:1231
  12.7 22.4 %collective-permute-start.3 = (bf16[1,1024]{1,0:T(2,128)(2,1)S(1)}, bf16[1,1024]{1,0:T(2,128)(2,1)S(1)}, u32[]{:S(2)}, u32[]{:S(2)}) collective-permute-start(bf16[1,1024]{1,0:T(2,128)(2,1)S(1)} %broadcast_in_dim.25), channel_id=1, source_target_pairs={{0,16},{16,0},{1,17},{17,1},{2,18},{18,2},{3,19},{19,3},{4,20},{20... | collective-permute-start | bytes 6152 | tf_op jit(solution)/shard_map/ppermute | solution.py:1231
  13.3 21.5 %collective-permute-start = (f32[4,1]{1,0:T(4,128)S(1)}, f32[4,1]{1,0:T(4,128)S(1)}, u32[]{:S(2)}, u32[]{:S(2)}) collective-permute-start(f32[4,1]{1,0:T(4,128)S(1)} %slice_convert_fusion), channel_id=1, source_target_pairs={{0,4},{4,8},{8,12},{1,5},{5,9},{9,13},{2,6},{6,10},{10,14},{3,7},{... | collective-permute-start | bytes 56 | tf_op jit(solution)/shard_map/ppermute | solution.py:1239
  25.8 4.8 copy-start.14
  35.1 27.7 %copy-start.1 = (f32[4,256,1]{2,1,0:T(8,128)}, f32[4,256,1]{2,1,0:T(8,128)S(1)}, u32[]{:S(2)}) copy-start(f32[4,256,1]{2,1,0:T(8,128)S(1)} %copy.30.keep) | copy-start | bytes 12292
  39.1 5.8 copy-start.11
  44.9 1.7 copy-start.8
  44.9 2.7 copy-start.10
  56.2 6.6 copy-start.2
  56.2 6.6 copy-start.3
  62.8 2.8 copy-start
  81.0 1.3 copy-start.4
  82.4 1.1 copy-start.5
  83.4 0.6 copy-start.6
  84.0 0.6 copy-start.7
  328.2 1.9 copy-start.9
  676.0 6.7 copy-start.13
  682.7 3.3 copy-start.15
  682.7 4.8 copy-start.17
  688.7 12.8 %copy-start.12 = (bf16[1024,2048]{1,0:T(8,128)(2,1)S(1)}, bf16[1024,2048]{1,0:T(8,128)(2,1)}, u32[]{:S(2)}) copy-start(bf16[1024,2048]{1,0:T(8,128)(2,1)} %get-tuple-element.39) | copy-start | bytes 12582916
Sparse Core Ops, SparseCore 0:
  328.4 129.5 all-reduce.1

commit v4 on v3

--- a/solution.py
+++ b/solution.py
@@ -37,9 +37,9 @@
     return [{axis: lax.rem(mine + step, count)} for step in range(1, count)]
 
 
-def share(slots, axis, count, send, recv):
+def shares(slots, axis, count, send, recv):
     mine = lax.axis_index(axis)
-    copies = [
+    return [
         pltpu.make_async_remote_copy(
             src_ref=slots.at[mine],
             dst_ref=slots.at[mine],
@@ -50,6 +50,10 @@
         )
         for step, peer in enumerate(others(axis, count))
     ]
+
+
+def share(slots, axis, count, send, recv):
+    copies = shares(slots, axis, count, send, recv)
     for copy in copies:
         copy.start()
     for copy in copies:
@@ -227,26 +231,30 @@
         def _():
             self.inward(job, q).start()
 
-    def tick(self, job, step):
-        slot, cross_slot = self.slot(job, self.held), self.slot(job, self.cross)
+    def forward(self, job, q):
+        slot = self.slot(job, self.held)
 
         @pl.when(self.inner)
         def _():
-            if step < PIECES:
-                self.inward(job, step).wait_recv()
-                value = self.held[slot, step].astype(FLOAT) + self.total[job, step].astype(FLOAT)
-                self.held[slot, step] = value.astype(HALF)
-                self.across(job, step).start()
-            if step > 0:
-                q = step - 1
-                self.across(job, q).wait_recv()
-                value = self.held[slot, q].astype(FLOAT) + self.cross[cross_slot, q].astype(FLOAT)
-                self.total[job, q] = value.astype(HALF)
-                self.outward(job, q).start()
-
-    def relay(self, job):
-        for step in range(PIECES + 1):
-            self.tick(job, step)
+            self.inward(job, q).wait_recv()
+            self.held[slot, q] = self.held[slot, q] + self.total[job, q]
+            self.across(job, q).start()
+
+    def close(self, job, q):
+        slot, cross_slot = self.slot(job, self.held), self.slot(job, self.cross)
+
+        @pl.when(self.inner)
+        def _():
+            self.across(job, q).wait_recv()
+            self.total[job, q] = self.held[slot, q] + self.cross[cross_slot, q]
+            self.outward(job, q).start()
+
+    def tick(self, base, step):
+        if step > 0:
+            self.close(base, step - 1)
+        if step < PIECES:
+            ahead = step + 1
+            self.forward(base + ahead // PIECES, ahead % PIECES)
 
     def arrive(self, job):
         @pl.when(jnp.logical_not(self.inner))
@@ -332,6 +340,10 @@
     return jnp.concatenate([ref[c, q, rows, :].astype(FLOAT) for q in range(PIECES)], -1)
 
 
+def add_to(target, extra, rows):
+    target[rows, :] = target[rows, :] + extra[rows, :]
+
+
 def halves(n_fsdp, store_sem, send_sem, recv_sem, spare, inbox):
     mine = lax.axis_index("fsdp")
     pending = {}
@@ -366,12 +378,7 @@
         if n_fsdp == 2:
             send(index, view).wait_recv()
             extra = view(inbox.at[slot])
-
-            def add(rows):
-                value = target[rows, :].astype(FLOAT) + extra[rows, :].astype(FLOAT)
-                target[rows, :] = value.astype(HALF)
-
-            row_blocks(target.shape[0], 16, add)
+            row_blocks(target.shape[0], 32, lambda rows: add_to(target, extra, rows))
 
     def finish():
         for wait in pending.values():
@@ -431,11 +438,8 @@
         )
 
     def add(self, cols, extra):
-        def body(rows):
-            value = self.tile[rows, cols].astype(FLOAT) + extra[rows, :].astype(FLOAT)
-            self.tile[rows, cols] = value.astype(HALF)
-
-        row_blocks(self.tile.shape[0], 16, body)
+        target = self.tile.at[:, cols]
+        row_blocks(self.tile.shape[0], 32, lambda rows: add_to(target, extra, rows))
 
     def store(self):
         return pltpu.make_async_copy(self.tile, self.place_of(), self.store_sem.at[self.index])
@@ -538,7 +542,9 @@
 
     for load in loads:
         load.wait()
-    line.relay(0)
+    line.forward(0, 0)
+    for step in range(PIECES + 1):
+        line.tick(0, step)
     for index in (1, 2, 3):
         ready(index)
     w_down_store = pltpu.make_async_copy(wd, w_down_out, again_sem.at[3])
@@ -681,7 +687,10 @@
                 if step % 2 == 0:
                     weight_item(count)
                     count += 1
-                line.tick(n_chunks + c + 1, step)
+                if c + 2 == n_chunks and step == PIECES - 1:
+                    line.close(2 * n_chunks - 1, step - 1)
+                else:
+                    line.tick(n_chunks + c + 1, step)
     finish()
     for store in own_stores.values():
         store.wait()
@@ -764,22 +773,15 @@
     )(gated, tokens, cotangent, gain, *parts)
 
 
-def scan_back(
-    n_ctx, n_tp, width, pump,
-    proj, keep, gain, lower, state, scale, carry_in, near,
-    grad_proj, gain_out, lower_out,
-    reach, rate_wide, cross_wide, ends, cross, ctx_sems, tp_sems,
-):
+def scan_cross(gate_all, state, scale, gain, near, grad_proj, gain_out, cross):
     n_seq, length, chan = state.shape
-    low = lower[...].reshape(1, 1, chan)
     mine = lax.axis_index("tp")
     gain_total = jnp.zeros((8, chan), FLOAT)
     for seq in range(n_seq):
         for start in range(0, length, BLOCK):
             rows = slice(start, start + BLOCK)
             rate = columns(scale[seq : seq + 1, rows])
-            rate_wide[seq, rows, :] = rate
-            gate = proj[2, seq, rows, :]
+            gate = gate_all[seq, rows, :]
             sig = jax.nn.sigmoid(gate)
             swish = gate * sig
             value = state[seq, rows, :]
@@ -792,8 +794,16 @@
             near[seq, rows, :] = grad_unit
             cross[mine, seq : seq + 1, rows] = lane_sums(grad_unit * value)
     gain_out[...] = jnp.sum(gain_total, 0, keepdims=True)
-    share(cross, "tp", n_tp, *tp_sems)
-    pump()
+
+
+def scan_back(
+    n_ctx, n_tp, width, pump,
+    proj, keep, lower, state, scale, carry_in, near,
+    grad_proj, lower_out,
+    reach, rate_wide, cross_wide, ends, cross, ctx_sems,
+):
+    n_seq, length, chan = state.shape
+    low = lower[...].reshape(1, 1, chan)
     total = cross[0]
     for place in range(1, n_tp):
         total = total + cross[place]
@@ -802,6 +812,7 @@
     for seq in range(n_seq):
         for start in range(0, length, BLOCK):
             rows = slice(start, start + BLOCK)
+            rate_wide[seq, rows, :] = columns(rate[seq : seq + 1, rows])
             cross_wide[seq, rows, :] = columns(total[seq : seq + 1, rows])
 
     row = lax.broadcasted_iota(jnp.int32, (n_seq, GROUP, chan), 1)
@@ -877,7 +888,7 @@
     grad_tokens_out, output_out, vectors_out, w_in_out, w_out_out, w_down_out,
     grad_proj, held, crossed, total, spare, inbox,
     in_tile, in_half, in_quarter, out_tile, out_half, out_quarter, down_tile, down_half, down_quarter,
-    gain_total, ends, cross, over_ctx, over_fsdp,
+    gain_total, ends, cross, over_ctx, over_fsdp, near,
     load_sem, store_sem, end_send, end_recv, cross_send, cross_recv, ctx_send, ctx_recv,
     fsdp_send, fsdp_recv, part_sem, part_send, part_recv, square_send, square_recv, square_store,
     *line_sems,
@@ -892,20 +903,26 @@
     whole = n_fsdp != 2
     greet(others("ctx", n_ctx) + others("tp", n_tp) + others("fsdp", n_fsdp))
     line = Line(held, crossed, total, line_sems)
-    ticks = [(job, step) for job in range(2 * n_chunks) for step in range(PIECES + 1)]
+    pieces = [(job, q) for job in range(2 * n_chunks) for q in range(PIECES)]
+    relay = [(line.forward, spot) for spot in pieces[:2]]
+    for index, spot in enumerate(pieces):
+        relay.append((line.close, spot))
+        relay += [(line.forward, ahead) for ahead in pieces[index + 2 : index + 3]]
     squares = []
     turn = [0]
     SPACE = 3
 
-    def pump(count=1):
-        for _ in range(count):
-            if ticks:
-                line.tick(*ticks.pop(0))
-            for index, square in enumerate(squares):
-                if square[1] < 5 and turn[0] >= square[2] + SPACE * square[1]:
-                    square[0].advance(square[1])
-                    square[1] += 1
-            turn[0] += 1
+    def pump():
+        while relay:
+            action, spot = relay.pop(0)
+            action(*spot)
+            if action == line.forward:
+                break
+        for square in squares:
+            if square[1] < 5 and turn[0] >= square[2] + SPACE * square[1]:
+                square[0].advance(square[1])
+                square[1] += 1
+        turn[0] += 1
 
     def start_loads(pairs, first=0):
         copies = [
@@ -919,8 +936,25 @@
     def chunk_rows(c):
         return pl.ds(c * length, length) if isinstance(c, int) else span(c * length, length, length)
 
+    shape = (n_seq, length, chan)
+
+    crossing = shares(cross, "tp", n_tp, cross_send, cross_recv)
+
     def down_terms(w_all, act_all):
-        for copy in start_loads([(w_down, w_all), (act, act_all)]):
+        copies = start_loads([(w_down, w_all), (act, act_all)], 3)
+
+        def cross_terms(gate_all, state_all):
+            for copy in start_loads(
+                [(proj.at[2], gate_all), (state, state_all), (grad_gated, near)]
+            ):
+                copy.wait()
+            gain_at = over_ctx.at[lax.axis_index("ctx"), :, 2 * width : 2 * width + chan]
+            scan_cross(gate_all, state_all, scale, gate_gain, near, grad_proj, gain_at, cross)
+
+        pl.run_scoped(cross_terms, pltpu.VMEM(shape, FLOAT), pltpu.VMEM(shape, FLOAT))
+        for copy in crossing:
+            copy.start()
+        for copy in copies:
             copy.wait()
 
         for c in range(n_chunks):
@@ -930,30 +964,30 @@
                 held[c, q] = dot(act_all[chunk_rows(c), :], w_all[:, cols]).astype(HALF)
                 line.offer(c, q)
 
-            if c == n_chunks - 1:
+            if c >= n_chunks // 2:
                 pump()
 
     pl.run_scoped(
         down_terms, pltpu.VMEM((units, width), HALF), pltpu.VMEM((rows, units), HALF)
     )
 
-    def back(proj_all, state_all, near, reach, rate_wide, cross_wide):
-        for copy in start_loads([(proj, proj_all), (state, state_all), (grad_gated, near)]):
+    for copy in crossing:
+        copy.wait()
+
+    def back(proj_all, state_all, reach, rate_wide, cross_wide):
+        for copy in start_loads([(proj.at[:2], proj_all), (state, state_all)]):
             copy.wait()
-        gain_at = over_ctx.at[lax.axis_index("ctx"), :, 2 * width : 2 * width + chan]
         lower_at = over_ctx.at[lax.axis_index("ctx"), :, 2 * width + chan :]
         scan_back(
             n_ctx, n_tp, width, pump,
-            proj_all, keep, gate_gain, lower, state_all, scale, carry_in, near,
-            grad_proj, gain_at, lower_at,
-            reach, rate_wide, cross_wide, ends, cross, (end_send, end_recv), (cross_send, cross_recv),
-        )
-
-    shape = (n_seq, length, chan)
+            proj_all, keep, lower, state_all, scale, carry_in, near,
+            grad_proj, lower_at,
+            reach, rate_wide, cross_wide, ends, cross, (end_send, end_recv),
+        )
+
     pl.run_scoped(
         back,
-        pltpu.VMEM((3, *shape), FLOAT),
-        pltpu.VMEM(shape, FLOAT),
+        pltpu.VMEM((2, *shape), FLOAT),
         pltpu.VMEM(shape, FLOAT),
         pltpu.VMEM(shape, FLOAT),
         pltpu.VMEM((n_seq, length, BLOCK), FLOAT),
@@ -1059,8 +1093,9 @@
     finish()
 
     def ends_of(resid_all, x_all, mixed_all):
-        for copy in start_loads([(tokens, x_all), (mixed, mixed_all), (grad_resid, resid_all)]):
-            copy.wait()
+        copies = start_loads([(tokens, x_all), (mixed, mixed_all), (grad_resid, resid_all)])
+        copies[0].wait()
+        copies[1].wait()
         gain_total[...] = jnp.zeros_like(gain_total)
 
         def token_store(c):
@@ -1074,8 +1109,12 @@
             return pltpu.make_async_copy(mixed_all.at[at], output_out.at[at], store_sem.at[1, c])
 
         def until(job):
-            while ticks and ticks[0][0] <= job:
-                pump()
+            while (line.close, (job, PIECES - 1)) in relay:
+                if relay[0] == (line.close, (job, PIECES - 1)):
+                    action, spot = relay.pop(0)
+                    action(*spot)
+                else:
+                    pump()
 
         for c in range(n_chunks):
             until(c)
@@ -1090,6 +1129,7 @@
 
             output_store(c).start()
 
+        copies[2].wait()
         for c in range(n_chunks):
             until(n_chunks + c)
             line.arrive(n_chunks + c)
@@ -1198,6 +1238,7 @@
             pltpu.VMEM((n_tp, n_seq, length), FLOAT),
             pltpu.VMEM((n_ctx, 1, size), FLOAT),
             pltpu.VMEM((n_fsdp, 1, size), FLOAT),
+            pltpu.VMEM((n_seq, length, chan), FLOAT),
             pltpu.SemaphoreType.DMA((6,)),
             pltpu.SemaphoreType.DMA((2, n_seq)),
             pltpu.SemaphoreType.DMA((n_ctx,)),

time: 727 us -> 643 us (0.88)
  Pallas kernels: 594 us -> 510 us
    pallas_call x1, Pallas kernels: 335 us -> 271 us  [run_tail(): pl.pallas_call(functools.partial(tail, n_fsdp, n_ctx, n_tp), name='tail',...]
    pallas_call x1, Pallas kernels: 244 us -> 224 us  [run_middle(): pl.pallas_call(functools.partial(middle, n_fsdp, length), name='middle',...]
  transfers between devices with their start and end apart: 5 -> 5, of which waited for: 0 -> 0; matrix products, arithmetic and copies ran while one was open for 6% -> 7% of each run, Pallas kernels for 47% -> 43%
where the time goes in v4:
time: 643 us; the launch traced here: 635 us
  Pallas kernels  510 us (79%)
  local copies, waits for them, and re-layouts  61 us (9%)
  other arithmetic  34.2 us (5%)
  between operations  14.7 us (2%)
  matrix products  8.65 us (1%)
    pallas_call x1, Pallas kernels, run_tail(): pl.pallas_call(functools.partial(tail, n_fsdp, n_ctx, n_tp), name='tail',...  271 us
    pallas_call x1, Pallas kernels, run_middle(): pl.pallas_call(functools.partial(middle, n_fsdp, length), name='middle',...  224 us
    unnamed x46, local copies, waits for them, and re-layouts  44.7 us
    pallas_call x1, Pallas kernels, run_scan_forward(): pl.pallas_call(functools.partial(scan_forward, n_ctx, n_tp, width), name=...  15.4 us
  transfers between devices with their start and end apart: 5, of which 0 were waited for; matrix products, arithmetic and copies ran while one was open for 7% of the time, Pallas kernels for 43%

profile of v4, /device:TPU:0, one launch (start us, length us, event | category | flops | bytes accessed | tf_op | source)
XLA Modules:
  0.0 634.7 jit_solution(6298157608965528172)
XLA Ops:
  7.2 0.0 copy-start.18
  7.2 0.0 copy-start.19
  7.2 0.0 copy-start.16
  7.2 0.0 all-reduce.2.cloned.1.call-start
  7.3 4.9 convert_element_type.71
  12.1 0.5 collective-permute-start.1
  12.6 0.0 copy-done.18
  12.6 0.1 collective-permute-start.2
  12.7 0.0 copy-done.19
  12.7 0.5 collective-permute-start.3
  13.2 0.0 copy-done.16
  13.2 0.1 slice_convert_fusion
  13.3 4.4 collective-permute-start
  17.7 3.1 multiply_reduce_fusion
  20.9 4.9 copy.37
  25.8 0.0 copy-start.14
  25.8 4.8 convert_element_type.83.wd_part
  30.6 0.0 copy-done.14
  30.6 1.2 convert_element_type.80.wo_part
  31.8 3.0 slice_bitcast_fusion
  34.8 0.0 collective-permute-done
  34.8 0.1 select_bitcast_fusion
  34.9 0.2 copy.30.keep
  35.1 0.0 copy-start.1
  35.1 0.0 collective-permute-done.2
  35.1 0.0 collective-permute-done.3
  35.2 0.7 maximum_convert_fusion.1.gain
  35.9 3.2 multiply_convert_fusion.normed
  39.1 0.0 copy-start.11
  39.1 0.0 collective-permute-done.1
  39.1 5.8 broadcast_select_fusion.1
  44.9 0.0 copy-start.8
  44.9 0.0 copy-start.10
  44.9 0.0 copy-done.11
  44.9 1.6 copy-done.8
  46.5 1.0 copy-done.10
  47.6 8.7 %fusion.2 = f32[3,1024,512]{1,2,0:T(8,128)} fusion(bf16[1024,2048]{1,0:T(8,128)(2,1)S(1)} %multiply_convert_fusion.normed, bf16[3,1024,512]{2,1,0:T(8,128)(2,1)S(1)} %get-tuple-element.71, bf16[3,1024,512]{2,1,0:T(8,128)(2,1)S(1)} %get-tuple-element.70), kind=kOutput, calls=%fused_computation.10 | convolution fusion | flops 6455033856 | bytes 16777216 | tf_op jit(solution)/shard_map/td,wdc->wtc/dot_general | solution.py:1310
  56.2 6.6 %copy.27 = f32[3,1024,512]{2,1,0:T(8,128)} copy(f32[3,1024,512]{1,2,0:T(8,128)} %fusion.2) | data formatting | bytes 12582912 | tf_op jit(solution)/shard_map/td,wdc->wtc/transpose | solution.py:1310
  62.8 0.0 copy-done.1
  62.8 0.0 copy-done.2
  62.8 0.0 copy-start
  62.8 2.8 copy-done
  65.6 15.4 %scan_forward.1 = (bf16[4,256,512]{2,1,0:T(8,128)(2,1)S(1)}, f32[4,256,512]{2,1,0:T(8,128)S(1)}, f32[4,256]{1,0:T(4,128)S(1)}, f32[4,512]{1,0:T(4,128)S(1)}) custom-call(f32[3,4,256,512]{3,2,1,0:T(8,128)S(1)} %bitcast.36, f32[4,256,1]{2,1,0:T(8,128)S(1)} %copy.30.keep, f32[1,512]{1,0:T(1,128)S(1)} %bitcast.38, f32[1,512]{1,0:T(1,128)S(1)} %bitcast.40), custom_call_target="tpu_custom_call" | custom-call | tf_op jit(solution)/shard_map/scan_forward/pallas_call | solution.py:140
  81.0 0.0 copy-start.4
  81.0 1.3 copy-done.4
  82.4 1.1 copy-done.5
  83.4 0.6 copy-done.6
  84.0 0.6 copy-done.7
  84.6 224.4 %middle.1 = (bf16[1024,2048]{1,0:T(8,128)(2,1)}, bf16[1024,2048]{1,0:T(8,128)(2,1)}, bf16[1024,1408]{1,0:T(8,128)(2,1)}, bf16[2,1024,1408]{2,1,0:T(8,128)(2,1)},...) custom-call(bf16[1024,512]{1,0:T(8,128)(2,1)} %bitcast.41, ...), custom_call_target="tpu_custom_call" | custom-call | flops 47244640256 | bytes 419430400 | tf_op jit(solution)/shard_map/middle/pallas_call | solution.py:719
  309.0 0.0 copy-start.9
  309.0 0.0 all-reduce.2.cloned.1.call-update
  309.0 0.6 maximum_convert_fusion.gain
  309.6 1.2 copy-done.9
  310.9 5.0 pad_maximum_fusion.w_in
  315.9 270.7 %tail.1 = (f32[1024,2048]{1,0:T(8,128)}, bf16[1024,2048]{1,0:T(8,128)(2,1)}, f32[1,5120]{1,0:T(1,128)}, bf16[1024,1536]{1,0:T(8,128)(2,1)}, bf16[512,1024]{1,0:T(8,128)(2,1)}, /*index=5*/bf16[1408,1024]{1,0:T(8,128)(2,1)}) custom-call(f32[4,256,1]{2,1,0:T(8,128)} %copy-done.1, f32[1,512]{1,0:T(1,128)} %bitcast.37, f32[1,512]{1,0:T(1,128)} %bitcast.39, ...), custom_call_target="tpu_custom_call" | custom-call | flops 29527900160 | bytes 734003200 | tf_op jit(solution)/shard_map/tail/pallas_call | solution.py:1213
  586.6 5.4 copy.31
  592.0 6.7 %copy.32 = f32[3,1024,512]{2,1,0:T(8,128)} copy(f32[3,1024,512]{1,2,0:T(8,128)} %bitcast.43) | data formatting | bytes 12582912
  598.7 3.3 convert_element_type.90
  602.0 1.6 convert_element_type.87
  603.5 0.6 constant_dynamic-slice_fusion
  604.1 0.6 fusion.7
  604.7 12.8 %copy.33 = f32[1024,2,1408]{2,1,0:T(2,128)} copy(bf16[1024,2,1408]{2,0,1:T(8,128)(2,1)} %all-reduce.2.cloned.1.call-done) | data formatting | bytes 17301504
  617.5 2.0 copy.41
  619.5 7.9 %copy.42 = f32[4,256,2048]{2,1,0:T(8,128)} copy(f32[4,256,2048]{2,1,0:T(8,128)} %bitcast.46) | data formatting | bytes 16777216
  (25 shorter events, 0.1 us)
Async XLA Ops:
  7.2 5.4 copy-start.18
  7.2 5.5 copy-start.19
  7.2 6.0 copy-start.16
  7.2 597.5 %all-reduce.2.cloned.1.call-start = ((), (), s32[]{:S(2)}) async-start(), calls=%async_computation | async-start | bytes 11534336 | tf_op jit(solution)/shard_map/psum | solution.py:1323
  12.1 27.0 %collective-permute-start.1 = (bf16[3,1024,512]{2,1,0:T(8,128)(2,1)}, bf16[3,1024,512]{2,1,0:T(8,128)(2,1)}, u32[]{:S(2)}, u32[]{:S(2)}) collective-permute-start(bf16[3,1024,512]{2,1,0:T(8,128)(2,1)} %convert_element_type.71), channel_id=1, source_target_pairs={{0,16},{16,0},{1,17},{17,1},{2,18},{18,2},{3,19},{19,3},{4,20},{20... | collective-permute-start | bytes 9437192 | tf_op jit(solution)/shard_map/ppermute | solution.py:1272
  12.6 22.5 %collective-permute-start.2 = (bf16[1,1024]{1,0:T(2,128)(2,1)S(1)}, bf16[1,1024]{1,0:T(2,128)(2,1)S(1)}, u32[]{:S(2)}, u32[]{:S(2)}) collective-permute-start(bf16[1,1024]{1,0:T(2,128)(2,1)S(1)} %broadcast_in_dim.24), channel_id=1, source_target_pairs={{0,16},{16,0},{1,17},{17,1},{2,18},{18,2},{3,19},{19,3},{4,20},{20... | collective-permute-start | bytes 6152 | tf_op jit(solution)/shard_map/ppermute | solution.py:1272
  12.7 22.4 %collective-permute-start.3 = (bf16[1,1024]{1,0:T(2,128)(2,1)S(1)}, bf16[1,1024]{1,0:T(2,128)(2,1)S(1)}, u32[]{:S(2)}, u32[]{:S(2)}) collective-permute-start(bf16[1,1024]{1,0:T(2,128)(2,1)S(1)} %broadcast_in_dim.25), channel_id=1, source_target_pairs={{0,16},{16,0},{1,17},{17,1},{2,18},{18,2},{3,19},{19,3},{4,20},{20... | collective-permute-start | bytes 6152 | tf_op jit(solution)/shard_map/ppermute | solution.py:1272
  13.3 21.5 %collective-permute-start = (f32[4,1]{1,0:T(4,128)S(1)}, f32[4,1]{1,0:T(4,128)S(1)}, u32[]{:S(2)}, u32[]{:S(2)}) collective-permute-start(f32[4,1]{1,0:T(4,128)S(1)} %slice_convert_fusion), channel_id=1, source_target_pairs={{0,4},{4,8},{8,12},{1,5},{5,9},{9,13},{2,6},{6,10},{10,14},{3,7},{... | collective-permute-start | bytes 56 | tf_op jit(solution)/shard_map/ppermute | solution.py:1280
  25.8 4.8 copy-start.14
  35.1 27.7 %copy-start.1 = (f32[4,256,1]{2,1,0:T(8,128)}, f32[4,256,1]{2,1,0:T(8,128)S(1)}, u32[]{:S(2)}) copy-start(f32[4,256,1]{2,1,0:T(8,128)S(1)} %copy.30.keep) | copy-start | bytes 12292
  39.1 5.8 copy-start.11
  44.9 1.7 copy-start.8
  44.9 2.7 copy-start.10
  56.2 6.6 %copy-start.2 = (f32[512]{0:T(512)S(1)}, f32[512]{0:T(512)}, u32[]{:S(2)}) copy-start(f32[512]{0:T(512)} %param.19) | copy-start | bytes 6148
  56.2 6.6 %copy-start.3 = (f32[512]{0:T(512)S(1)}, f32[512]{0:T(512)}, u32[]{:S(2)}) copy-start(f32[512]{0:T(512)} %param.20) | copy-start | bytes 6148
  62.8 2.8 copy-start
  81.0 1.3 copy-start.4
  82.4 1.1 copy-start.5
  83.4 0.6 copy-start.6
  84.0 0.6 copy-start.7
  309.0 1.9 copy-start.9
  592.0 6.7 %copy-start.13 = (bf16[1408,1024]{1,0:T(8,128)(2,1)S(1)}, bf16[1408,1024]{1,0:T(8,128)(2,1)}, u32[]{:S(2)}) copy-start(bf16[1408,1024]{1,0:T(8,128)(2,1)} %get-tuple-element.44) | copy-start | bytes 8650756
  598.7 3.3 copy-start.15
  598.7 4.8 copy-start.17
  604.7 12.8 %copy-start.12 = (bf16[1024,2048]{1,0:T(8,128)(2,1)S(1)}, bf16[1024,2048]{1,0:T(8,128)(2,1)}, u32[]{:S(2)}) copy-start(bf16[1024,2048]{1,0:T(8,128)(2,1)} %get-tuple-element.39) | copy-start | bytes 12582916
Sparse Core Ops, SparseCore 0:
  309.1 179.3 all-reduce.1

commit v5 on v4

--- a/solution.py
+++ b/solution.py
@@ -394,15 +394,15 @@
 
     @property
     def tile(self):
-        return self.buffers[0].at[self.at]
+        return self.buffers[0].at[self.at[0]]
 
     @property
     def half(self):
-        return self.buffers[1].at[self.at]
+        return self.buffers[1].at[self.at[1]]
 
     @property
     def quarter(self):
-        return self.buffers[2].at[self.at]
+        return self.buffers[2].at[self.at[2]]
 
     def geometry(self):
         here = lax.axis_index("ctx")
@@ -410,23 +410,23 @@
         near, far = here + 1 - 2 * low, here + 2 - 4 * high
         bits = (low, high) if self.index % 2 == 0 else (high, low)
         peers = (near, far) if self.index % 2 == 0 else (far, near)
-        wide, thin = self.half.shape[1], self.quarter.shape[1]
+        wide, thin = self.half.shape[0], self.quarter.shape[0]
         begin = bits[0] * wide
         return (
             peers,
-            span(begin, wide, BLOCK),
-            span((1 - bits[0]) * wide, wide, BLOCK),
-            span(begin + bits[1] * thin, thin, BLOCK),
-            span(begin + (1 - bits[1]) * thin, thin, BLOCK),
+            span(begin, wide, wide),
+            span((1 - bits[0]) * wide, wide, wide),
+            span(begin + bits[1] * thin, thin, thin),
+            span(begin + (1 - bits[1]) * thin, thin, thin),
         )
 
     def round(self, number):
         peers, mine, yours, my_part, your_part = self.geometry()
         source, target, peer = (
-            (self.tile.at[:, yours], self.half, 0),
-            (self.tile.at[:, your_part], self.quarter, 1),
-            (self.tile.at[:, my_part], self.place_of().at[:, my_part], 1),
-            (self.place_of().at[:, mine], self.place_of().at[:, mine], 0),
+            (self.tile.at[yours], self.half, 0),
+            (self.tile.at[your_part], self.quarter, 1),
+            (self.tile.at[my_part], self.place_of().at[my_part], 1),
+            (self.place_of().at[mine], self.place_of().at[mine], 0),
         )[number]
         return pltpu.make_async_remote_copy(
             src_ref=source,
@@ -437,9 +437,9 @@
             device_id_type=MESH,
         )
 
-    def add(self, cols, extra):
-        target = self.tile.at[:, cols]
-        row_blocks(self.tile.shape[0], 32, lambda rows: add_to(target, extra, rows))
+    def add(self, part, extra):
+        target = self.tile.at[part]
+        row_blocks(extra.shape[0], 32, lambda rows: add_to(target, extra, rows))
 
     def store(self):
         return pltpu.make_async_copy(self.tile, self.place_of(), self.store_sem.at[self.index])
@@ -447,7 +447,7 @@
     def store_part(self):
         part = self.geometry()[3]
         return pltpu.make_async_copy(
-            self.tile.at[:, part], self.place_of().at[:, part], self.store_sem.at[self.index]
+            self.tile.at[part], self.place_of().at[part], self.store_sem.at[self.index]
         )
 
     def advance(self, number):
@@ -475,18 +475,18 @@
 
 
 def middle(
-    n_fsdp, CHUNK,
+    n_fsdp, n_ctx, CHUNK,
     gated, tokens, cotangent, gain, wo_part, wg_part, wu_part, wd_part,
     mixed_out, normed_out, act_out, grad_glu_out, grad_resid_out, grad_mixed_out,
-    grad_gated_out, w_glu_out, w_down_out, grad_gain_out,
+    grad_gated_out, w_gate_out, w_up_out, w_down_out, grad_gain_out,
     wo, wg, wu, wd, x_all, dy_all, held, crossed, total, normed, act, grad_glu,
-    grad_resid, grad_mixed, grad_gated, gain_total, spare, own, inbox,
-    weight_sem, weight_send, weight_recv, again_sem, own_sem, send_sem, recv_sem, load_sem, store_sem, *line_sems,
+    grad_resid, grad_mixed, grad_gated, gain_total, spare, inbox, half, quarter,
+    square_send, square_recv, square_store, weight_sem, weight_send, weight_recv, again_sem, own_sem, send_sem, recv_sem, load_sem, store_sem, *line_sems,
 ):
     n_chunks, _, _, piece = held.shape
     units = wd.shape[0]
     width = wd.shape[1]
-    peers = line_peers()
+    peers = line_peers() + others("ctx", n_ctx)
     if n_fsdp == 2:
         peers.append({"fsdp": 1 - lax.axis_index("fsdp")})
     greet(peers)
@@ -622,29 +622,41 @@
     depth = width // 2
     whole = n_fsdp != 2
     per_part = depth // TILE
-    own_stores = {}
+    squares, plain, turn = [], [], [0]
 
     def weight_item(index):
         if index >= 2 * per_part:
             return
         part, k = divmod(index, per_part)
         right = (wg, wu)[part].at[:rows]
-        slot = index % 2
-        if index > 1:
-            own_stores.pop(slot).wait()
+        out = (w_gate_out, w_up_out)[part]
 
         def compute(side):
             at = pl.ds(pl.multiple_of(side * depth + k * TILE, TILE), TILE)
             return lambda target: fill(target, wd[:rows, at].T, right, 0)
 
         at = slice(k * TILE + whole * depth, (k + 1) * TILE + whole * depth)
+        square = Square(
+            index, ((wg, wu)[part], half, quarter),
+            (slice(rows + k * TILE, rows + (k + 1) * TILE), k, k), lambda: out.at[at],
+            square_send, square_recv, square_store,
+        )
         item(
             index, lambda ref: ref, compute(1 - mine), compute(mine),
-            lambda: w_glu_out.at[part, k * TILE : (k + 1) * TILE], own.at[slot],
-        )
-        store = pltpu.make_async_copy(own.at[slot], w_glu_out.at[part, at], weight_sem.at[2 + slot])
-        store.start()
-        own_stores[slot] = store
+            lambda: out.at[k * TILE : (k + 1) * TILE], square.tile,
+        )
+        if whole or part == 1:
+            square.store().start()
+            plain.append(square)
+        else:
+            squares.append([square, 0, turn[0]])
+
+    def pump():
+        for square in squares:
+            if square[1] < 5 and turn[0] >= square[2] + 2 * square[1]:
+                square[0].advance(square[1])
+                square[1] += 1
+        turn[0] += 1
 
     def backward(c):
         line.arrive(n_chunks + c)
@@ -684,16 +696,20 @@
         backward(c)
         if c + 1 < n_chunks:
             for step in range(PIECES + 1):
-                if step % 2 == 0:
-                    weight_item(count)
-                    count += 1
+                weight_item(count)
+                count += 1
                 if c + 2 == n_chunks and step == PIECES - 1:
                     line.close(2 * n_chunks - 1, step - 1)
                 else:
                     line.tick(n_chunks + c + 1, step)
+                pump()
+    while any(square[1] < 5 for square in squares):
+        pump()
     finish()
-    for store in own_stores.values():
-        store.wait()
+    for square, _, _ in squares:
+        square.settle()
+    for square in plain:
+        square.store().wait()
 
     grad_gain_out[...] = jnp.sum(gain_total[...], 0, keepdims=True)
     for store in stores(n_chunks - 1, BACKWARD):
@@ -706,7 +722,7 @@
         line.release(n_chunks + c)
 
 
-def run_middle(gated, tokens, cotangent, gain, parts, n_fsdp, length):
+def run_middle(gated, tokens, cotangent, gain, parts, n_fsdp, n_ctx, length):
     rows, chan = gated.shape
     width = tokens.shape[1]
     wg = parts[1]
@@ -717,7 +733,7 @@
     hbm = pl.BlockSpec(memory_space=pl.ANY)
     sems = pltpu.SemaphoreType.DMA((2 * n_chunks, PIECES))
     return pl.pallas_call(
-        functools.partial(middle, n_fsdp, length),
+        functools.partial(middle, n_fsdp, n_ctx, length),
         name="middle",
         out_shape=(
             jax.ShapeDtypeStruct((rows, width), HALF),
@@ -727,12 +743,13 @@
             jax.ShapeDtypeStruct((rows, width), FLOAT),
             jax.ShapeDtypeStruct((rows, width), HALF),
             jax.ShapeDtypeStruct((rows, chan), FLOAT),
-            jax.ShapeDtypeStruct((2, width if n_fsdp != 2 else width // 2, units), HALF),
+            jax.ShapeDtypeStruct((width if n_fsdp != 2 else width // 2, units), HALF),
+            jax.ShapeDtypeStruct((width if n_fsdp != 2 else width // 2, units), HALF),
             jax.ShapeDtypeStruct((units, width), HALF),
             jax.ShapeDtypeStruct((1, width), FLOAT),
         ),
         in_specs=[vmem, hbm, hbm, vmem, hbm, hbm, hbm, hbm],
-        out_specs=[hbm] * 9 + [vmem],
+        out_specs=[hbm] * 10 + [vmem],
         scratch_shapes=[
             pltpu.VMEM((chan, width), HALF),
             pltpu.VMEM((width, units), HALF),
@@ -752,7 +769,11 @@
             pltpu.VMEM((8, width), FLOAT),
             pltpu.VMEM((2, TILE, units), HALF),
             pltpu.VMEM((2, TILE, units), HALF),
-            pltpu.VMEM((2, TILE, units), HALF),
+            pltpu.VMEM((width // 2 // TILE, TILE // 2, units), HALF),
+            pltpu.VMEM((width // 2 // TILE, TILE // 4, units), HALF),
+            pltpu.SemaphoreType.DMA((width // 2 // TILE, 4)),
+            pltpu.SemaphoreType.DMA((width // 2 // TILE, 4)),
+            pltpu.SemaphoreType.DMA((width // TILE,)),
             pltpu.SemaphoreType.DMA((4,)),
             pltpu.SemaphoreType.DMA((2,)),
             pltpu.SemaphoreType.DMA((2,)),
@@ -1051,7 +1072,8 @@
             tile(
                 lambda ref, size=size: ref.at[:size, :depth], compute,
                 lambda at=at: w_down_out.at[at, :depth], lambda at=at: w_down_out.at[at, skip:],
-                (down_tile, down_half, down_quarter), at,
+                (down_tile, down_half, down_quarter),
+                [slice(start // cut, (start + size) // cut) for cut in (1, 2, 4)],
             )
         copies[2].wait()
         flat_proj = grad_proj.reshape(rows, wide)
@@ -1065,7 +1087,7 @@
                 lambda ref: ref, compute,
                 lambda at=at: w_in_out.at[at],
                 lambda k=k: w_in_out.at[k * TILE + skip : (k + 1) * TILE + skip],
-                (in_tile, in_half, in_quarter), k,
+                (in_tile, in_half, in_quarter), (k, k, k),
             )
         copies[3].wait()
         copies[4].wait()
@@ -1079,7 +1101,7 @@
             tile(
                 lambda ref: ref.at[:, :depth], compute,
                 lambda at=at: w_out_out.at[at, :depth], lambda at=at: w_out_out.at[at, skip:],
-                (out_tile, out_half, out_quarter), k,
+                (out_tile, out_half, out_quarter), (k, k, k),
             )
 
     pl.run_scoped(
@@ -1101,7 +1123,7 @@
         def token_store(c):
             at = chunk_rows(c)
             return pltpu.make_async_copy(
-                resid_all.at[at], grad_tokens_out.at[at], store_sem.at[0, c]
+                x_all.at[at], grad_tokens_out.at[at], store_sem.at[0, c]
             )
 
         def output_store(c):
@@ -1148,9 +1170,8 @@
                     gain_total[...] += by_gain[:8] + by_gain[8:]
                     inner = gain[...] * grad
                     mean = jnp.mean(inner * value, -1, keepdims=True)
-                    resid_all[at, :] = (
-                        resid_all[at, :] + rate * inner - value * (rate * rate * rate * mean)
-                    )
+                    result = resid_all[at, :] + rate * inner - value * (rate * rate * rate * mean)
+                    x_all[at, :] = result.astype(HALF)
 
             token_store(c).start()
 
@@ -1208,13 +1229,15 @@
     wide = max(3 * chan, depth)
 
     def tiles(*shape):
-        return [pltpu.VMEM((*shape[:-1], shape[-1] // cut), HALF) for cut in (1, 2, 4)]
+        return [
+            pltpu.VMEM((*shape[:-2], shape[-2] // cut, shape[-1]), HALF) for cut in (1, 2, 4)
+        ]
 
     return pl.pallas_call(
         functools.partial(tail, n_fsdp, n_ctx, n_tp),
         name="tail",
         out_shape=(
-            jax.ShapeDtypeStruct((rows, width), FLOAT),
+            jax.ShapeDtypeStruct((rows, width), HALF),
             jax.ShapeDtypeStruct((rows, width), HALF),
             jax.ShapeDtypeStruct((1, size), FLOAT),
             jax.ShapeDtypeStruct((spread, 3 * chan), HALF),
@@ -1266,6 +1289,52 @@
     )(*small, *large)
 
 
+def widen_outputs(w_in, w_out, w_gate, w_up, w_down, tokens, w_in_out, w_out_out, w_glu_out, w_down_out, tokens_out):
+    chan = w_in_out.shape[2]
+    for gate in range(3):
+        w_in_out[gate] = w_in[:, gate * chan : (gate + 1) * chan].astype(FLOAT)
+    w_out_out[...] = w_out[...].astype(FLOAT)
+    w_glu_out[:, 0, :] = w_gate[...].astype(FLOAT)
+    w_glu_out[:, 1, :] = w_up[...].astype(FLOAT)
+    w_down_out[...] = w_down[...].astype(FLOAT)
+    tokens_out[...] = tokens[...].astype(FLOAT)
+
+
+def run_widen_outputs(w_in, w_out, w_gate, w_up, w_down, tokens):
+    steps = 8
+    arrays = (w_in, w_out, w_gate, w_up, w_down, tokens)
+
+    def spec(array):
+        return pl.BlockSpec((array.shape[0] // steps, array.shape[1]), lambda i: (i, 0))
+
+    depth, wide = w_in.shape
+    chan = wide // 3
+    units = w_gate.shape[1]
+    shapes = [
+        jax.ShapeDtypeStruct((3, depth, chan), FLOAT),
+        jax.ShapeDtypeStruct(w_out.shape, FLOAT),
+        jax.ShapeDtypeStruct((depth, 2, units), FLOAT),
+        jax.ShapeDtypeStruct(w_down.shape, FLOAT),
+        jax.ShapeDtypeStruct(tokens.shape, FLOAT),
+    ]
+    specs = [
+        pl.BlockSpec((3, depth // steps, chan), lambda i: (0, i, 0)),
+        spec(w_out),
+        pl.BlockSpec((depth // steps, 2, units), lambda i: (i, 0, 0)),
+        spec(w_down),
+        spec(tokens),
+    ]
+    return pl.pallas_call(
+        widen_outputs,
+        name="widen_outputs",
+        grid=(steps,),
+        out_shape=shapes,
+        in_specs=[spec(array) for array in arrays],
+        out_specs=specs,
+        compiler_params=pltpu.CompilerParams(vmem_limit_bytes=48 * MIB),
+    )(*arrays)
+
+
 def gather_fsdp(part, dim, count):
     if count != 2:
         return lax.all_gather(part, "fsdp", axis=dim, tiled=True)
@@ -1316,11 +1385,11 @@
     x_half = tokens.reshape(rows, width)
     grad_y_half = cotangent.reshape(rows, width)
     (
-        mixed, _, act, _, grad_resid, grad_mixed, grad_gated, grad_w_glu, w_down_all, grad_gain_two
-    ) = run_middle(gated, x_half, grad_y_half, gain_b, parts, n_fsdp, length)
-    if n_fsdp != 2:
-        grad_w_glu = lax.psum_scatter(grad_w_glu, "fsdp", scatter_dimension=1, tiled=True)
-    grad_w_glu = lax.psum(grad_w_glu, "ctx")
+        mixed, _, act, _, grad_resid, grad_mixed, grad_gated, grad_w_gate, grad_w_up, w_down_all,
+        grad_gain_two,
+    ) = run_middle(gated, x_half, grad_y_half, gain_b, parts, n_fsdp, n_ctx, length)
+    if n_fsdp == 2:
+        grad_w_up = lax.psum(grad_w_up, "ctx")
     grad_tokens, output, vectors, grad_w_in, grad_w_out, grad_w_down = run_tail(
         (keep, gain_gate, low, gate_scale, carry, gain_a, grad_gain_two),
         (
@@ -1329,26 +1398,24 @@
         ),
         n_fsdp, n_ctx, n_tp,
     )
-    if n_fsdp == 2:
-        grad_w_in = jnp.moveaxis(grad_w_in.reshape(width // 2, 3, chan), 1, 0)
-    else:
-        grad_w_in, grad_w_out, grad_w_down = (
+    grads = (grad_w_in, grad_w_out, grad_w_gate, grad_w_up, grad_w_down)
+    if n_fsdp != 2:
+        grads = tuple(
             lax.psum(lax.psum_scatter(value, "fsdp", scatter_dimension=dim, tiled=True), "ctx")
-            for value, dim in (
-                (jnp.moveaxis(grad_w_in.reshape(width, 3, chan), 1, 0), 1),
-                (grad_w_out, 1),
-                (grad_w_down, 1),
-            )
-        )
+            for value, dim in zip(grads, (0, 1, 0, 0, 1))
+        )
+    grad_w_in, grad_w_out, grad_w_glu, grad_w_down, grad_tokens = run_widen_outputs(
+        *grads, grad_tokens
+    )
     part = gain_one.shape[0]
     begin = lax.axis_index("fsdp") * part
     return (
         output.reshape(n_seq, length, width),
         grad_tokens.reshape(n_seq, length, width),
-        grad_w_in.astype(FLOAT),
-        grad_w_out.astype(FLOAT),
-        jnp.moveaxis(grad_w_glu, 0, 1).astype(FLOAT),
-        grad_w_down.astype(FLOAT),
+        grad_w_in,
+        grad_w_out,
+        grad_w_glu,
+        grad_w_down,
         lax.dynamic_slice(vectors[0], (begin,), (part,)),
         lax.dynamic_slice(vectors[0], (width + begin,), (part,)),
         vectors[0, 2 * width : 2 * width + chan],

time: 643 us -> 598 us (0.930)
  local copies, waits for them, and re-layouts: 61 us -> 34.2 us
  Pallas kernels: 510 us -> 499 us
  other arithmetic: 34.2 us -> 25.3 us
    pallas_call x1, Pallas kernels: 271 us -> 239 us  [run_tail(): pl.pallas_call(functools.partial(tail, n_fsdp, n_ctx, n_tp), name='tail',...]
    unnamed x46 -> x37, local copies, waits for them, and re-layouts: 44.7 us -> 19.3 us
    pallas_call x1 -> x2, Pallas kernels: 224 us -> 245 us  [the longest x1 228 us: run_middle(): pl.pallas_call(functools.partial(middle, n_fsdp, n_ctx, length), name='mi...]
  transfers between devices with their start and end apart: 5 -> 5, of which waited for: 0 -> 0; matrix products, arithmetic and copies ran while one was open for 7% -> 5% of each run, Pallas kernels for 43% -> 41%
where the time goes in v5:
time: 598 us; the launch traced here: 589 us
  Pallas kernels  499 us (83%)
  local copies, waits for them, and re-layouts  34.2 us (6%)
  other arithmetic  25.3 us (4%)
  between operations  14.7 us (2%)
  matrix products  10.2 us (2%)
    pallas_call x1, Pallas kernels, run_tail(): pl.pallas_call(functools.partial(tail, n_fsdp, n_ctx, n_tp), name='tail',...  239 us
    pallas_call x1, Pallas kernels, run_middle(): pl.pallas_call(functools.partial(middle, n_fsdp, n_ctx, length), name='mi...  228 us
    unnamed x37, local copies, waits for them, and re-layouts  19.3 us
    pallas_call x1, Pallas kernels, run_widen_outputs(): pl.pallas_call(widen_outputs, name='widen_outputs', grid=(steps,), out_sh...  16.9 us
    pallas_call x1, Pallas kernels, run_scan_forward(): pl.pallas_call(functools.partial(scan_forward, n_ctx, n_tp, width), name=...  15.4 us
  transfers between devices with their start and end apart: 5, of which 0 were waited for; matrix products, arithmetic and copies ran while one was open for 5% of the time, Pallas kernels for 41%

profile of v5, /device:TPU:0, one launch (start us, length us, event | category | flops | bytes accessed | tf_op | source)
XLA Modules:
  0.0 589.4 jit_solution(4105955772787065842)
XLA Ops:
  7.2 0.0 copy-start.12
  7.2 0.0 copy-start.13
  7.2 0.0 copy-start.14
  7.2 0.0 all-reduce.2.cloned.1.call-start
  7.3 4.9 convert_element_type.50
  12.1 0.0 copy-start.11
  12.1 0.5 collective-permute-start.1
  12.6 0.0 copy-done.12
  12.6 0.1 slice_convert_fusion
  12.6 4.5 collective-permute-start
  17.2 0.0 copy-done.13
  17.2 0.1 collective-permute-start.3
  17.4 0.0 copy-done.14
  17.4 0.5 collective-permute-start.2
  17.9 3.1 multiply_reduce_fusion
  21.0 0.0 copy-done.11
  21.0 0.0 slice-start
  21.0 1.2 convert_element_type.59.wo_part
  22.2 0.0 slice-start.1
  22.2 7.9 %copy.32 = bf16[1024,2,1408]{2,0,1:T(8,128)(2,1)} copy(f32[1024,2,1408]{2,1,0:T(2,128)} %param.15) | data formatting | bytes 17301504 | tf_op args[4]
  30.1 0.0 slice-done
  30.1 0.0 slice-done.1
  30.1 2.1 convert_element_type.62.wd_part
  32.1 5.6 slice_bitcast_fusion
  37.7 0.0 collective-permute-done
  37.7 0.1 select_bitcast_fusion
  37.8 0.2 copy.28.keep
  38.0 0.0 copy-start.2
  38.0 0.0 collective-permute-done.3
  38.0 0.0 collective-permute-done.2
  38.1 0.7 maximum_convert_fusion.gain
  38.8 0.6 maximum_convert_fusion.1.gain
  39.4 5.2 multiply_convert_fusion.normed
  44.7 0.0 collective-permute-done.1
  44.7 4.3 broadcast_select_fusion.1
  49.0 3.1 pad_maximum_fusion.w_in
  52.1 10.2 %fusion.2 = f32[3,1024,512]{1,2,0:T(8,128)} fusion(bf16[1024,2048]{1,0:T(8,128)(2,1)} %multiply_convert_fusion.normed, bf16[3,1024,512]{2,1,0:T(8,128)(2,1)S(1)} %get-tuple-element.63, bf16[3,1024,512]{2,1,0:T(8,128)(2,1)S(1)} %get-tuple-element.62), kind=kOutput, calls=%fused_computation.10 | convolution fusion | flops 6455033856 | bytes 16777216 | tf_op jit(solution)/shard_map/td,wdc->wtc/dot_general | solution.py:1379
  62.3 0.0 copy-start.4
  62.3 0.0 copy-start.5
  62.3 6.6 %copy.25 = f32[3,1024,512]{2,1,0:T(8,128)} copy(f32[3,1024,512]{1,2,0:T(8,128)} %fusion.2) | data formatting | bytes 12582912 | tf_op jit(solution)/shard_map/td,wdc->wtc/transpose | solution.py:1379
  68.9 0.0 copy-done.2
  68.9 0.0 copy-done.4
  68.9 0.0 copy-done.5
  68.9 0.0 copy-start
  68.9 2.8 copy-done
  71.7 15.4 %scan_forward.1 = (bf16[4,256,512]{2,1,0:T(8,128)(2,1)S(1)}, f32[4,256,512]{2,1,0:T(8,128)S(1)}, f32[4,256]{1,0:T(4,128)S(1)}, f32[4,512]{1,0:T(4,128)S(1)}) custom-call(f32[3,4,256,512]{3,2,1,0:T(8,128)S(1)} %bitcast.32, f32[4,256,1]{2,1,0:T(8,128)S(1)} %copy.28.keep, f32[1,512]{1,0:T(1,128)S(1)} %bitcast.34, f32[1,512]{1,0:T(1,128)S(1)} %bitcast.36), custom_call_target="tpu_custom_call" | custom-call | tf_op jit(solution)/shard_map/scan_forward/pallas_call | solution.py:140
  87.1 0.0 copy-start.6
  87.1 1.3 copy-done.6
  88.4 0.0 copy-start.7
  88.4 1.0 copy-done.7
  89.4 0.0 copy-start.8
  89.4 0.6 copy-done.8
  90.0 0.0 copy-start.9
  90.0 0.6 copy-done.9
  90.6 227.7 %middle.1 = (bf16[1024,2048]{1,0:T(8,128)(2,1)}, bf16[1024,2048]{1,0:T(8,128)(2,1)}, bf16[1024,1408]{1,0:T(8,128)(2,1)}, bf16[2,1024,1408]{2,1,0:T(8,128)(2,1)},...) custom-call(bf16[1024,512]{1,0:T(8,128)(2,1)} %bitcast.37, ...), custom_call_target="tpu_custom_call" | custom-call | flops 47244640256 | bytes 419430400 | tf_op jit(solution)/shard_map/middle/pallas_call | solution.py:735
  318.3 0.0 all-reduce.2.cloned.1.call-update
  318.4 239.2 %tail.1 = (bf16[1024,2048]{1,0:T(8,128)(2,1)}, bf16[1024,2048]{1,0:T(8,128)(2,1)}, f32[1,5120]{1,0:T(1,128)}, bf16[1024,1536]{1,0:T(8,128)(2,1)}, bf16[512,1024]{1,0:T(8,128)(2,1)}, /*index=5*/bf16[1408,1024]{1,0:T(8,128)(2,1)}) custom-call(f32[4,256,1]{2,1,0:T(8,128)} %copy-done.2, f32[1,512]{1,0:T(1,128)} %bitcast.33, f32[1,512]{1,0:T(1,128)} %bitcast.35, ...), custom_call_target="tpu_custom_call" | custom-call | flops 29527900160 | bytes 734003200 | tf_op jit(solution)/shard_map/tail/pallas_call | solution.py:1236
  557.6 1.3 constant_dynamic-slice_fusion
  558.9 1.3 fusion.7
  560.1 1.8 copy-done.1
  562.0 1.2 copy-done.3
  563.2 16.9 %widen_outputs.1 = (f32[3,1024,512]{2,1,0:T(8,128)}, f32[512,1024]{1,0:T(8,128)}, f32[1024,2,1408]{2,1,0:T(2,128)}, f32[1408,1024]{1,0:T(8,128)}, f32[1024,2048]{1,0:T(8,128)}) custom-call(bf16[1024,1536]{1,0:T(8,128)(2,1)} %get-tuple-element.46.w_in, bf16[512,1024]{1,0:T(8,128)(2,1)S(1)} %copy-done.3, bf16[1024,1408]{1,0:T(8,128)(2,1)S(1)} %copy-done.1, ...), custom_call_target="tpu_custom_call" | custom-call | tf_op jit(solution)/shard_map/widen_outputs/pallas_call | solution.py:1327
  580.1 0.0 copy-done.10
  580.1 2.0 copy.35
  (15 shorter events, 0.1 us)
Async XLA Ops:
  7.2 5.4 copy-start.12
  7.2 10.0 %copy-start.13 = (f32[1024]{0:T(1024)S(1)}, f32[1024]{0:T(1024)}, u32[]{:S(2)}) copy-start(f32[1024]{0:T(1024)} %param.18) | copy-start | bytes 12292
  7.2 10.2 %copy-start.14 = (f32[1024]{0:T(1024)S(1)}, f32[1024]{0:T(1024)}, u32[]{:S(2)}) copy-start(f32[1024]{0:T(1024)} %param.17) | copy-start | bytes 12292
  7.2 552.9 %all-reduce.2.cloned.1.call-start = ((), (), s32[]{:S(2)}) async-start(), calls=%async_computation | async-start | bytes 5767168 | tf_op jit(solution)/shard_map/psum | solution.py:1392
  12.1 8.9 %copy-start.11 = (f32[512,1024]{1,0:T(8,128)S(1)}, f32[512,1024]{1,0:T(8,128)}, u32[]{:S(2)}) copy-start(f32[512,1024]{1,0:T(8,128)} %param.14) | copy-start | bytes 6291460
  12.1 32.6 %collective-permute-start.1 = (bf16[3,1024,512]{2,1,0:T(8,128)(2,1)}, bf16[3,1024,512]{2,1,0:T(8,128)(2,1)}, u32[]{:S(2)}, u32[]{:S(2)}) collective-permute-start(bf16[3,1024,512]{2,1,0:T(8,128)(2,1)} %convert_element_type.50), channel_id=1, source_target_pairs={{0,16},{16,0},{1,17},{17,1},{2,18},{18,2},{3,19},{19,3},{4,20},{20... | collective-permute-start | bytes 9437192 | tf_op jit(solution)/shard_map/ppermute | solution.py:1341
  12.6 25.1 %collective-permute-start = (f32[4,1]{1,0:T(4,128)S(1)}, f32[4,1]{1,0:T(4,128)S(1)}, u32[]{:S(2)}, u32[]{:S(2)}) collective-permute-start(f32[4,1]{1,0:T(4,128)S(1)} %slice_convert_fusion), channel_id=1, source_target_pairs={{0,4},{4,8},{8,12},{1,5},{5,9},{9,13},{2,6},{6,10},{10,14},{3,7},{... | collective-permute-start | bytes 56 | tf_op jit(solution)/shard_map/ppermute | solution.py:1349
  17.2 20.8 %collective-permute-start.3 = (bf16[1,1024]{1,0:T(2,128)(2,1)S(1)}, bf16[1,1024]{1,0:T(2,128)(2,1)S(1)}, u32[]{:S(2)}, u32[]{:S(2)}) collective-permute-start(bf16[1,1024]{1,0:T(2,128)(2,1)S(1)} %broadcast_in_dim.25), channel_id=1, source_target_pairs={{0,16},{16,0},{1,17},{17,1},{2,18},{18,2},{3,19},{19,3},{4,20},{20... | collective-permute-start | bytes 6152 | tf_op jit(solution)/shard_map/ppermute | solution.py:1341
  17.4 20.7 %collective-permute-start.2 = (bf16[1,1024]{1,0:T(2,128)(2,1)S(1)}, bf16[1,1024]{1,0:T(2,128)(2,1)S(1)}, u32[]{:S(2)}, u32[]{:S(2)}) collective-permute-start(bf16[1,1024]{1,0:T(2,128)(2,1)S(1)} %broadcast_in_dim.24), channel_id=1, source_target_pairs={{0,16},{16,0},{1,17},{17,1},{2,18},{18,2},{3,19},{19,3},{4,20},{20... | collective-permute-start | bytes 6152 | tf_op jit(solution)/shard_map/ppermute | solution.py:1341
  21.0 9.1 %slice-start = ((s8[5767168]{0:T(1024)(128)(4,1)}), s8[4194304]{0:T(1024)(128)(4,1)S(1)}, s32[]{:S(2)}) async-start(s8[5767168]{0:T(1024)(128)(4,1)} %bitcast.41), calls=%async_computation.1 | async-start | bytes 8388608
  22.2 7.9 %slice-start.1 = ((s8[5767168]{0:T(1024)(128)(4,1)}), s8[1572864]{0:T(1024)(128)(4,1)S(1)}, s32[]{:S(2)}) async-start(s8[5767168]{0:T(1024)(128)(4,1)} %bitcast.41), calls=%async_computation.2 | async-start | bytes 3145728
  38.0 30.9 %copy-start.2 = (f32[4,256,1]{2,1,0:T(8,128)}, f32[4,256,1]{2,1,0:T(8,128)S(1)}, u32[]{:S(2)}) copy-start(f32[4,256,1]{2,1,0:T(8,128)S(1)} %copy.28.keep) | copy-start | bytes 12292
  62.3 6.6 %copy-start.4 = (f32[512]{0:T(512)S(1)}, f32[512]{0:T(512)}, u32[]{:S(2)}) copy-start(f32[512]{0:T(512)} %param.19) | copy-start | bytes 6148
  62.3 6.6 %copy-start.5 = (f32[512]{0:T(512)S(1)}, f32[512]{0:T(512)}, u32[]{:S(2)}) copy-start(f32[512]{0:T(512)} %param.20) | copy-start | bytes 6148
  68.9 2.8 copy-start
  87.1 1.3 copy-start.6
  88.4 1.0 copy-start.7
  89.4 0.6 copy-start.8
  90.0 0.6 copy-start.9
  560.1 1.8 copy-start.1
  562.0 1.2 copy-start.3
  563.2 16.9 %copy-start.10 = (bf16[1024,2048]{1,0:T(8,128)(2,1)S(1)}, bf16[1024,2048]{1,0:T(8,128)(2,1)}, u32[]{:S(2)}) copy-start(bf16[1024,2048]{1,0:T(8,128)(2,1)} %get-tuple-element.45) | copy-start | bytes 12582916
Sparse Core Ops, SparseCore 0:
  318.5 100.3 all-reduce.1

commit v6 on v5

--- a/solution.py
+++ b/solution.py
@@ -73,95 +73,6 @@
 
 def widen(values, chan):
     return jnp.concatenate([values] * (chan // BLOCK), -1)
-
-
-def scan_forward(
-    n_ctx, n_tp, width,
-    proj, keep, gain, lower,
-    gated, state, scale, carry_out,
-    local, reach, ends, squares, ctx_send, ctx_recv, tp_send, tp_recv,
-):
-    n_seq, length, chan = state.shape
-    greet(others("ctx", n_ctx) + others("tp", n_tp))
-    low = lower[...].reshape(1, 1, chan)
-    row = lax.broadcasted_iota(jnp.int32, (n_seq, GROUP, chan), 1)
-
-    def step(index, carry):
-        prod, total = carry
-        rows = pl.ds(pl.multiple_of(index * GROUP, GROUP), GROUP)
-        inp = proj[0, :, rows, :]
-        decay = low + (1.0 - low) * jax.nn.sigmoid(proj[1, :, rows, :])
-        add = inp * jax.nn.sigmoid(inp) * (1.0 - decay)
-        mult = decay * keep[:, rows, :]
-        for hop in (1, 2, 4):
-            inside = row >= hop
-            add = jnp.where(inside, mult * pltpu.roll(add, hop, 1) + add, add)
-            mult = jnp.where(inside, mult * pltpu.roll(mult, hop, 1), mult)
-        add = add + mult * total
-        mult = mult * prod
-        local[:, rows, :] = add
-        reach[:, rows, :] = mult
-        return mult[:, GROUP - 1 :, :], add[:, GROUP - 1 :, :]
-
-    start = (jnp.ones((n_seq, 1, chan), FLOAT), jnp.zeros((n_seq, 1, chan), FLOAT))
-    prod, total = lax.fori_loop(0, length // GROUP, step, start)
-    here = lax.axis_index("ctx")
-    ends[here, 0] = prod.reshape(n_seq, chan)
-    ends[here, 1] = total.reshape(n_seq, chan)
-    share(ends, "ctx", n_ctx, ctx_send, ctx_recv)
-    carry = jnp.zeros((n_seq, chan), FLOAT)
-    for place in range(n_ctx - 1):
-        carry = jnp.where(place < here, ends[place, 1] + ends[place, 0] * carry, carry)
-    carry_out[...] = carry
-    mine = lax.axis_index("tp")
-    for seq in range(n_seq):
-        for start in range(0, length, BLOCK):
-            rows = slice(start, start + BLOCK)
-            value = local[seq, rows, :] + reach[seq, rows, :] * carry[seq : seq + 1]
-            state[seq, rows, :] = value
-            squares[mine, seq : seq + 1, rows] = lane_sums(value * value)
-    share(squares, "tp", n_tp, tp_send, tp_recv)
-    total = squares[0]
-    for place in range(1, n_tp):
-        total = total + squares[place]
-    rate = lax.rsqrt(total / width + EPS)
-    scale[...] = rate
-    for seq in range(n_seq):
-        for start in range(0, length, BLOCK):
-            rows = slice(start, start + BLOCK)
-            gate = proj[2, seq, rows, :]
-            unit = state[seq, rows, :] * widen(columns(rate[seq : seq + 1, rows]), chan)
-            gated[seq, rows, :] = (unit * gain[...] * (gate * jax.nn.sigmoid(gate))).astype(HALF)
-
-
-def run_scan_forward(proj, keep, gain, lower, n_ctx, n_tp, width):
-    _, n_seq, length, chan = proj.shape
-    vmem = pl.BlockSpec(memory_space=pltpu.VMEM)
-    return pl.pallas_call(
-        functools.partial(scan_forward, n_ctx, n_tp, width),
-        name="scan_forward",
-        out_shape=(
-            jax.ShapeDtypeStruct((n_seq, length, chan), HALF),
-            jax.ShapeDtypeStruct((n_seq, length, chan), FLOAT),
-            jax.ShapeDtypeStruct((n_seq, length), FLOAT),
-            jax.ShapeDtypeStruct((n_seq, chan), FLOAT),
-        ),
-        in_specs=[vmem] * 4,
-        out_specs=[vmem] * 4,
-        scratch_shapes=[
-            pltpu.VMEM((n_seq, length, chan), FLOAT),
-            pltpu.VMEM((n_seq, length, chan), FLOAT),
-            pltpu.VMEM((n_ctx, 2, n_seq, chan), FLOAT),
-            pltpu.VMEM((n_tp, n_seq, length), FLOAT),
-            pltpu.SemaphoreType.DMA((n_ctx,)),
-            pltpu.SemaphoreType.DMA((n_ctx,)),
-            pltpu.SemaphoreType.DMA((n_tp,)),
-            pltpu.SemaphoreType.DMA((n_tp,)),
-        ],
-        compiler_params=pltpu.CompilerParams(
-            collective_id=0, has_side_effects=True, vmem_limit_bytes=40 * MIB
-        ),
-    )(proj, keep, gain, lower)
 
 
 PIECES = 4
@@ -1016,9 +927,7 @@
     )
 
     def back_terms(w_all):
-        for copy in start_loads(
-            [(w_in.at[gate], w_all.at[:, gate * chan : (gate + 1) * chan]) for gate in range(3)]
-        ):
+        for copy in start_loads([(w_in, w_all)]):
             copy.wait()
 
         for c in range(n_chunks):
@@ -1335,25 +1244,224 @@
     )(*arrays)
 
 
-def gather_fsdp(part, dim, count):
-    if count != 2:
-        return lax.all_gather(part, "fsdp", axis=dim, tiled=True)
-    other = lax.ppermute(part, "fsdp", [(0, 1), (1, 0)])
-    first = lax.axis_index("fsdp") == 0
-    return jnp.concatenate(
-        [jnp.where(first, part, other), jnp.where(first, other, part)], dim
-    )
-
-
-def keep_flags(segment_ids, count):
-    last = lax.ppermute(
-        segment_ids[:, -1:].astype(FLOAT), "ctx", [(place, place + 1) for place in range(count - 1)]
-    )
-    seg = segment_ids.astype(FLOAT)
-    before = jnp.concatenate([last, seg[:, :-1]], 1)
-    token = lax.broadcasted_iota(jnp.int32, seg.shape, 1)
-    start = (token == 0) & (lax.axis_index("ctx") == 0)
-    return jnp.where(start, 0.0, (seg == before).astype(FLOAT))
+def head(
+    n_fsdp, n_ctx, n_tp,
+    gains, same, first, last, gate_gain, lower, w_in, tokens,
+    gated, scale, carry_out, keep, gain_one, gain_two, proj_out, state_out, normed_out, w_out,
+    staged, w_all, normed, proj, state, local, reach, ends, squares, gain_slots, edge_slots,
+    load_sem, store_sem, half_send, half_recv, ctx_send, ctx_recv, tp_send, tp_recv,
+    gain_send, gain_recv, edge_send, edge_recv,
+):
+    n_seq, length, chan = state.shape
+    rows = n_seq * length
+    depth = w_in.shape[1]
+    width = w_all.shape[0]
+    greet(others("ctx", n_ctx) + others("tp", n_tp) + others("fsdp", n_fsdp))
+    core = lax.axis_index("fsdp")
+    gate_cols = [slice(gate * chan, (gate + 1) * chan) for gate in range(3)]
+    x_load = pltpu.make_async_copy(tokens, normed, load_sem.at[3])
+    if n_fsdp == 2:
+        w_loads = [
+            pltpu.make_async_copy(w_in.at[gate], staged.at[gate], load_sem.at[gate])
+            for gate in range(3)
+        ]
+    else:
+        w_loads = [
+            pltpu.make_async_copy(w_in.at[gate], w_all.at[:, gate_cols[gate]], load_sem.at[gate])
+            for gate in range(3)
+        ]
+    for load in w_loads + [x_load]:
+        load.start()
+    gain_slots[core] = gains[...].astype(HALF).astype(FLOAT)
+    edge_slots[lax.axis_index("ctx")] = last[...]
+    small = shares(gain_slots, "fsdp", n_fsdp, gain_send, gain_recv)
+    small += shares(edge_slots, "ctx", n_ctx, edge_send, edge_recv)
+    for copy in small:
+        copy.start()
+    halves_sent = []
+    if n_fsdp == 2:
+        own = span(core * depth, depth, depth)
+        for gate in range(3):
+            w_loads[gate].wait()
+
+            def cast(at):
+                to = span(core * depth + at.start, at.size, at.size)
+                w_all[to, gate_cols[gate]] = staged[gate, at, :].astype(HALF)
+
+            row_blocks(depth, 32, cast)
+            place = w_all.at[own, gate_cols[gate]]
+            copy = pltpu.make_async_remote_copy(
+                src_ref=place,
+                dst_ref=place,
+                send_sem=half_send.at[gate],
+                recv_sem=half_recv.at[gate],
+                device_id={"fsdp": 1 - core},
+                device_id_type=MESH,
+            )
+            copy.start()
+            halves_sent.append(copy)
+    for copy in small:
+        copy.wait()
+    part = gains.shape[1]
+    for place in range(n_fsdp):
+        cols = slice(place * part, (place + 1) * part)
+        gain_one[:, cols] = gain_slots[place, :1, :]
+        gain_two[:, cols] = gain_slots[place, 1:2, :]
+    here = lax.axis_index("ctx")
+    keep[...] = same[...]
+    before = edge_slots[0]
+    for place in range(1, n_ctx):
+        before = jnp.where(place == here - 1, edge_slots[place], before)
+    joins = jnp.where((before == first[...]) & (here > 0), 1.0, 0.0)
+    keep[:, :1, :] = joins[:, :1].reshape(n_seq, 1, 1)
+    x_load.wait()
+
+    def norm(at):
+        value = normed[at, :].astype(FLOAT)
+        normed[at, :] = (value * rms_scale(value) * gain_one[...]).astype(HALF)
+
+    row_blocks(rows, 16, norm)
+    normed_store = pltpu.make_async_copy(normed, normed_out, store_sem.at[0])
+    normed_store.start()
+    flat = proj.reshape(3, rows, chan)
+    band = min(rows, WIDE)
+    if n_fsdp == 2:
+        for gate in range(3):
+            @pl.loop(0, rows // band)
+            def _(index):
+                at = span(index * band, band, band)
+                cols = span(core * depth, depth, depth)
+                flat[gate, at, :] = dot(normed[at, cols], w_all[own, gate_cols[gate]])
+
+        for gate in range(3):
+            halves_sent[gate].wait_recv()
+
+            @pl.loop(0, rows // band)
+            def _(index):
+                at = span(index * band, band, band)
+                other = span((1 - core) * depth, depth, depth)
+                flat[gate, at, :] += dot(normed[at, other], w_all[other, gate_cols[gate]])
+    else:
+        for gate in range(3):
+            w_loads[gate].wait()
+
+            @pl.loop(0, rows // band)
+            def _(index):
+                at = span(index * band, band, band)
+                flat[gate, at, :] = dot(normed[at, :], w_all[:, gate_cols[gate]])
+
+    stores = [
+        pltpu.make_async_copy(proj, proj_out, store_sem.at[1]),
+        pltpu.make_async_copy(w_all, w_out, store_sem.at[2]),
+    ]
+    for store in stores:
+        store.start()
+    low = lower[...].reshape(1, 1, chan)
+    row = lax.broadcasted_iota(jnp.int32, (n_seq, GROUP, chan), 1)
+
+    def step(index, carry):
+        prod, total = carry
+        rows = pl.ds(pl.multiple_of(index * GROUP, GROUP), GROUP)
+        inp = proj[0, :, rows, :]
+        decay = low + (1.0 - low) * jax.nn.sigmoid(proj[1, :, rows, :])
+        add = inp * jax.nn.sigmoid(inp) * (1.0 - decay)
+        mult = decay * keep[:, rows, :]
+        for hop in (1, 2, 4):
+            inside = row >= hop
+            add = jnp.where(inside, mult * pltpu.roll(add, hop, 1) + add, add)
+            mult = jnp.where(inside, mult * pltpu.roll(mult, hop, 1), mult)
+        add = add + mult * total
+        mult = mult * prod
+        local[:, rows, :] = add
+        reach[:, rows, :] = mult
+        return mult[:, GROUP - 1 :, :], add[:, GROUP - 1 :, :]
+
+    start = (jnp.ones((n_seq, 1, chan), FLOAT), jnp.zeros((n_seq, 1, chan), FLOAT))
+    prod, total = lax.fori_loop(0, length // GROUP, step, start)
+    ends[here, 0] = prod.reshape(n_seq, chan)
+    ends[here, 1] = total.reshape(n_seq, chan)
+    share(ends, "ctx", n_ctx, ctx_send, ctx_recv)
+    carry = jnp.zeros((n_seq, chan), FLOAT)
+    for place in range(n_ctx - 1):
+        carry = jnp.where(place < here, ends[place, 1] + ends[place, 0] * carry, carry)
+    carry_out[...] = carry
+    mine = lax.axis_index("tp")
+    for seq in range(n_seq):
+        for start in range(0, length, BLOCK):
+            rows = slice(start, start + BLOCK)
+            value = local[seq, rows, :] + reach[seq, rows, :] * carry[seq : seq + 1]
+            state[seq, rows, :] = value
+            squares[mine, seq : seq + 1, rows] = lane_sums(value * value)
+    state_store = pltpu.make_async_copy(state, state_out, store_sem.at[3])
+    state_store.start()
+    share(squares, "tp", n_tp, tp_send, tp_recv)
+    total = squares[0]
+    for place in range(1, n_tp):
+        total = total + squares[place]
+    rate = lax.rsqrt(total / width + EPS)
+    scale[...] = rate
+    for seq in range(n_seq):
+        for start in range(0, length, BLOCK):
+            rows = slice(start, start + BLOCK)
+            gate = proj[2, seq, rows, :]
+            unit = state[seq, rows, :] * widen(columns(rate[seq : seq + 1, rows]), chan)
+            swish = gate * jax.nn.sigmoid(gate)
+            gated[seq, rows, :] = (unit * gate_gain[...] * swish).astype(HALF)
+    for copy in halves_sent:
+        copy.wait_send()
+    for store in stores + [normed_store, state_store]:
+        store.wait()
+
+
+def run_head(gains, same, first, last, gate_gain, lower, w_in, tokens, n_fsdp, n_ctx, n_tp):
+    n_seq, length, _ = same.shape
+    rows, width = tokens.shape
+    chan = w_in.shape[2]
+    shape = (n_seq, length, chan)
+    vmem = pl.BlockSpec(memory_space=pltpu.VMEM)
+    hbm = pl.BlockSpec(memory_space=pl.ANY)
+    staged = w_in.shape if n_fsdp == 2 else (3, 8, BLOCK)
+    dma = pltpu.SemaphoreType.DMA
+    return pl.pallas_call(
+        functools.partial(head, n_fsdp, n_ctx, n_tp),
+        name="head",
+        out_shape=(
+            jax.ShapeDtypeStruct(shape, HALF),
+            jax.ShapeDtypeStruct((n_seq, length), FLOAT),
+            jax.ShapeDtypeStruct((n_seq, chan), FLOAT),
+            jax.ShapeDtypeStruct((n_seq, length, 1), FLOAT),
+            jax.ShapeDtypeStruct((1, width), FLOAT),
+            jax.ShapeDtypeStruct((1, width), FLOAT),
+            jax.ShapeDtypeStruct((3, *shape), FLOAT),
+            jax.ShapeDtypeStruct(shape, FLOAT),
+            jax.ShapeDtypeStruct((rows, width), HALF),
+            jax.ShapeDtypeStruct((width, 3 * chan), HALF),
+        ),
+        in_specs=[vmem] * 6 + [hbm] * 2,
+        out_specs=[vmem] * 6 + [hbm] * 4,
+        scratch_shapes=[
+            pltpu.VMEM(staged, FLOAT),
+            pltpu.VMEM((width, 3 * chan), HALF),
+            pltpu.VMEM((rows, width), HALF),
+            pltpu.VMEM((3, *shape), FLOAT),
+            pltpu.VMEM(shape, FLOAT),
+            pltpu.VMEM(shape, FLOAT),
+            pltpu.VMEM(shape, FLOAT),
+            pltpu.VMEM((n_ctx, 2, n_seq, chan), FLOAT),
+            pltpu.VMEM((n_tp, n_seq, length), FLOAT),
+            pltpu.VMEM((n_fsdp, *gains.shape), FLOAT),
+            pltpu.VMEM((n_ctx, *last.shape), FLOAT),
+            dma((4,)), dma((4,)), dma((3,)), dma((3,)), dma((n_ctx,)), dma((n_ctx,)),
+            dma((n_tp,)), dma((n_tp,)), dma((n_fsdp,)), dma((n_fsdp,)), dma((n_ctx,)), dma((n_ctx,)),
+        ],
+        compiler_params=pltpu.CompilerParams(
+            collective_id=0, has_side_effects=True, vmem_limit_bytes=56 * MIB
+        ),
+    )(gains, same, first, last, gate_gain, lower, w_in, tokens)
+
+
+def gather_fsdp(part, dim):
+    return lax.all_gather(part, "fsdp", axis=dim, tiled=True)
 
 
 def local(
@@ -1364,25 +1472,21 @@
     n_seq, length, width = tokens.shape
     rows = n_seq * length
     chan = w_in.shape[2]
-    gain_a = gather_fsdp(gain_one.astype(HALF)[None], 1, n_fsdp).astype(FLOAT)
-    gain_b = gather_fsdp(gain_two.astype(HALF)[None], 1, n_fsdp).astype(FLOAT)
-    w_in_all = gather_fsdp(w_in.astype(HALF), 1, n_fsdp)
+    x_half = tokens.reshape(rows, width)
     parts = (w_out.astype(HALF), w_glu[:, 0].astype(HALF), w_glu[:, 1].astype(HALF), w_down.astype(HALF))
     if n_fsdp != 2:
-        parts = tuple(gather_fsdp(part, dim, n_fsdp) for part, dim in zip(parts, (1, 0, 0, 1)))
-    keep = keep_flags(segment_ids, n_ctx)[..., None]
+        parts = tuple(gather_fsdp(part, dim) for part, dim in zip(parts, (1, 0, 0, 1)))
+        w_in = gather_fsdp(w_in.astype(HALF), 1)
     gain_gate = gate_gain[None]
     low = lower[None]
-    flat = tokens.reshape(rows, width).astype(FLOAT)
-    scale_one = rms_scale(flat)
-    normed = (flat * scale_one * gain_a).astype(HALF)
-    proj = jnp.einsum("td,wdc->wtc", normed, w_in_all, preferred_element_type=FLOAT)
-    proj = proj.reshape(3, n_seq, length, chan)
-    gated, state, gate_scale, carry = run_scan_forward(
-        proj, keep, gain_gate, low, n_ctx, n_tp, width
+    seg = segment_ids.astype(FLOAT)
+    same = jnp.pad((seg[:, 1:] == seg[:, :-1]).astype(FLOAT), ((0, 0), (1, 0)))[..., None]
+    first, last = (jnp.broadcast_to(seg[:, at], (n_seq, BLOCK)) for at in (slice(0, 1), slice(-1, None)))
+    gated, gate_scale, carry, keep, gain_a, gain_b, proj, state, normed, w_in_all = run_head(
+        jnp.stack([gain_one, gain_two]), same, first, last, gain_gate, low, w_in, x_half,
+        n_fsdp, n_ctx, n_tp,
     )
     gated = gated.reshape(rows, chan)
-    x_half = tokens.reshape(rows, width)
     grad_y_half = cotangent.reshape(rows, width)
     (
         mixed, _, act, _, grad_resid, grad_mixed, grad_gated, grad_w_gate, grad_w_up, w_down_all,

time: 598 us -> 571 us (0.955)
  Pallas kernels: 499 us -> 523 us
  other arithmetic: 25.3 us -> 4.61 us
  local copies, waits for them, and re-layouts: 34.2 us -> 19.8 us
  matrix products: 10.2 us -> 0 us
    pallas_call x1, Pallas kernels: 15.4 us -> 39.2 us  [run_head(): pl.pallas_call(functools.partial(head, n_fsdp, n_ctx, n_tp), name='head',...]
    convert_element_type x9 -> x1, other arithmetic: 11.5 us -> 0.69 us  [local(): seg = segment_ids.astype(FLOAT)]
    dot_general x1 -> x0, matrix products: 10.2 us -> none  [local(): jnp.einsum('td,wdc->wtc', normed, w_in_all, preferred_element_type=FLOAT)]
    unnamed x37 -> x16, local copies, waits for them, and re-layouts: 19.3 us -> 11.4 us
    transpose x1 -> x0, local copies, waits for them, and re-layouts: 6.59 us -> none  [local(): jnp.einsum('td,wdc->wtc', normed, w_in_all, preferred_element_type=FLOAT)]
  transfers between devices with their start and end apart: 5 -> 1, of which waited for: 0 -> 0; matrix products, arithmetic and copies ran while one was open for 5% -> 0% of each run, Pallas kernels for 41% -> 43%
where the time goes in v6:
time: 571 us; the launch traced here: 562 us
  Pallas kernels  523 us (92%)
  local copies, waits for them, and re-layouts  19.8 us (3%)
  between operations  14.5 us (3%)
    pallas_call x1, Pallas kernels, run_tail(): pl.pallas_call(functools.partial(tail, n_fsdp, n_ctx, n_tp), name='tail',...  239 us
    pallas_call x1, Pallas kernels, run_middle(): pl.pallas_call(functools.partial(middle, n_fsdp, n_ctx, length), name='mi...  228 us
    pallas_call x1, Pallas kernels, run_head(): pl.pallas_call(functools.partial(head, n_fsdp, n_ctx, n_tp), name='head',...  39.2 us
    pallas_call x1, Pallas kernels, run_widen_outputs(): pl.pallas_call(widen_outputs, name='widen_outputs', grid=(steps,), out_sh...  16.9 us
  transfers between devices with their start and end apart: 1, of which 0 were waited for; matrix products, arithmetic and copies ran while one was open for 0% of the time, Pallas kernels for 43%

profile of v6, /device:TPU:0, one launch (start us, length us, event | category | flops | bytes accessed | tf_op | source)
XLA Modules:
  0.0 562.4 jit_solution(4869762350075049060)
XLA Ops:
  7.2 0.0 all-reduce.3.cloned.1.call-start
  7.2 0.7 convert_element_type.18
  7.9 0.2 slice_reduce_fusion
  8.1 0.1 slice_compare_fusion
  8.2 0.1 convert_bitcast_fusion
  8.3 1.0 copy.22.same
  9.3 4.9 copy.25
  14.2 0.0 copy-start.2
  14.2 3.4 slice_bitcast_fusion
  17.6 1.3 copy-done.2
  18.9 0.0 copy-start.4
  18.9 0.0 copy-start.5
  18.9 0.0 copy-start.6
  18.9 2.0 convert_element_type.22.wd_part
  21.0 0.0 copy-done.4
  21.0 1.1 convert_element_type.19.wo_part
  22.1 0.0 copy-done.5
  22.1 0.0 copy-done.6
  22.1 0.6 pad_maximum_fusion.gains
  22.7 0.6 broadcast_in_dim.28.first
  23.4 0.6 broadcast_in_dim.30.last
  24.0 39.2 %head.1 = (bf16[4,256,512]{2,1,0:T(8,128)(2,1)}, f32[4,256]{1,0:T(4,128)}, f32[4,512]{1,0:T(4,128)}, f32[4,256,1]{2,1,0:T(8,128)}, f32[1,2048]{1,0:T(1,128)}, /*...) custom-call(f32[2,1024]{1,0:T(2,128)} %pad_maximum_fusion.gains, ...), custom_call_target="tpu_custom_call" | custom-call | tf_op jit(solution)/shard_map/head/pallas_call | solution.py:1425
  63.2 228.1 %middle.1 = (bf16[1024,2048]{1,0:T(8,128)(2,1)}, bf16[1024,2048]{1,0:T(8,128)(2,1)}, bf16[1024,1408]{1,0:T(8,128)(2,1)}, bf16[2,1024,1408]{2,1,0:T(8,128)(2,1)},...) custom-call(bf16[1024,512]{1,0:T(8,128)(2,1)} %bitcast.37, ...), custom_call_target="tpu_custom_call" | custom-call | flops 47244640256 | bytes 419430400 | tf_op jit(solution)/shard_map/middle/pallas_call | solution.py:646
  291.4 0.0 all-reduce.3.cloned.1.call-update
  291.4 239.2 %tail.1 = (bf16[1024,2048]{1,0:T(8,128)(2,1)}, bf16[1024,2048]{1,0:T(8,128)(2,1)}, f32[1,5120]{1,0:T(1,128)}, bf16[1024,1536]{1,0:T(8,128)(2,1)}, bf16[512,1024]{1,0:T(8,128)(2,1)}, /*index=5*/bf16[1408,1024]{1,0:T(8,128)(2,1)}) custom-call(f32[4,256,1]{2,1,0:T(8,128)} %get-tuple-element.40.keep, f32[1,512]{1,0:T(1,128)} %bitcast.31, f32[1,512]{1,0:T(1,128)} %bitcast.33, ...), custom_call_target="tpu_custom_call" | custom-call | flops 29527900160 | bytes 734003200 | tf_op jit(solution)/shard_map/tail/pallas_call | solution.py:1145
  530.6 1.3 constant_dynamic-slice_fusion
  531.9 1.3 fusion
  533.2 0.0 all-reduce.3.cloned.1.call-done.w_up
  533.2 0.0 copy-start
  533.2 1.8 copy-done
  535.0 0.0 copy-start.1
  535.0 1.2 copy-done.1
  536.2 0.0 copy-start.3
  536.2 16.9 %widen_outputs.1 = (f32[3,1024,512]{2,1,0:T(8,128)}, f32[512,1024]{1,0:T(8,128)}, f32[1024,2,1408]{2,1,0:T(2,128)}, f32[1408,1024]{1,0:T(8,128)}, f32[1024,2048]{1,0:T(8,128)}) custom-call(bf16[1024,1536]{1,0:T(8,128)(2,1)} %get-tuple-element.58.w_in, bf16[512,1024]{1,0:T(8,128)(2,1)S(1)} %copy-done.1, bf16[1024,1408]{1,0:T(8,128)(2,1)S(1)} %copy-done, ...), custom_call_target="tpu_custom_call" | custom-call | tf_op jit(solution)/shard_map/widen_outputs/pallas_call | solution.py:1236
  553.1 0.0 copy-done.3
  553.1 2.0 copy.28
Async XLA Ops:
  7.2 526.0 %all-reduce.3.cloned.1.call-start = ((), (), s32[]{:S(2)}) async-start(), calls=%async_computation | async-start | bytes 5767168 | tf_op jit(solution)/shard_map/psum | solution.py:1496
  14.2 4.7 copy-start.2
  18.9 2.0 copy-start.4
  18.9 3.2 copy-start.5
  18.9 3.2 copy-start.6
  533.2 1.8 copy-start
  535.0 1.2 copy-start.1
  536.2 16.9 %copy-start.3 = (bf16[1024,2048]{1,0:T(8,128)(2,1)S(1)}, bf16[1024,2048]{1,0:T(8,128)(2,1)}, u32[]{:S(2)}) copy-start(bf16[1024,2048]{1,0:T(8,128)(2,1)} %get-tuple-element.57) | copy-start | bytes 12582916
Sparse Core Ops, SparseCore 0:
  291.5 99.7 all-reduce.2

commit v7 on v6

--- a/solution.py
+++ b/solution.py
@@ -564,12 +564,12 @@
 
     def pump():
         for square in squares:
-            if square[1] < 5 and turn[0] >= square[2] + 2 * square[1]:
+            if square[1] < 5 and turn[0] >= square[2] + 3 * square[1]:
                 square[0].advance(square[1])
                 square[1] += 1
         turn[0] += 1
 
-    def backward(c):
+    def backward(c, between):
         line.arrive(n_chunks + c)
         if c > 0:
             for store in stores(c - 1, BACKWARD):
@@ -589,6 +589,7 @@
             grad_mixed[rows, :] = value.astype(HALF)
 
         row_blocks(CHUNK, 16, norm_back)
+        between()
         for start, size in bands(grad_gated.shape[1], WIDE):
             grad_gated[:, start : start + size] = dot_nt(
                 grad_mixed[...], wo[start : start + size, :]
@@ -604,16 +605,23 @@
             while count < 2 * per_part:
                 weight_item(count)
                 count += 1
-        backward(c)
-        if c + 1 < n_chunks:
-            for step in range(PIECES + 1):
-                weight_item(count)
-                count += 1
-                if c + 2 == n_chunks and step == PIECES - 1:
-                    line.close(2 * n_chunks - 1, step - 1)
-                else:
-                    line.tick(n_chunks + c + 1, step)
-                pump()
+        if c + 1 == n_chunks:
+            backward(c, lambda: None)
+            continue
+
+        def between():
+            line.tick(n_chunks + c + 1, 0)
+            pump()
+
+        backward(c, between)
+        for step in range(1, PIECES + 1):
+            weight_item(count)
+            count += 1
+            if c + 2 == n_chunks and step == PIECES - 1:
+                line.close(2 * n_chunks - 1, step - 1)
+            else:
+                line.tick(n_chunks + c + 1, step)
+            pump()
     while any(square[1] < 5 for square in squares):
         pump()
     finish()
@@ -771,8 +779,10 @@
         return mult[:, :1, :], add[:, :1, :]
 
     held = (jnp.ones((n_seq, 1, chan), FLOAT), jnp.zeros((n_seq, 1, chan), FLOAT))
-    held = lax.fori_loop(0, length // GROUP, back, held)
-    prod, total = held
+    middle_of = length // GROUP // 2
+    held = lax.fori_loop(0, middle_of, back, held)
+    pump()
+    prod, total = lax.fori_loop(middle_of, length // GROUP, back, held)
     here = lax.axis_index("ctx")
     ends[here, 0] = prod.reshape(n_seq, chan)
     ends[here, 1] = total.reshape(n_seq, chan)
@@ -807,7 +817,10 @@
         return value[:, wide - 1 :, :], low_total + grad_decay * rest
 
     held = (carry_in[...].reshape(n_seq, 1, chan), jnp.zeros((n_seq, wide, chan), FLOAT))
-    _, low_total = lax.fori_loop(0, length // wide, finish, held)
+    middle_of = length // wide // 2
+    held = lax.fori_loop(0, middle_of, finish, held)
+    pump()
+    _, low_total = lax.fori_loop(middle_of, length // wide, finish, held)
     lower_out[...] = jnp.sum(jnp.sum(low_total, 0), 0, keepdims=True)
     pump()
 
@@ -842,7 +855,7 @@
         relay += [(line.forward, ahead) for ahead in pieces[index + 2 : index + 3]]
     squares = []
     turn = [0]
-    SPACE = 3
+    SPACE = 4
 
     def pump():
         while relay:
@@ -1198,7 +1211,10 @@
     )(*small, *large)
 
 
-def widen_outputs(w_in, w_out, w_gate, w_up, w_down, tokens, w_in_out, w_out_out, w_glu_out, w_down_out, tokens_out):
+def widen_outputs(
+    w_in, w_out, w_gate, w_up, w_down, tokens, vectors,
+    w_in_out, w_out_out, w_glu_out, w_down_out, tokens_out, one_out, two_out, gate_out, lower_out,
+):
     chan = w_in_out.shape[2]
     for gate in range(3):
         w_in_out[gate] = w_in[:, gate * chan : (gate + 1) * chan].astype(FLOAT)
@@ -1208,8 +1224,18 @@
     w_down_out[...] = w_down[...].astype(FLOAT)
     tokens_out[...] = tokens[...].astype(FLOAT)
 
-
-def run_widen_outputs(w_in, w_out, w_gate, w_up, w_down, tokens):
+    @pl.when(pl.program_id(0) == 0)
+    def _():
+        part = one_out.shape[1]
+        width = (vectors.shape[1] - 2 * chan) // 2
+        begin = lax.axis_index("fsdp") * part
+        one_out[...] = vectors[:, span(begin, part, part)]
+        two_out[...] = vectors[:, span(width + begin, part, part)]
+        gate_out[...] = vectors[:, 2 * width : 2 * width + chan]
+        lower_out[...] = vectors[:, 2 * width + chan :]
+
+
+def run_widen_outputs(w_in, w_out, w_gate, w_up, w_down, tokens, vectors):
     steps = 8
     arrays = (w_in, w_out, w_gate, w_up, w_down, tokens)
 
@@ -1219,6 +1245,8 @@
     depth, wide = w_in.shape
     chan = wide // 3
     units = w_gate.shape[1]
+    whole = pl.BlockSpec(vectors.shape, lambda i: (0, 0))
+    thin = [jax.ShapeDtypeStruct((1, size), FLOAT) for size in (depth, depth, chan, chan)]
     shapes = [
         jax.ShapeDtypeStruct((3, depth, chan), FLOAT),
         jax.ShapeDtypeStruct(w_out.shape, FLOAT),
@@ -1226,22 +1254,23 @@
         jax.ShapeDtypeStruct(w_down.shape, FLOAT),
         jax.ShapeDtypeStruct(tokens.shape, FLOAT),
     ]
+    in_specs = [spec(array) for array in arrays] + [whole]
     specs = [
         pl.BlockSpec((3, depth // steps, chan), lambda i: (0, i, 0)),
         spec(w_out),
         pl.BlockSpec((depth // steps, 2, units), lambda i: (i, 0, 0)),
         spec(w_down),
         spec(tokens),
-    ]
+    ] + [pl.BlockSpec(shape.shape, lambda i: (0, 0)) for shape in thin]
     return pl.pallas_call(
         widen_outputs,
         name="widen_outputs",
         grid=(steps,),
-        out_shape=shapes,
-        in_specs=[spec(array) for array in arrays],
+        out_shape=shapes + thin,
+        in_specs=in_specs,
         out_specs=specs,
-        compiler_params=pltpu.CompilerParams(vmem_limit_bytes=48 * MIB),
-    )(*arrays)
+        compiler_params=pltpu.CompilerParams(vmem_limit_bytes=62 * MIB),
+    )(*arrays, vectors)
 
 
 def head(
@@ -1324,7 +1353,7 @@
     normed_store = pltpu.make_async_copy(normed, normed_out, store_sem.at[0])
     normed_store.start()
     flat = proj.reshape(3, rows, chan)
-    band = min(rows, WIDE)
+    band = rows
     if n_fsdp == 2:
         for gate in range(3):
             @pl.loop(0, rows // band)
@@ -1455,7 +1484,7 @@
             dma((n_tp,)), dma((n_tp,)), dma((n_fsdp,)), dma((n_fsdp,)), dma((n_ctx,)), dma((n_ctx,)),
         ],
         compiler_params=pltpu.CompilerParams(
-            collective_id=0, has_side_effects=True, vmem_limit_bytes=56 * MIB
+            collective_id=0, has_side_effects=True, vmem_limit_bytes=63 * MIB
         ),
     )(gains, same, first, last, gate_gain, lower, w_in, tokens)
 
@@ -1508,11 +1537,8 @@
             lax.psum(lax.psum_scatter(value, "fsdp", scatter_dimension=dim, tiled=True), "ctx")
             for value, dim in zip(grads, (0, 1, 0, 0, 1))
         )
-    grad_w_in, grad_w_out, grad_w_glu, grad_w_down, grad_tokens = run_widen_outputs(
-        *grads, grad_tokens
-    )
-    part = gain_one.shape[0]
-    begin = lax.axis_index("fsdp") * part
+    results = run_widen_outputs(*grads, grad_tokens, vectors)
+    grad_w_in, grad_w_out, grad_w_glu, grad_w_down, grad_tokens = results[:5]
     return (
         output.reshape(n_seq, length, width),
         grad_tokens.reshape(n_seq, length, width),
@@ -1520,10 +1546,7 @@
         grad_w_out,
         grad_w_glu,
         grad_w_down,
-        lax.dynamic_slice(vectors[0], (begin,), (part,)),
-        lax.dynamic_slice(vectors[0], (width + begin,), (part,)),
-        vectors[0, 2 * width : 2 * width + chan],
-        vectors[0, 2 * width + chan :],
+        *(vector[0] for vector in results[5:]),
     )
 
 

time: 571 us -> 543 us (0.951)
  Pallas kernels: 523 us -> 498 us
    pallas_call x1, Pallas kernels: 239 us -> 224 us  [run_tail(): pl.pallas_call(functools.partial(tail, n_fsdp, n_ctx, n_tp), name='tail',...]
    pallas_call x1, Pallas kernels: 228 us -> 218 us  [run_middle(): pl.pallas_call(functools.partial(middle, n_fsdp, n_ctx, length), name='mi...]
  transfers between devices with their start and end apart: 1 -> 1, of which waited for: 0 -> 0; matrix products, arithmetic and copies ran while one was open for 0% -> 0% of each run, Pallas kernels for 43% -> 42%
where the time goes in v7:
time: 543 us; the launch traced here: 537 us
  Pallas kernels  498 us (92%)
  local copies, waits for them, and re-layouts  15.2 us (3%)
  between operations  14.5 us (3%)
  other arithmetic  8.84 us (2%)
    pallas_call x1, Pallas kernels, run_tail(): pl.pallas_call(functools.partial(tail, n_fsdp, n_ctx, n_tp), name='tail',...  224 us
    pallas_call x1, Pallas kernels, run_middle(): pl.pallas_call(functools.partial(middle, n_fsdp, n_ctx, length), name='mi...  218 us
    pallas_call x1, Pallas kernels, run_head(): pl.pallas_call(functools.partial(head, n_fsdp, n_ctx, n_tp), name='head',...  37.9 us
    pallas_call x1, Pallas kernels, run_widen_outputs(): pl.pallas_call(widen_outputs, name='widen_outputs', grid=(steps,), out_sh...  19 us
  transfers between devices with their start and end apart: 1, of which 0 were waited for; matrix products, arithmetic and copies ran while one was open for 0% of the time, Pallas kernels for 42%

profile of v7, /device:TPU:0, one launch (start us, length us, event | category | flops | bytes accessed | tf_op | source)
XLA Modules:
  0.0 536.8 jit_solution(14951274086456347586)
XLA Ops:
  7.2 0.0 all-reduce.3.cloned.1.call-start
  7.2 0.7 convert_element_type.18
  7.9 0.1 slice_compare_fusion
  8.0 0.2 slice_reduce_fusion
  8.2 0.1 convert_bitcast_fusion
  8.2 1.0 copy.22.same
  9.3 2.7 convert_element_type.19.wo_part
  12.0 4.7 convert_element_type.22.wd_part
  16.7 4.9 copy.25
  21.6 0.0 copy-start
  21.6 0.0 copy-start.1
  21.6 3.0 slice_bitcast_fusion
  24.6 0.0 copy-done
  24.6 0.0 copy-done.1
  24.6 0.6 pad_maximum_fusion.gains
  25.2 0.6 broadcast_in_dim.30.last
  25.8 0.6 broadcast_in_dim.28.first
  26.5 37.9 %head.1 = (bf16[4,256,512]{2,1,0:T(8,128)(2,1)}, f32[4,256]{1,0:T(4,128)}, f32[4,512]{1,0:T(4,128)}, f32[4,256,1]{2,1,0:T(8,128)}, f32[1,2048]{1,0:T(1,128)}, /*...) custom-call(f32[2,1024]{1,0:T(2,128)} %pad_maximum_fusion.gains, ...), custom_call_target="tpu_custom_call" | custom-call | tf_op jit(solution)/shard_map/head/pallas_call | solution.py:1454
  64.4 217.6 %middle.1 = (bf16[1024,2048]{1,0:T(8,128)(2,1)}, bf16[1024,2048]{1,0:T(8,128)(2,1)}, bf16[1024,1408]{1,0:T(8,128)(2,1)}, bf16[2,1024,1408]{2,1,0:T(8,128)(2,1)},...) custom-call(bf16[1024,512]{1,0:T(8,128)(2,1)} %bitcast.33, ...), custom_call_target="tpu_custom_call" | custom-call | flops 47244640256 | bytes 419430400 | tf_op jit(solution)/shard_map/middle/pallas_call | solution.py:654
  282.0 0.0 all-reduce.3.cloned.1.call-update
  282.0 223.7 %tail.1 = (bf16[1024,2048]{1,0:T(8,128)(2,1)}, bf16[1024,2048]{1,0:T(8,128)(2,1)}, f32[1,5120]{1,0:T(1,128)}, bf16[1024,1536]{1,0:T(8,128)(2,1)}, bf16[512,1024]{1,0:T(8,128)(2,1)}, /*index=5*/bf16[1408,1024]{1,0:T(8,128)(2,1)}) custom-call(f32[4,256,1]{2,1,0:T(8,128)} %get-tuple-element.44.keep, f32[1,512]{1,0:T(1,128)} %bitcast.27, f32[1,512]{1,0:T(1,128)} %bitcast.29, ...), custom_call_target="tpu_custom_call" | custom-call | flops 29527900160 | bytes 734003200 | tf_op jit(solution)/shard_map/tail/pallas_call | solution.py:1158
  505.7 0.0 all-reduce.3.cloned.1.call-done.w_up
  505.7 19.0 %widen_outputs.1 = (f32[3,1024,512]{2,1,0:T(8,128)}, f32[512,1024]{1,0:T(8,128)}, f32[1024,2,1408]{2,1,0:T(2,128)}, f32[1408,1024]{1,0:T(8,128)}, f32[1024,2048]...) custom-call(bf16[1024,1536]{1,0:T(8,128)(2,1)} %get-tuple-element.62.w_in, ...), custom_call_target="tpu_custom_call" | custom-call | tf_op jit(solution)/shard_map/widen_outputs/pallas_call | solution.py:1265
  524.7 4.8 copy.28
Async XLA Ops:
  7.2 498.6 %all-reduce.3.cloned.1.call-start = ((), (), s32[]{:S(2)}) async-start(), calls=%async_computation | async-start | bytes 5767168 | tf_op jit(solution)/shard_map/psum | solution.py:1525
  21.6 3.0 copy-start
  21.6 3.0 copy-start.1
Sparse Core Ops, SparseCore 0:
  282.1 100.2 all-reduce.2

commit v8 on v7

--- a/solution.py
+++ b/solution.py
@@ -193,43 +193,6 @@
             @pl.loop(0, PIECES)
             def _(q):
                 self.outward(job, q).wait_send()
-
-
-def pull(parts, wholes, dims, n_fsdp, own_sem, send_sem, recv_sem):
-    if n_fsdp != 2:
-        copies = [
-            pltpu.make_async_copy(part, whole, own_sem.at[index])
-            for index, (part, whole) in enumerate(zip(parts, wholes))
-        ]
-        for copy in copies:
-            copy.start()
-        return lambda index: copies[index].wait()
-    mine = lax.axis_index("fsdp")
-    near, far = [], []
-    for index, (part, whole, dim) in enumerate(zip(parts, wholes, dims)):
-        size = part.shape[dim]
-        at = pl.ds(pl.multiple_of(mine * size, size), size)
-        place = whole.at[at] if dim == 0 else whole.at[:, at]
-        near.append(pltpu.make_async_copy(part, place, own_sem.at[index]))
-        far.append(
-            pltpu.make_async_remote_copy(
-                src_ref=part,
-                dst_ref=place,
-                send_sem=send_sem.at[index],
-                recv_sem=recv_sem.at[index],
-                device_id={"fsdp": 1 - mine},
-                device_id_type=MESH,
-            )
-        )
-    for one, two in zip(near, far):
-        two.start()
-        one.start()
-
-    def wait(index):
-        near[index].wait()
-        far[index].wait()
-
-    return wait
 
 
 def span(start, size, unit):
@@ -392,7 +355,9 @@
     grad_gated_out, w_gate_out, w_up_out, w_down_out, grad_gain_out,
     wo, wg, wu, wd, x_all, dy_all, held, crossed, total, normed, act, grad_glu,
     grad_resid, grad_mixed, grad_gated, gain_total, spare, inbox, half, quarter,
-    square_send, square_recv, square_store, weight_sem, weight_send, weight_recv, again_sem, own_sem, send_sem, recv_sem, load_sem, store_sem, *line_sems,
+    square_send, square_recv, square_store, weight_sem, weight_send, weight_recv, again_sem,
+    own_sem, stage_sem, glu_send, glu_recv, down_send, down_recv,
+    load_sem, store_sem, *line_sems,
 ):
     n_chunks, _, _, piece = held.shape
     units = wd.shape[0]
@@ -401,10 +366,69 @@
     if n_fsdp == 2:
         peers.append({"fsdp": 1 - lax.axis_index("fsdp")})
     greet(peers)
-    ready = pull(
-        (wo_part, wg_part, wu_part, wd_part), (wo, wg, wu, wd), (1, 0, 0, 1),
-        n_fsdp, own_sem, send_sem, recv_sem,
-    )
+    local_parts = [(wo_part, wo)]
+    if n_fsdp != 2:
+        local_parts += [(wg_part, wg), (wu_part, wu), (wd_part, wd)]
+    ready = [
+        pltpu.make_async_copy(part, whole, own_sem.at[index])
+        for index, (part, whole) in enumerate(local_parts)
+    ]
+    for copy in ready:
+        copy.start()
+    core = lax.axis_index("fsdp")
+    n_bands = units // BLOCK
+
+    def to_sibling(place, send, recv):
+        return pltpu.make_async_remote_copy(
+            src_ref=place,
+            dst_ref=place,
+            send_sem=send,
+            recv_sem=recv,
+            device_id={"fsdp": 1 - core},
+            device_id_type=MESH,
+        )
+
+    def glu_copies(number):
+        part, whole = ((wg_part, wg), (wu_part, wu))[number]
+        at = span(core * (width // 2), width // 2, width // 2)
+        far = pltpu.make_async_remote_copy(
+            src_ref=part,
+            dst_ref=whole.at[at],
+            send_sem=glu_send.at[number],
+            recv_sem=glu_recv.at[number],
+            device_id={"fsdp": 1 - core},
+            device_id_type=MESH,
+        )
+        return far, pltpu.make_async_copy(part, whole.at[at], own_sem.at[1 + number])
+
+    def down_stage(index):
+        return grad_resid.at[span(lax.rem(index, 2) * BLOCK, BLOCK, BLOCK), : width // 2]
+
+    def down_load(index):
+        return pltpu.make_async_copy(
+            wd_part.at[span(index * BLOCK, BLOCK, BLOCK)], down_stage(index),
+            stage_sem.at[lax.rem(index, 2)],
+        )
+
+    def down_copy(index):
+        cols = span(core * (width // 2), width // 2, width // 2)
+        place = wd.at[span(index * BLOCK, BLOCK, BLOCK), cols]
+        return to_sibling(place, down_send.at[index], down_recv.at[index])
+
+    def down_band(index):
+        down_load(index).wait()
+        cols = span(core * (width // 2), width // 2, width // 2)
+        wd[span(index * BLOCK, BLOCK, BLOCK), cols] = down_stage(index)[...].astype(HALF)
+
+        @pl.when(index + 2 < n_bands)
+        def _():
+            down_load(index + 2).start()
+
+        down_copy(index).start()
+
+    if n_fsdp == 2:
+        for first_load in (*glu_copies(0), *glu_copies(1), down_load(0), down_load(1)):
+            first_load.start()
     loads = [
         pltpu.make_async_copy(tokens, x_all, load_sem.at[0]),
         pltpu.make_async_copy(cotangent, dy_all, load_sem.at[1]),
@@ -439,7 +463,7 @@
     FORWARD = (0, 1, 2, 3, 7, 8, 9, 10)
     BACKWARD = (4, 5, 6)
 
-    ready(0)
+    ready[0].wait()
 
     @pl.loop(0, n_chunks)
     def _(c):
@@ -453,13 +477,31 @@
 
     for load in loads:
         load.wait()
-    line.forward(0, 0)
-    for step in range(PIECES + 1):
-        line.tick(0, step)
-    for index in (1, 2, 3):
-        ready(index)
+    def cast_down(part):
+        pl.loop(part * n_bands // 4, (part + 1) * n_bands // 4)(down_band)
+
+    for step in range(PIECES + 2):
+        if n_fsdp == 2 and step < 4:
+            cast_down(step)
+        if step == 0:
+            line.forward(0, 0)
+        else:
+            line.tick(0, step - 1)
+
     w_down_store = pltpu.make_async_copy(wd, w_down_out, again_sem.at[3])
-    w_down_store.start()
+
+    def weights_here():
+        for copy in ready[1:]:
+            copy.wait()
+        if n_fsdp == 2:
+            for copy in (*glu_copies(0), *glu_copies(1)):
+                copy.wait()
+
+            @pl.loop(0, n_bands)
+            def _(index):
+                down_copy(index).wait()
+
+        w_down_store.start()
 
     @pl.loop(0, n_chunks)
     def _(c):
@@ -477,6 +519,7 @@
             normed[rows, :] = (resid * rms_scale(resid) * gain[...]).astype(HALF)
 
         row_blocks(CHUNK, 16, norm)
+        pl.when(c == 0)(weights_here)
 
         def unit(cols):
             glu_gate = dot(normed[...], wg[:, cols])
@@ -644,8 +687,7 @@
 def run_middle(gated, tokens, cotangent, gain, parts, n_fsdp, n_ctx, length):
     rows, chan = gated.shape
     width = tokens.shape[1]
-    wg = parts[1]
-    units = wg.shape[1]
+    units = parts[3].shape[0]
     n_chunks = rows // length
     piece = width // PIECES
     vmem = pl.BlockSpec(memory_space=pltpu.VMEM)
@@ -698,8 +740,11 @@
             pltpu.SemaphoreType.DMA((2,)),
             pltpu.SemaphoreType.DMA((4,)),
             pltpu.SemaphoreType.DMA((4,)),
-            pltpu.SemaphoreType.DMA((4,)),
-            pltpu.SemaphoreType.DMA((4,)),
+            pltpu.SemaphoreType.DMA((2,)),
+            pltpu.SemaphoreType.DMA((2,)),
+            pltpu.SemaphoreType.DMA((2,)),
+            pltpu.SemaphoreType.DMA((units // BLOCK,)),
+            pltpu.SemaphoreType.DMA((units // BLOCK,)),
             pltpu.SemaphoreType.DMA((2,)),
             pltpu.SemaphoreType.DMA((12,)),
         ]
@@ -896,18 +941,22 @@
             gain_at = over_ctx.at[lax.axis_index("ctx"), :, 2 * width : 2 * width + chan]
             scan_cross(gate_all, state_all, scale, gate_gain, near, grad_proj, gain_at, cross)
 
-        pl.run_scoped(cross_terms, pltpu.VMEM(shape, FLOAT), pltpu.VMEM(shape, FLOAT))
-        for copy in crossing:
-            copy.start()
-        for copy in copies:
-            copy.wait()
-
-        for c in range(n_chunks):
-            @pl.loop(0, PIECES)
+        def down_term(c, first, stop):
+            @pl.loop(first, stop)
             def _(q):
                 cols = pl.ds(pl.multiple_of(q * piece, piece), piece)
                 held[c, q] = dot(act_all[chunk_rows(c), :], w_all[:, cols]).astype(HALF)
                 line.offer(c, q)
+
+        for copy in copies:
+            copy.wait()
+        down_term(0, 0, 2)
+        pl.run_scoped(cross_terms, pltpu.VMEM(shape, FLOAT), pltpu.VMEM(shape, FLOAT))
+        for copy in crossing:
+            copy.start()
+
+        for c in range(n_chunks):
+            down_term(c, 0 if c else 2, PIECES)
 
             if c >= n_chunks // 2:
                 pump()
@@ -1212,8 +1261,8 @@
 
 
 def widen_outputs(
-    w_in, w_out, w_gate, w_up, w_down, tokens, vectors,
-    w_in_out, w_out_out, w_glu_out, w_down_out, tokens_out, one_out, two_out, gate_out, lower_out,
+    w_in, w_out, w_gate, w_up, w_down, tokens, output, vectors,
+    w_in_out, w_out_out, w_glu_out, w_down_out, tokens_out, output_out, one_out, two_out, gate_out, lower_out,
 ):
     chan = w_in_out.shape[2]
     for gate in range(3):
@@ -1223,6 +1272,7 @@
     w_glu_out[:, 1, :] = w_up[...].astype(FLOAT)
     w_down_out[...] = w_down[...].astype(FLOAT)
     tokens_out[...] = tokens[...].astype(FLOAT)
+    output_out[...] = output[...]
 
     @pl.when(pl.program_id(0) == 0)
     def _():
@@ -1235,9 +1285,9 @@
         lower_out[...] = vectors[:, 2 * width + chan :]
 
 
-def run_widen_outputs(w_in, w_out, w_gate, w_up, w_down, tokens, vectors):
+def run_widen_outputs(w_in, w_out, w_gate, w_up, w_down, tokens, output, vectors):
     steps = 8
-    arrays = (w_in, w_out, w_gate, w_up, w_down, tokens)
+    arrays = (w_in, w_out, w_gate, w_up, w_down, tokens, output)
 
     def spec(array):
         return pl.BlockSpec((array.shape[0] // steps, array.shape[1]), lambda i: (i, 0))
@@ -1253,6 +1303,7 @@
         jax.ShapeDtypeStruct((depth, 2, units), FLOAT),
         jax.ShapeDtypeStruct(w_down.shape, FLOAT),
         jax.ShapeDtypeStruct(tokens.shape, FLOAT),
+        jax.ShapeDtypeStruct(output.shape, HALF),
     ]
     in_specs = [spec(array) for array in arrays] + [whole]
     specs = [
@@ -1261,6 +1312,7 @@
         pl.BlockSpec((depth // steps, 2, units), lambda i: (i, 0, 0)),
         spec(w_down),
         spec(tokens),
+        spec(output),
     ] + [pl.BlockSpec(shape.shape, lambda i: (0, 0)) for shape in thin]
     return pl.pallas_call(
         widen_outputs,
@@ -1275,9 +1327,9 @@
 
 def head(
     n_fsdp, n_ctx, n_tp,
-    gains, same, first, last, gate_gain, lower, w_in, tokens,
-    gated, scale, carry_out, keep, gain_one, gain_two, proj_out, state_out, normed_out, w_out,
-    staged, w_all, normed, proj, state, local, reach, ends, squares, gain_slots, edge_slots,
+    gains, same, first, last, gate_gain, lower, w_in, tokens, wo_in,
+    gated, scale, carry_out, keep, gain_one, gain_two, proj_out, state_out, normed_out, w_out, wo_out,
+    staged, w_all, wo_staged, wo_all, normed, proj, state, local, reach, ends, squares, gain_slots, edge_slots,
     load_sem, store_sem, half_send, half_recv, ctx_send, ctx_recv, tp_send, tp_recv,
     gain_send, gain_recv, edge_send, edge_recv,
 ):
@@ -1299,7 +1351,11 @@
             pltpu.make_async_copy(w_in.at[gate], w_all.at[:, gate_cols[gate]], load_sem.at[gate])
             for gate in range(3)
         ]
-    for load in w_loads + [x_load]:
+    if n_fsdp == 2:
+        wo_load = pltpu.make_async_copy(wo_in, wo_staged, load_sem.at[4])
+    else:
+        wo_load = pltpu.make_async_copy(wo_in, wo_out, load_sem.at[4])
+    for load in w_loads + [x_load, wo_load]:
         load.start()
     gain_slots[core] = gains[...].astype(HALF).astype(FLOAT)
     edge_slots[lax.axis_index("ctx")] = last[...]
@@ -1350,6 +1406,25 @@
         normed[at, :] = (value * rms_scale(value) * gain_one[...]).astype(HALF)
 
     row_blocks(rows, 16, norm)
+    if n_fsdp == 2:
+        size = wo_staged.shape[1]
+        own_cols = span(core * size, size, size)
+        wo_load.wait()
+
+        def cast_out(at):
+            wo_all[at, own_cols] = wo_staged[at, :].astype(HALF)
+
+        row_blocks(chan, 32, cast_out)
+        copy = pltpu.make_async_remote_copy(
+            src_ref=wo_all.at[:, own_cols],
+            dst_ref=wo_all.at[:, own_cols],
+            send_sem=half_send.at[3],
+            recv_sem=half_recv.at[3],
+            device_id={"fsdp": 1 - core},
+            device_id_type=MESH,
+        )
+        copy.start()
+        halves_sent.append(copy)
     normed_store = pltpu.make_async_copy(normed, normed_out, store_sem.at[0])
     normed_store.start()
     flat = proj.reshape(3, rows, chan)
@@ -1438,11 +1513,19 @@
             gated[seq, rows, :] = (unit * gate_gain[...] * swish).astype(HALF)
     for copy in halves_sent:
         copy.wait_send()
+    if n_fsdp == 2:
+        halves_sent[3].wait_recv()
+        stores.append(pltpu.make_async_copy(wo_all, wo_out, load_sem.at[4]))
+        stores[-1].start()
+    else:
+        stores.append(wo_load)
     for store in stores + [normed_store, state_store]:
         store.wait()
 
 
-def run_head(gains, same, first, last, gate_gain, lower, w_in, tokens, n_fsdp, n_ctx, n_tp):
+def run_head(
+    gains, same, first, last, gate_gain, lower, w_in, tokens, w_out, n_fsdp, n_ctx, n_tp
+):
     n_seq, length, _ = same.shape
     rows, width = tokens.shape
     chan = w_in.shape[2]
@@ -1450,6 +1533,7 @@
     vmem = pl.BlockSpec(memory_space=pltpu.VMEM)
     hbm = pl.BlockSpec(memory_space=pl.ANY)
     staged = w_in.shape if n_fsdp == 2 else (3, 8, BLOCK)
+    wo_staged = w_out.shape if n_fsdp == 2 else (8, BLOCK)
     dma = pltpu.SemaphoreType.DMA
     return pl.pallas_call(
         functools.partial(head, n_fsdp, n_ctx, n_tp),
@@ -1465,12 +1549,15 @@
             jax.ShapeDtypeStruct(shape, FLOAT),
             jax.ShapeDtypeStruct((rows, width), HALF),
             jax.ShapeDtypeStruct((width, 3 * chan), HALF),
+            jax.ShapeDtypeStruct((chan, width), HALF),
         ),
-        in_specs=[vmem] * 6 + [hbm] * 2,
-        out_specs=[vmem] * 6 + [hbm] * 4,
+        in_specs=[vmem] * 6 + [hbm] * 3,
+        out_specs=[vmem] * 6 + [hbm] * 5,
         scratch_shapes=[
             pltpu.VMEM(staged, FLOAT),
             pltpu.VMEM((width, 3 * chan), HALF),
+            pltpu.VMEM(wo_staged, FLOAT),
+            pltpu.VMEM((chan, width), HALF),
             pltpu.VMEM((rows, width), HALF),
             pltpu.VMEM((3, *shape), FLOAT),
             pltpu.VMEM(shape, FLOAT),
@@ -1480,13 +1567,13 @@
             pltpu.VMEM((n_tp, n_seq, length), FLOAT),
             pltpu.VMEM((n_fsdp, *gains.shape), FLOAT),
             pltpu.VMEM((n_ctx, *last.shape), FLOAT),
-            dma((4,)), dma((4,)), dma((3,)), dma((3,)), dma((n_ctx,)), dma((n_ctx,)),
+            dma((5,)), dma((4,)), dma((4,)), dma((4,)), dma((n_ctx,)), dma((n_ctx,)),
             dma((n_tp,)), dma((n_tp,)), dma((n_fsdp,)), dma((n_fsdp,)), dma((n_ctx,)), dma((n_ctx,)),
         ],
         compiler_params=pltpu.CompilerParams(
             collective_id=0, has_side_effects=True, vmem_limit_bytes=63 * MIB
         ),
-    )(gains, same, first, last, gate_gain, lower, w_in, tokens)
+    )(gains, same, first, last, gate_gain, lower, w_in, tokens, w_out)
 
 
 def gather_fsdp(part, dim):
@@ -1502,17 +1589,21 @@
     rows = n_seq * length
     chan = w_in.shape[2]
     x_half = tokens.reshape(rows, width)
-    parts = (w_out.astype(HALF), w_glu[:, 0].astype(HALF), w_glu[:, 1].astype(HALF), w_down.astype(HALF))
+    parts = (w_glu[:, 0].astype(HALF), w_glu[:, 1].astype(HALF), w_down)
     if n_fsdp != 2:
-        parts = tuple(gather_fsdp(part, dim) for part, dim in zip(parts, (1, 0, 0, 1)))
+        parts = (*parts[:2], w_down.astype(HALF))
+        parts = tuple(gather_fsdp(part, dim) for part, dim in zip(parts, (0, 0, 1)))
         w_in = gather_fsdp(w_in.astype(HALF), 1)
+        w_out = gather_fsdp(w_out.astype(HALF), 1)
     gain_gate = gate_gain[None]
     low = lower[None]
     seg = segment_ids.astype(FLOAT)
     same = jnp.pad((seg[:, 1:] == seg[:, :-1]).astype(FLOAT), ((0, 0), (1, 0)))[..., None]
     first, last = (jnp.broadcast_to(seg[:, at], (n_seq, BLOCK)) for at in (slice(0, 1), slice(-1, None)))
-    gated, gate_scale, carry, keep, gain_a, gain_b, proj, state, normed, w_in_all = run_head(
-        jnp.stack([gain_one, gain_two]), same, first, last, gain_gate, low, w_in, x_half,
+    (
+        gated, gate_scale, carry, keep, gain_a, gain_b, proj, state, normed, w_in_all, w_out_all
+    ) = run_head(
+        jnp.stack([gain_one, gain_two]), same, first, last, gain_gate, low, w_in, x_half, w_out,
         n_fsdp, n_ctx, n_tp,
     )
     gated = gated.reshape(rows, chan)
@@ -1520,7 +1611,9 @@
     (
         mixed, _, act, _, grad_resid, grad_mixed, grad_gated, grad_w_gate, grad_w_up, w_down_all,
         grad_gain_two,
-    ) = run_middle(gated, x_half, grad_y_half, gain_b, parts, n_fsdp, n_ctx, length)
+    ) = run_middle(
+        gated, x_half, grad_y_half, gain_b, (w_out_all, *parts), n_fsdp, n_ctx, length
+    )
     if n_fsdp == 2:
         grad_w_up = lax.psum(grad_w_up, "ctx")
     grad_tokens, output, vectors, grad_w_in, grad_w_out, grad_w_down = run_tail(
@@ -1537,8 +1630,8 @@
             lax.psum(lax.psum_scatter(value, "fsdp", scatter_dimension=dim, tiled=True), "ctx")
             for value, dim in zip(grads, (0, 1, 0, 0, 1))
         )
-    results = run_widen_outputs(*grads, grad_tokens, vectors)
-    grad_w_in, grad_w_out, grad_w_glu, grad_w_down, grad_tokens = results[:5]
+    results = run_widen_outputs(*grads, grad_tokens, output, vectors)
+    grad_w_in, grad_w_out, grad_w_glu, grad_w_down, grad_tokens, output = results[:6]
     return (
         output.reshape(n_seq, length, width),
         grad_tokens.reshape(n_seq, length, width),
@@ -1546,7 +1639,7 @@
         grad_w_out,
         grad_w_glu,
         grad_w_down,
-        *(vector[0] for vector in results[5:]),
+        *(vector[0] for vector in results[6:]),
     )
 
 

time: 543 us -> 531 us (0.978)
  other arithmetic: 8.84 us -> 1.45 us
    convert_element_type x2 -> x0, other arithmetic: 7.39 us -> none  [the longest x1 4.67 us: local(): w_down.astype(HALF)]
where the time goes in v8:
time: 531 us; the launch traced here: 525 us
  Pallas kernels  498 us (94%)
  between operations  14.6 us (3%)
  local copies, waits for them, and re-layouts  10.4 us (2%)
    pallas_call x1, Pallas kernels, run_tail(): pl.pallas_call(functools.partial(tail, n_fsdp, n_ctx, n_tp), name='tail',...  220 us
    pallas_call x1, Pallas kernels, run_middle(): pl.pallas_call(functools.partial(middle, n_fsdp, n_ctx, length), name='mi...  217 us
    pallas_call x1, Pallas kernels, run_head(): pl.pallas_call(functools.partial(head, n_fsdp, n_ctx, n_tp), name='head',...  39.3 us
    pallas_call x1, Pallas kernels, run_widen_outputs(): pl.pallas_call(widen_outputs, name='widen_outputs', grid=(steps,), out_sh...  21.8 us
  transfers between devices with their start and end apart: 1, of which 0 were waited for; matrix products, arithmetic and copies ran while one was open for 0% of the time, Pallas kernels for 42%

profile of v8, /device:TPU:0, one launch (start us, length us, event | category | flops | bytes accessed | tf_op | source)
XLA Modules:
  0.0 525.0 jit_solution(16131047471156161789)
XLA Ops:
  7.2 0.0 all-reduce.3.cloned.1.call-start
  7.2 0.7 convert_element_type.12
  7.9 0.1 slice_compare_fusion
  8.0 0.2 slice_reduce_fusion
  8.2 0.1 convert_bitcast_fusion
  8.2 1.0 copy.22.same
  9.3 4.9 copy.25
  14.2 0.0 copy-start
  14.2 0.0 copy-start.1
  14.2 3.0 slice_bitcast_fusion
  17.2 0.0 copy-done
  17.2 0.0 copy-done.1
  17.2 0.6 pad_maximum_fusion.gains
  17.8 0.6 broadcast_in_dim.30.last
  18.5 0.6 broadcast_in_dim.28.first
  19.1 39.3 %head.1 = (bf16[4,256,512]{2,1,0:T(8,128)(2,1)}, f32[4,256]{1,0:T(4,128)}, f32[4,512]{1,0:T(4,128)}, f32[4,256,1]{2,1,0:T(8,128)}, f32[1,2048]{1,0:T(1,128)}, /*...) custom-call(f32[2,1024]{1,0:T(2,128)} %pad_maximum_fusion.gains, ...), custom_call_target="tpu_custom_call" | custom-call | tf_op jit(solution)/shard_map/head/pallas_call | solution.py:1538
  58.5 217.1 %middle.1 = (bf16[1024,2048]{1,0:T(8,128)(2,1)}, bf16[1024,2048]{1,0:T(8,128)(2,1)}, bf16[1024,1408]{1,0:T(8,128)(2,1)}, bf16[2,1024,1408]{2,1,0:T(8,128)(2,1)},...) custom-call(bf16[1024,512]{1,0:T(8,128)(2,1)} %bitcast.33, ...), custom_call_target="tpu_custom_call" | custom-call | flops 47244640256 | bytes 419430400 | tf_op jit(solution)/shard_map/middle/pallas_call | solution.py:696
  275.6 0.0 all-reduce.3.cloned.1.call-update
  275.6 220.2 %tail.1 = (bf16[1024,2048]{1,0:T(8,128)(2,1)}, bf16[1024,2048]{1,0:T(8,128)(2,1)}, f32[1,5120]{1,0:T(1,128)}, bf16[1024,1536]{1,0:T(8,128)(2,1)}, bf16[512,1024]{1,0:T(8,128)(2,1)}, /*index=5*/bf16[1408,1024]{1,0:T(8,128)(2,1)}) custom-call(f32[4,256,1]{2,1,0:T(8,128)} %get-tuple-element.46.keep, f32[1,512]{1,0:T(1,128)} %bitcast.26, f32[1,512]{1,0:T(1,128)} %bitcast.28, ...), custom_call_target="tpu_custom_call" | custom-call | flops 29527900160 | bytes 734003200 | tf_op jit(solution)/shard_map/tail/pallas_call | solution.py:1207
  495.8 0.0 all-reduce.3.cloned.1.call-done.w_up
  495.8 21.8 %widen_outputs.1 = (f32[3,1024,512]{2,1,0:T(8,128)}, f32[512,1024]{1,0:T(8,128)}, f32[1024,2,1408]{2,1,0:T(2,128)}, f32[1408,1024]{1,0:T(8,128)}, f32[1024,2048]...) custom-call(bf16[1024,1536]{1,0:T(8,128)(2,1)} %get-tuple-element.64, ...), custom_call_target="tpu_custom_call" | custom-call | tf_op jit(solution)/shard_map/widen_outputs/pallas_call | solution.py:1317
Async XLA Ops:
  7.2 488.6 %all-reduce.3.cloned.1.call-start = ((), (), s32[]{:S(2)}) async-start(), calls=%async_computation | async-start | bytes 5767168 | tf_op jit(solution)/shard_map/psum | solution.py:1618
  14.2 3.0 copy-start
  14.2 3.0 copy-start.1
Sparse Core Ops, SparseCore 0:
  275.7 97.2 all-reduce.2

commit v9 on v8

--- a/solution.py
+++ b/solution.py
@@ -365,7 +365,6 @@
     peers = line_peers() + others("ctx", n_ctx)
     if n_fsdp == 2:
         peers.append({"fsdp": 1 - lax.axis_index("fsdp")})
-    greet(peers)
     local_parts = [(wo_part, wo)]
     if n_fsdp != 2:
         local_parts += [(wg_part, wg), (wu_part, wu), (wd_part, wd)]
@@ -375,6 +374,7 @@
     ]
     for copy in ready:
         copy.start()
+    greet(peers)
     core = lax.axis_index("fsdp")
     n_bands = units // BLOCK
 
@@ -1327,7 +1327,7 @@
 
 def head(
     n_fsdp, n_ctx, n_tp,
-    gains, same, first, last, gate_gain, lower, w_in, tokens, wo_in,
+    gains, same, edges, gate_gain, lower, w_in, tokens, wo_in,
     gated, scale, carry_out, keep, gain_one, gain_two, proj_out, state_out, normed_out, w_out, wo_out,
     staged, w_all, wo_staged, wo_all, normed, proj, state, local, reach, ends, squares, gain_slots, edge_slots,
     load_sem, store_sem, half_send, half_recv, ctx_send, ctx_recv, tp_send, tp_recv,
@@ -1337,7 +1337,6 @@
     rows = n_seq * length
     depth = w_in.shape[1]
     width = w_all.shape[0]
-    greet(others("ctx", n_ctx) + others("tp", n_tp) + others("fsdp", n_fsdp))
     core = lax.axis_index("fsdp")
     gate_cols = [slice(gate * chan, (gate + 1) * chan) for gate in range(3)]
     x_load = pltpu.make_async_copy(tokens, normed, load_sem.at[3])
@@ -1358,7 +1357,8 @@
     for load in w_loads + [x_load, wo_load]:
         load.start()
     gain_slots[core] = gains[...].astype(HALF).astype(FLOAT)
-    edge_slots[lax.axis_index("ctx")] = last[...]
+    edge_slots[lax.axis_index("ctx")] = edges[1]
+    greet(others("ctx", n_ctx) + others("tp", n_tp) + others("fsdp", n_fsdp))
     small = shares(gain_slots, "fsdp", n_fsdp, gain_send, gain_recv)
     small += shares(edge_slots, "ctx", n_ctx, edge_send, edge_recv)
     for copy in small:
@@ -1397,7 +1397,7 @@
     before = edge_slots[0]
     for place in range(1, n_ctx):
         before = jnp.where(place == here - 1, edge_slots[place], before)
-    joins = jnp.where((before == first[...]) & (here > 0), 1.0, 0.0)
+    joins = jnp.where((before == edges[0]) & (here > 0), 1.0, 0.0)
     keep[:, :1, :] = joins[:, :1].reshape(n_seq, 1, 1)
     x_load.wait()
 
@@ -1524,7 +1524,7 @@
 
 
 def run_head(
-    gains, same, first, last, gate_gain, lower, w_in, tokens, w_out, n_fsdp, n_ctx, n_tp
+    gains, same, edges, gate_gain, lower, w_in, tokens, w_out, n_fsdp, n_ctx, n_tp
 ):
     n_seq, length, _ = same.shape
     rows, width = tokens.shape
@@ -1551,7 +1551,7 @@
             jax.ShapeDtypeStruct((width, 3 * chan), HALF),
             jax.ShapeDtypeStruct((chan, width), HALF),
         ),
-        in_specs=[vmem] * 6 + [hbm] * 3,
+        in_specs=[vmem] * 5 + [hbm] * 3,
         out_specs=[vmem] * 6 + [hbm] * 5,
         scratch_shapes=[
             pltpu.VMEM(staged, FLOAT),
@@ -1566,14 +1566,14 @@
             pltpu.VMEM((n_ctx, 2, n_seq, chan), FLOAT),
             pltpu.VMEM((n_tp, n_seq, length), FLOAT),
             pltpu.VMEM((n_fsdp, *gains.shape), FLOAT),
-            pltpu.VMEM((n_ctx, *last.shape), FLOAT),
+            pltpu.VMEM((n_ctx, *edges.shape[1:]), FLOAT),
             dma((5,)), dma((4,)), dma((4,)), dma((4,)), dma((n_ctx,)), dma((n_ctx,)),
             dma((n_tp,)), dma((n_tp,)), dma((n_fsdp,)), dma((n_fsdp,)), dma((n_ctx,)), dma((n_ctx,)),
         ],
         compiler_params=pltpu.CompilerParams(
             collective_id=0, has_side_effects=True, vmem_limit_bytes=63 * MIB
         ),
-    )(gains, same, first, last, gate_gain, lower, w_in, tokens, w_out)
+    )(gains, same, edges, gate_gain, lower, w_in, tokens, w_out)
 
 
 def gather_fsdp(part, dim):
@@ -1599,11 +1599,11 @@
     low = lower[None]
     seg = segment_ids.astype(FLOAT)
     same = jnp.pad((seg[:, 1:] == seg[:, :-1]).astype(FLOAT), ((0, 0), (1, 0)))[..., None]
-    first, last = (jnp.broadcast_to(seg[:, at], (n_seq, BLOCK)) for at in (slice(0, 1), slice(-1, None)))
+    edges = jnp.broadcast_to(jnp.stack([seg[:, 0], seg[:, -1]])[..., None], (2, n_seq, BLOCK))
     (
         gated, gate_scale, carry, keep, gain_a, gain_b, proj, state, normed, w_in_all, w_out_all
     ) = run_head(
-        jnp.stack([gain_one, gain_two]), same, first, last, gain_gate, low, w_in, x_half, w_out,
+        jnp.stack([gain_one, gain_two]), same, edges, gain_gate, low, w_in, x_half, w_out,
         n_fsdp, n_ctx, n_tp,
     )
     gated = gated.reshape(rows, chan)

time: 531 us -> 528 us (level)
  no operation moved by 1% of the time
where the time goes in v9:
time: 528 us; the launch traced here: 522 us
  Pallas kernels  496 us (94%)
  between operations  14.6 us (3%)
  local copies, waits for them, and re-layouts  9.77 us (2%)
    pallas_call x1, Pallas kernels, run_tail(): pl.pallas_call(functools.partial(tail, n_fsdp, n_ctx, n_tp), name='tail',...  220 us
    pallas_call x1, Pallas kernels, run_middle(): pl.pallas_call(functools.partial(middle, n_fsdp, n_ctx, length), name='mi...  215 us
    pallas_call x1, Pallas kernels, run_head(): pl.pallas_call(functools.partial(head, n_fsdp, n_ctx, n_tp), name='head',...  39.1 us
    pallas_call x1, Pallas kernels, run_widen_outputs(): pl.pallas_call(widen_outputs, name='widen_outputs', grid=(steps,), out_sh...  21.8 us
  transfers between devices with their start and end apart: 1, of which 0 were waited for; matrix products, arithmetic and copies ran while one was open for 0% of the time, Pallas kernels for 42%

profile of v9, /device:TPU:0, one launch (start us, length us, event | category | flops | bytes accessed | tf_op | source)
XLA Modules:
  0.0 521.8 jit_solution(11354111351477727822)
XLA Ops:
  7.2 0.0 all-reduce.3.cloned.1.call-start
  7.2 0.7 convert_element_type.12
  7.9 0.1 slice_compare_fusion
  8.0 0.2 slice_reduce_fusion.1
  8.2 0.1 convert_bitcast_fusion
  8.2 1.0 copy.22.same
  9.3 4.9 copy.25
  14.2 0.0 copy-start
  14.2 0.0 copy-start.1
  14.2 3.0 slice_bitcast_fusion
  17.2 0.0 copy-done
  17.2 0.0 copy-done.1
  17.2 0.6 pad_maximum_fusion.gains
  17.8 0.7 broadcast_in_dim.19.edges
  18.5 39.1 %head.1 = (bf16[4,256,512]{2,1,0:T(8,128)(2,1)}, f32[4,256]{1,0:T(4,128)}, f32[4,512]{1,0:T(4,128)}, f32[4,256,1]{2,1,0:T(8,128)}, f32[1,2048]{1,0:T(1,128)}, /*...) custom-call(f32[2,1024]{1,0:T(2,128)} %pad_maximum_fusion.gains, ...), custom_call_target="tpu_custom_call" | custom-call | tf_op jit(solution)/shard_map/head/pallas_call | solution.py:1538
  57.6 214.9 %middle.1 = (bf16[1024,2048]{1,0:T(8,128)(2,1)}, bf16[1024,2048]{1,0:T(8,128)(2,1)}, bf16[1024,1408]{1,0:T(8,128)(2,1)}, bf16[2,1024,1408]{2,1,0:T(8,128)(2,1)},...) custom-call(bf16[1024,512]{1,0:T(8,128)(2,1)} %bitcast.37, ...), custom_call_target="tpu_custom_call" | custom-call | flops 47244640256 | bytes 419430400 | tf_op jit(solution)/shard_map/middle/pallas_call | solution.py:696
  272.5 0.0 all-reduce.3.cloned.1.call-update
  272.6 220.0 %tail.1 = (bf16[1024,2048]{1,0:T(8,128)(2,1)}, bf16[1024,2048]{1,0:T(8,128)(2,1)}, f32[1,5120]{1,0:T(1,128)}, bf16[1024,1536]{1,0:T(8,128)(2,1)}, bf16[512,1024]{1,0:T(8,128)(2,1)}, /*index=5*/bf16[1408,1024]{1,0:T(8,128)(2,1)}) custom-call(f32[4,256,1]{2,1,0:T(8,128)} %get-tuple-element.46.keep, f32[1,512]{1,0:T(1,128)} %bitcast.28, f32[1,512]{1,0:T(1,128)} %bitcast.30, ...), custom_call_target="tpu_custom_call" | custom-call | flops 29527900160 | bytes 734003200 | tf_op jit(solution)/shard_map/tail/pallas_call | solution.py:1207
  492.6 0.0 all-reduce.3.cloned.1.call-done.w_up
  492.6 21.8 %widen_outputs.1 = (f32[3,1024,512]{2,1,0:T(8,128)}, f32[512,1024]{1,0:T(8,128)}, f32[1024,2,1408]{2,1,0:T(2,128)}, f32[1408,1024]{1,0:T(8,128)}, f32[1024,2048]...) custom-call(bf16[1024,1536]{1,0:T(8,128)(2,1)} %get-tuple-element.64, ...), custom_call_target="tpu_custom_call" | custom-call | tf_op jit(solution)/shard_map/widen_outputs/pallas_call | solution.py:1317
  (1 shorter events, 0.0 us)
Async XLA Ops:
  7.2 485.4 %all-reduce.3.cloned.1.call-start = ((), (), s32[]{:S(2)}) async-start(), calls=%async_computation | async-start | bytes 5767168 | tf_op jit(solution)/shard_map/psum | solution.py:1618
  14.2 3.0 copy-start
  14.2 3.0 copy-start.1
Sparse Core Ops, SparseCore 0:
  272.7 97.3 all-reduce.2

commit v10 on v9

--- a/solution.py
+++ b/solution.py
@@ -891,7 +891,6 @@
     piece = width // PIECES
     n_chunks = n_seq
     whole = n_fsdp != 2
-    greet(others("ctx", n_ctx) + others("tp", n_tp) + others("fsdp", n_fsdp))
     line = Line(held, crossed, total, line_sems)
     pieces = [(job, q) for job in range(2 * n_chunks) for q in range(PIECES)]
     relay = [(line.forward, spot) for spot in pieces[:2]]
@@ -932,6 +931,7 @@
 
     def down_terms(w_all, act_all):
         copies = start_loads([(w_down, w_all), (act, act_all)], 3)
+        greet(others("ctx", n_ctx) + others("tp", n_tp) + others("fsdp", n_fsdp))
 
         def cross_terms(gate_all, state_all):
             for copy in start_loads(

time: 528 us -> 526 us (level)
  no operation moved by 1% of the time
where the time goes in v10:
time: 526 us; the launch traced here: 520 us
  Pallas kernels  494 us (94%)
  between operations  14.6 us (3%)
  local copies, waits for them, and re-layouts  9.77 us (2%)
    pallas_call x1, Pallas kernels, run_tail(): pl.pallas_call(functools.partial(tail, n_fsdp, n_ctx, n_tp), name='tail',...  218 us
    pallas_call x1, Pallas kernels, run_middle(): pl.pallas_call(functools.partial(middle, n_fsdp, n_ctx, length), name='mi...  215 us
    pallas_call x1, Pallas kernels, run_head(): pl.pallas_call(functools.partial(head, n_fsdp, n_ctx, n_tp), name='head',...  39.1 us
    pallas_call x1, Pallas kernels, run_widen_outputs(): pl.pallas_call(widen_outputs, name='widen_outputs', grid=(steps,), out_sh...  21.8 us
  transfers between devices with their start and end apart: 1, of which 0 were waited for; matrix products, arithmetic and copies ran while one was open for 0% of the time, Pallas kernels for 42%

profile of v10, /device:TPU:0, one launch (start us, length us, event | category | flops | bytes accessed | tf_op | source)
XLA Modules:
  0.0 519.7 jit_solution(9368846999505874965)
XLA Ops:
  7.2 0.0 all-reduce.3.cloned.1.call-start
  7.2 0.7 convert_element_type.12
  7.9 0.1 slice_compare_fusion
  8.0 0.2 slice_reduce_fusion.1
  8.2 0.1 convert_bitcast_fusion
  8.2 1.0 copy.22.same
  9.3 4.9 copy.25
  14.2 0.0 copy-start
  14.2 0.0 copy-start.1
  14.2 3.0 slice_bitcast_fusion
  17.2 0.0 copy-done
  17.2 0.0 copy-done.1
  17.2 0.6 pad_maximum_fusion.gains
  17.8 0.7 broadcast_in_dim.19.edges
  18.5 39.1 %head.1 = (bf16[4,256,512]{2,1,0:T(8,128)(2,1)}, f32[4,256]{1,0:T(4,128)}, f32[4,512]{1,0:T(4,128)}, f32[4,256,1]{2,1,0:T(8,128)}, f32[1,2048]{1,0:T(1,128)}, /*...) custom-call(f32[2,1024]{1,0:T(2,128)} %pad_maximum_fusion.gains, ...), custom_call_target="tpu_custom_call" | custom-call | tf_op jit(solution)/shard_map/head/pallas_call | solution.py:1538
  57.6 214.9 %middle.1 = (bf16[1024,2048]{1,0:T(8,128)(2,1)}, bf16[1024,2048]{1,0:T(8,128)(2,1)}, bf16[1024,1408]{1,0:T(8,128)(2,1)}, bf16[2,1024,1408]{2,1,0:T(8,128)(2,1)},...) custom-call(bf16[1024,512]{1,0:T(8,128)(2,1)} %bitcast.37, ...), custom_call_target="tpu_custom_call" | custom-call | flops 47244640256 | bytes 419430400 | tf_op jit(solution)/shard_map/middle/pallas_call | solution.py:696
  272.5 0.0 all-reduce.3.cloned.1.call-update
  272.6 217.9 %tail.1 = (bf16[1024,2048]{1,0:T(8,128)(2,1)}, bf16[1024,2048]{1,0:T(8,128)(2,1)}, f32[1,5120]{1,0:T(1,128)}, bf16[1024,1536]{1,0:T(8,128)(2,1)}, bf16[512,1024]{1,0:T(8,128)(2,1)}, /*index=5*/bf16[1408,1024]{1,0:T(8,128)(2,1)}) custom-call(f32[4,256,1]{2,1,0:T(8,128)} %get-tuple-element.46.keep, f32[1,512]{1,0:T(1,128)} %bitcast.28, f32[1,512]{1,0:T(1,128)} %bitcast.30, ...), custom_call_target="tpu_custom_call" | custom-call | flops 29527900160 | bytes 734003200 | tf_op jit(solution)/shard_map/tail/pallas_call | solution.py:1207
  490.5 0.0 all-reduce.3.cloned.1.call-done.w_up
  490.5 21.8 %widen_outputs.1 = (f32[3,1024,512]{2,1,0:T(8,128)}, f32[512,1024]{1,0:T(8,128)}, f32[1024,2,1408]{2,1,0:T(2,128)}, f32[1408,1024]{1,0:T(8,128)}, f32[1024,2048]...) custom-call(bf16[1024,1536]{1,0:T(8,128)(2,1)} %get-tuple-element.64, ...), custom_call_target="tpu_custom_call" | custom-call | tf_op jit(solution)/shard_map/widen_outputs/pallas_call | solution.py:1317
  (1 shorter events, 0.0 us)
Async XLA Ops:
  7.2 483.3 %all-reduce.3.cloned.1.call-start = ((), (), s32[]{:S(2)}) async-start(), calls=%async_computation | async-start | bytes 5767168 | tf_op jit(solution)/shard_map/psum | solution.py:1618
  14.2 3.0 copy-start
  14.2 3.0 copy-start.1
Sparse Core Ops, SparseCore 0:
  272.7 98.9 all-reduce.2
